TPU v7x, 32 devices: a whole 2x2x4 slice. The times are simulated.
32 devices in a mesh: seq: 4 (over y, core), fsdp: 8 (over z, x).
Axes of the slice: x: 2, y: 2, z: 4, core: 2. Of those that a mesh axis runs over, the one named last changes fastest.
Arguments:
- tokens: bfloat16 [8, 1024, 2048], P('fsdp', 'seq'), may hold values from -6 to 6
- cotangent: bfloat16 [8, 1024, 2048], P('fsdp', 'seq'), may hold values from -6 to 6
- lengths: int32 [8, 4], P('fsdp'), may hold values from 0 to 1024, as said below
- sequence_adapter: int32 [8, 4], P('fsdp'), may hold values from 0 to 7
- attention_norm_gain: float32 [2048], replicated, may hold values from 0.1 to 1.9
- feedfwd_norm_gain: float32 [2048], replicated, may hold values from 0.1 to 1.9
- query_matrix: bfloat16 [2048, 2048], P('fsdp'), may hold values from -0.5 to 0.5
- key_matrix: bfloat16 [2048, 512], P('fsdp'), may hold values from -0.5 to 0.5
- value_matrix: bfloat16 [2048, 512], P('fsdp'), may hold values from -0.125 to 0.125
- output_matrix: bfloat16 [2048, 2048], P('fsdp'), may hold values from -1.5 to 1.5
- gate_matrix: bfloat16 [2048, 8192], P('fsdp'), may hold values from -0.125 to 0.125
- up_matrix: bfloat16 [2048, 8192], P('fsdp'), may hold values from -0.125 to 0.125
- down_matrix: bfloat16 [8192, 2048], P('fsdp'), may hold values from -0.25 to 0.25
- adapter_first_factors: bfloat16 [6, 2048, 128], replicated, may hold values from -0.125 to 0.125
- adapter_first_down: bfloat16 [8192, 128], replicated, may hold values from -0.0625 to 0.0625
- adapter_second_model: bfloat16 [3, 128, 2048], replicated, may hold values from -1.5 to 1.5
- adapter_second_keyvalue: bfloat16 [2, 128, 512], replicated, may hold values from -1.5 to 1.5
- adapter_second_feedfwd: bfloat16 [2, 128, 8192], replicated, may hold values from -1.5 to 1.5
Outputs:
- layer_out: bfloat16 [8, 1024, 2048], P('fsdp', 'seq')
- grad_tokens: bfloat16 [8, 1024, 2048], P('fsdp', 'seq')
- grad_lora_a: float32 [6, 2048, 128], replicated
- grad_lora_a_down: float32 [8192, 128], replicated
- grad_lora_b_model: float32 [3, 128, 2048], replicated
- grad_lora_b_kv: float32 [2, 128, 512], replicated
- grad_lora_b_ffn: float32 [2, 128, 8192], replicated
Inputs may be any that keep to these rules, and one draw needn't show every extreme that they name: In each pack the lengths add up to 1024 or less; pack 0 holds one sequence of exactly 1024 tokens and three empty ones; in every other pack each sequence has 1 token or more and the first 512 or more; padded slots follow the last sequence.
All inputs are finite; a program needn't handle non-finite values.
Results may differ from a plain program's by a relative error of at most 0.018.
The roundings to bfloat16 on the way count: a program that leaves them out, or rounds other values in their place, can miss the bound.
Values may be sent and summed in bfloat16 or wider, within the bound.
No kernel may reach another device: no remote copies, remote signals or barrier semaphores. Data moves between devices by JAX's collectives and lax.ppermute only.
A program may use at most 384 MiB of HBM per device.

v0:
```python
import math

import jax
import jax.numpy as jnp
from jax import lax
from jax.sharding import PartitionSpec as P

MODEL_WIDTH = 2048
HEADS = 32
KV_HEADS = 8
HEAD_DIM = 64
ADAPTER_RANK = 16
ADAPTER_TOTAL = 8
PACK = 1024
QBLOCK = 512
KEY_HEAD_WIDTH = 512


SCORE_SCALE = 0.015625
RESIDUAL_FACTOR = 0.22
NORM_EPSILON = 1e-05
ROPE_BASE = 10000000.0
MASK_FILL = 1e30


def matrix_product(left, right):
    return jnp.dot(left, right, preferred_element_type=jnp.float32)


def product_right_transposed(left, right):
    return lax.dot_general(
        left, right, (((1,), (1,)), ((), ())), preferred_element_type=jnp.float32
    )


def product_left_transposed(left, right):
    return lax.dot_general(
        left, right, (((0,), (0,)), ((), ())), preferred_element_type=jnp.float32
    )


def rms_norm(hidden, gain_vec):
    mean_square = jnp.mean(hidden * hidden, axis=-1, keepdims=True)
    return hidden * lax.rsqrt(mean_square + NORM_EPSILON) * gain_vec


def rotate(vectors, cosine, sine_table):
    half_dim = vectors.shape[-1] // 2
    front_half = vectors[..., :half_dim]
    back_half = vectors[..., half_dim:]
    turned = jnp.concatenate([-back_half, front_half], axis=-1)
    return vectors * cosine + turned * sine_table


def pack_tables(seq_lengths, adapter_id, token_count, adapter_count):
    slots = seq_lengths.shape[0]
    places = jnp.arange(token_count, dtype=jnp.int32)
    seq_ends = jnp.cumsum(seq_lengths)
    seq_starts = seq_ends - seq_lengths
    used_len = seq_ends[slots - 1]
    segment = jnp.sum((places[:, None] >= seq_ends[None, :]).astype(jnp.int32), axis=1)
    member = segment[:, None] == jnp.arange(slots, dtype=jnp.int32)[None, :]
    start_tok = jnp.sum(jnp.where(member, seq_starts[None, :], 0), axis=1) + jnp.where(
        segment == slots, used_len, 0
    )
    position = places - start_tok
    valid_row = segment < slots
    chosen = adapter_id[:, None] == jnp.arange(adapter_count, dtype=jnp.int32)[None, :]
    onehot = jnp.sum(jnp.where(member[:, :, None] & chosen[None, :, :], 1.0, 0.0), axis=1).astype(
        jnp.float32
    )
    return (segment, position, valid_row, onehot)


def rope_tables(position, head_size):
    frequency = ROPE_BASE ** (-(jnp.arange(head_size // 2, dtype=jnp.float32) * 2.0) / head_size)
    angles = position.astype(jnp.float32)[:, None] * frequency[None, :]
    angles = jnp.concatenate([angles, angles], axis=1)
    return (jnp.cos(angles)[:, None, :], jnp.sin(angles)[:, None, :])


def block_allowed(segment, first_row):
    token_count = segment.shape[0]
    query_seg = lax.dynamic_slice_in_dim(segment, first_row, QBLOCK, 0)
    query_pos = first_row + jnp.arange(QBLOCK, dtype=jnp.int32)
    places = jnp.arange(token_count, dtype=jnp.int32)
    return (query_seg[:, None] == segment[None, :]) & (places[None, :] <= query_pos[:, None])


def split_heads(heads_in, group_ratio):
    query_width = group_ratio * HEAD_DIM
    key_rows = heads_in[:, :, query_width : query_width + HEAD_DIM]
    value_rows = heads_in[:, :, query_width + HEAD_DIM :]
    return (key_rows, value_rows)


def block_scores(heads_in, key_rows, segment, first_row, group_ratio):
    groups = heads_in.shape[1]
    query_width = group_ratio * HEAD_DIM
    queries = lax.dynamic_slice_in_dim(heads_in, first_row, QBLOCK, 0)[:, :, :query_width]
    queries = queries.reshape(QBLOCK, groups, group_ratio, HEAD_DIM)
    scores = (
        jnp.einsum("qgjd,kgd->gjqk", queries, key_rows, preferred_element_type=jnp.float32)
        * SCORE_SCALE
    )
    scores = jnp.where(block_allowed(segment, first_row), scores, -MASK_FILL)
    return (queries, scores)


def attend_forward(heads_in, segment, group_ratio):
    token_count, groups, _ = heads_in.shape
    key_rows, value_rows = split_heads(heads_in, group_ratio)

    def one_block(block_index):
        first_row = block_index * QBLOCK
        queries, scores = block_scores(heads_in, key_rows, segment, first_row, group_ratio)
        row_max = jnp.max(scores, axis=-1, keepdims=True)
        exponent = jnp.exp(scores - row_max)
        row_total = jnp.sum(exponent, axis=-1, keepdims=True)
        attn_probs = (exponent / row_total).astype(jnp.bfloat16)
        block_out = jnp.einsum(
            "gjqk,kgd->qgjd", attn_probs, value_rows, preferred_element_type=jnp.float32
        )
        log_total = (row_max + jnp.log(row_total))[..., 0]
        return (
            block_out.astype(jnp.bfloat16).reshape(QBLOCK, groups, group_ratio * HEAD_DIM),
            log_total,
        )

    block_outs, log_totals = lax.map(one_block, jnp.arange(token_count // QBLOCK, dtype=jnp.int32))
    return (block_outs.reshape(token_count, groups, group_ratio * HEAD_DIM), log_totals)


def attend_backward(heads_in, segment, log_totals, grad_heads, group_ratio):
    token_count, groups, _ = heads_in.shape
    key_rows, value_rows = split_heads(heads_in, group_ratio)

    def one_block(running, block_index):
        grad_keys, grad_values = running
        first_row = block_index * QBLOCK
        queries, scores = block_scores(heads_in, key_rows, segment, first_row, group_ratio)
        attn_exact = jnp.exp(scores - log_totals[block_index][..., None])
        attn_probs = attn_exact.astype(jnp.bfloat16)
        grad_block = lax.dynamic_slice_in_dim(grad_heads, first_row, QBLOCK, 0).reshape(
            QBLOCK, groups, group_ratio, HEAD_DIM
        )
        grad_probs = jnp.einsum(
            "qgjd,kgd->gjqk", grad_block, value_rows, preferred_element_type=jnp.float32
        )
        delta = jnp.sum(attn_exact * grad_probs, axis=-1, keepdims=True)
        grad_scores = (attn_exact * (grad_probs - delta)).astype(jnp.bfloat16)
        gradient_query_rows = (
            jnp.einsum("gjqk,kgd->qgjd", grad_scores, key_rows, preferred_element_type=jnp.float32)
            * SCORE_SCALE
        )
        grad_keys = (
            grad_keys
            + jnp.einsum("gjqk,qgjd->kgd", grad_scores, queries, preferred_element_type=jnp.float32)
            * SCORE_SCALE
        )
        grad_values = grad_values + jnp.einsum(
            "gjqk,qgjd->kgd", attn_probs, grad_block, preferred_element_type=jnp.float32
        )
        return (
            (grad_keys, grad_values),
            gradient_query_rows.astype(jnp.bfloat16).reshape(
                QBLOCK, groups, group_ratio * HEAD_DIM
            ),
        )

    zero_rows = jnp.zeros((token_count, groups, HEAD_DIM), jnp.float32)
    (grad_keys, grad_values), grad_queries = lax.scan(
        one_block, (zero_rows, zero_rows), jnp.arange(token_count // QBLOCK, dtype=jnp.int32)
    )
    grad_queries = grad_queries.reshape(token_count, groups, group_ratio * HEAD_DIM)
    return jnp.concatenate(
        [grad_queries, grad_keys.astype(jnp.bfloat16), grad_values.astype(jnp.bfloat16)], axis=2
    )


def shards(
    tokens,
    cotangent,
    lengths,
    sequence_adapter,
    attention_norm_gain,
    feedfwd_norm_gain,
    query_matrix,
    key_matrix,
    value_matrix,
    output_matrix,
    gate_matrix,
    up_matrix,
    down_matrix,
    adapter_first_factors,
    adapter_first_down,
    adapter_second_model,
    adapter_second_keyvalue,
    adapter_second_feedfwd,
):
    resid_in = tokens[0]
    row_count = resid_in.shape[0]
    adapter_columns_span = ADAPTER_TOTAL * ADAPTER_RANK
    group_ratio = HEADS // KV_HEADS
    query_width = group_ratio * HEAD_DIM
    segment, position, valid_row, onehot = pack_tables(
        lengths[0], sequence_adapter[0], PACK, ADAPTER_TOTAL
    )
    first_local = lax.axis_index("seq") * row_count
    pos_local = lax.dynamic_slice_in_dim(position, first_local, row_count, 0)
    valid_col = jnp.where(
        lax.dynamic_slice_in_dim(valid_row, first_local, row_count, 0), 1.0, 0.0
    ).astype(jnp.float32)[:, None]
    adapter_mask_repeated = jnp.repeat(
        lax.dynamic_slice_in_dim(onehot, first_local, row_count, 0), ADAPTER_RANK, axis=1
    ).astype(jnp.bfloat16)
    third_adapter_mask = jnp.tile(adapter_mask_repeated, (1, 3))
    second_adapter_mask = jnp.tile(adapter_mask_repeated, (1, 2))
    cosine, sine_table = rope_tables(pos_local, HEAD_DIM)
    hidden_in = resid_in.astype(jnp.float32)
    first_normed_input = rms_norm(hidden_in, attention_norm_gain).astype(jnp.bfloat16)
    query_total, full_key, value_total = (
        lax.all_gather(query_matrix, "fsdp", axis=0, tiled=True),
        lax.all_gather(key_matrix, "fsdp", axis=0, tiled=True),
        lax.all_gather(value_matrix, "fsdp", axis=0, tiled=True),
    )
    adapter_input = jnp.concatenate(
        [adapter_first_factors[0], adapter_first_factors[1], adapter_first_factors[2]], axis=1
    )
    lowrank_attention = (
        matrix_product(first_normed_input, adapter_input) * third_adapter_mask
    ).astype(jnp.bfloat16)
    query_rows_full = matrix_product(first_normed_input, query_total) + matrix_product(
        lowrank_attention[:, :adapter_columns_span], adapter_second_model[0]
    )
    key_portion = matrix_product(first_normed_input, full_key) + matrix_product(
        lowrank_attention[:, adapter_columns_span : 2 * adapter_columns_span],
        adapter_second_keyvalue[0],
    )
    value_portion = matrix_product(first_normed_input, value_total) + matrix_product(
        lowrank_attention[:, 2 * adapter_columns_span :], adapter_second_keyvalue[1]
    )
    query_r = rotate(query_rows_full.reshape(row_count, HEADS, HEAD_DIM), cosine, sine_table)
    key_r = rotate(key_portion.reshape(row_count, KV_HEADS, HEAD_DIM), cosine, sine_table)
    packed = jnp.concatenate(
        [
            query_r.reshape(row_count, KV_HEADS, query_width),
            key_r,
            value_portion.reshape(row_count, KV_HEADS, HEAD_DIM),
        ],
        axis=2,
    ).astype(jnp.bfloat16)
    heads_in = lax.all_to_all(packed, "seq", split_axis=1, concat_axis=0, tiled=True)
    attn_heads, log_totals = attend_forward(heads_in, segment, group_ratio)
    attention_token_rows = lax.all_to_all(
        attn_heads, "seq", split_axis=0, concat_axis=1, tiled=True
    ).reshape(row_count, MODEL_WIDTH)
    output_total = lax.all_gather(output_matrix, "fsdp", axis=0, tiled=True)
    lowrank_output = (
        matrix_product(attention_token_rows, adapter_first_factors[3]) * adapter_mask_repeated
    ).astype(jnp.bfloat16)
    residual_branch = matrix_product(attention_token_rows, output_total) + matrix_product(
        lowrank_output, adapter_second_model[1]
    )
    hidden_mid = hidden_in + RESIDUAL_FACTOR * residual_branch
    second_normed_input = rms_norm(hidden_mid, feedfwd_norm_gain).astype(jnp.bfloat16)
    gate_total, up_total = (
        lax.all_gather(gate_matrix, "fsdp", axis=0, tiled=True),
        lax.all_gather(up_matrix, "fsdp", axis=0, tiled=True),
    )
    adapter_feedfwd = jnp.concatenate([adapter_first_factors[4], adapter_first_factors[5]], axis=1)
    lowrank_feedfwd = (
        matrix_product(second_normed_input, adapter_feedfwd) * second_adapter_mask
    ).astype(jnp.bfloat16)
    gate_projected = matrix_product(second_normed_input, gate_total) + matrix_product(
        lowrank_feedfwd[:, :adapter_columns_span], adapter_second_feedfwd[0]
    )
    up_projected = matrix_product(second_normed_input, up_total) + matrix_product(
        lowrank_feedfwd[:, adapter_columns_span:], adapter_second_feedfwd[1]
    )

    def swiglu(gate_arg, up_arg):
        return jax.nn.sigmoid(gate_arg) * gate_arg * up_arg

    swiglu_output = swiglu(gate_projected, up_projected).astype(jnp.bfloat16)
    down_total = lax.all_gather(down_matrix, "fsdp", axis=0, tiled=True)
    lowrank_down = (
        matrix_product(swiglu_output, adapter_first_down) * adapter_mask_repeated
    ).astype(jnp.bfloat16)
    down_result = matrix_product(swiglu_output, down_total) + matrix_product(
        lowrank_down, adapter_second_model[2]
    )
    layer_out = (valid_col * (hidden_mid + RESIDUAL_FACTOR * down_result)).astype(jnp.bfloat16)
    grad_out = cotangent[0].astype(jnp.float32) * valid_col
    gradient_down_result = (RESIDUAL_FACTOR * grad_out).astype(jnp.bfloat16)
    gradient_lowrank_down = (
        product_right_transposed(gradient_down_result, adapter_second_model[2]).astype(jnp.bfloat16)
        * adapter_mask_repeated
    )
    grad_b_down = product_left_transposed(lowrank_down, gradient_down_result)
    grad_a_down = product_left_transposed(swiglu_output, gradient_lowrank_down)
    gradient_swiglu = product_right_transposed(
        gradient_down_result, lax.all_gather(down_matrix, "fsdp", axis=0, tiled=True)
    )
    gradient_swiglu = gradient_swiglu + product_right_transposed(
        gradient_lowrank_down, adapter_first_down
    )
    _, swiglu_back = jax.vjp(swiglu, gate_projected, up_projected)
    gradient_gate_total, gradient_up_total = swiglu_back(gradient_swiglu)
    gradient_gate_total = gradient_gate_total.astype(jnp.bfloat16)
    gradient_up_total = gradient_up_total.astype(jnp.bfloat16)
    gradient_lowrank_feedfwd = (
        jnp.concatenate(
            [
                product_right_transposed(gradient_gate_total, adapter_second_feedfwd[0]).astype(
                    jnp.bfloat16
                ),
                product_right_transposed(gradient_up_total, adapter_second_feedfwd[1]).astype(
                    jnp.bfloat16
                ),
            ],
            axis=1,
        )
        * second_adapter_mask
    )
    gradient_second_gate = product_left_transposed(
        lowrank_feedfwd[:, :adapter_columns_span], gradient_gate_total
    )
    gradient_second_up = product_left_transposed(
        lowrank_feedfwd[:, adapter_columns_span:], gradient_up_total
    )
    gradient_first_feedfwd = product_left_transposed(second_normed_input, gradient_lowrank_feedfwd)
    weight_pieces = (
        lax.all_gather(gate_matrix, "fsdp", axis=0, tiled=True),
        lax.all_gather(up_matrix, "fsdp", axis=0, tiled=True),
    )
    block_cols = product_right_transposed(
        gradient_gate_total, weight_pieces[0]
    ) + product_right_transposed(gradient_up_total, weight_pieces[1])
    gradient_second_normed = block_cols
    gradient_second_normed = gradient_second_normed + product_right_transposed(
        gradient_lowrank_feedfwd, adapter_feedfwd
    )
    _, norm_two_back = jax.vjp(lambda hidden: rms_norm(hidden, feedfwd_norm_gain), hidden_mid)
    grad_mid = grad_out + norm_two_back(gradient_second_normed)[0]
    gradient_residual = (RESIDUAL_FACTOR * grad_mid).astype(jnp.bfloat16)
    gradient_lowrank_output = (
        product_right_transposed(gradient_residual, adapter_second_model[1]).astype(jnp.bfloat16)
        * adapter_mask_repeated
    )
    grad_b_out = product_left_transposed(lowrank_output, gradient_residual)
    grad_a_out = product_left_transposed(attention_token_rows, gradient_lowrank_output)
    gradient_attention = product_right_transposed(
        gradient_residual, lax.all_gather(output_matrix, "fsdp", axis=0, tiled=True)
    )
    gradient_attention = (
        gradient_attention
        + product_right_transposed(gradient_lowrank_output, adapter_first_factors[3])
    ).astype(jnp.bfloat16)
    grad_heads = lax.all_to_all(
        gradient_attention.reshape(row_count, KV_HEADS, query_width),
        "seq",
        split_axis=1,
        concat_axis=0,
        tiled=True,
    )
    grad_packed = attend_backward(heads_in, segment, log_totals, grad_heads, group_ratio)
    grad_tok = lax.all_to_all(grad_packed, "seq", split_axis=0, concat_axis=1, tiled=True)
    grad_query_r = (
        grad_tok[:, :, :query_width].reshape(row_count, HEADS, HEAD_DIM).astype(jnp.float32)
    )
    grad_key_r = grad_tok[:, :, query_width : query_width + HEAD_DIM].astype(jnp.float32)
    gradient_value_rows = grad_tok[:, :, query_width + HEAD_DIM :].reshape(
        row_count, KEY_HEAD_WIDTH
    )
    _, query_turn_back = jax.vjp(lambda vectors: rotate(vectors, cosine, sine_table), query_r)
    _, key_turn_back = jax.vjp(lambda vectors: rotate(vectors, cosine, sine_table), key_r)
    gradient_query_rows = (
        query_turn_back(grad_query_r)[0].reshape(row_count, MODEL_WIDTH).astype(jnp.bfloat16)
    )
    gradient_key_rows = (
        key_turn_back(grad_key_r)[0].reshape(row_count, KEY_HEAD_WIDTH).astype(jnp.bfloat16)
    )
    gradient_lowrank_attention = (
        jnp.concatenate(
            [
                product_right_transposed(gradient_query_rows, adapter_second_model[0]).astype(
                    jnp.bfloat16
                ),
                product_right_transposed(gradient_key_rows, adapter_second_keyvalue[0]).astype(
                    jnp.bfloat16
                ),
                product_right_transposed(gradient_value_rows, adapter_second_keyvalue[1]).astype(
                    jnp.bfloat16
                ),
            ],
            axis=1,
        )
        * third_adapter_mask
    )
    gradient_second_query = product_left_transposed(
        lowrank_attention[:, :adapter_columns_span], gradient_query_rows
    )
    gradient_second_key = product_left_transposed(
        lowrank_attention[:, adapter_columns_span : 2 * adapter_columns_span], gradient_key_rows
    )
    gradient_second_value = product_left_transposed(
        lowrank_attention[:, 2 * adapter_columns_span :], gradient_value_rows
    )
    gradient_first_attention = product_left_transposed(
        first_normed_input, gradient_lowrank_attention
    )
    weight_pieces = (
        lax.all_gather(query_matrix, "fsdp", axis=0, tiled=True),
        lax.all_gather(key_matrix, "fsdp", axis=0, tiled=True),
        lax.all_gather(value_matrix, "fsdp", axis=0, tiled=True),
    )
    block_cols = (
        product_right_transposed(gradient_query_rows, weight_pieces[0])
        + product_right_transposed(gradient_key_rows, weight_pieces[1])
        + product_right_transposed(gradient_value_rows, weight_pieces[2])
    )
    gradient_first_normed = block_cols
    gradient_first_normed = gradient_first_normed + product_right_transposed(
        gradient_lowrank_attention, adapter_input
    )
    _, norm_one_back = jax.vjp(lambda hidden: rms_norm(hidden, attention_norm_gain), hidden_in)
    grad_input = (grad_mid + norm_one_back(gradient_first_normed)[0]).astype(jnp.bfloat16)
    grad_a_all = jnp.stack(
        [
            gradient_first_attention[:, :adapter_columns_span],
            gradient_first_attention[:, adapter_columns_span : 2 * adapter_columns_span],
            gradient_first_attention[:, 2 * adapter_columns_span :],
            grad_a_out,
            gradient_first_feedfwd[:, :adapter_columns_span],
            gradient_first_feedfwd[:, adapter_columns_span:],
        ]
    )
    grad_b_all = jnp.stack([gradient_second_query, grad_b_out, grad_b_down])
    grad_kv_all = jnp.stack([gradient_second_key, gradient_second_value])
    grad_ffn_all = jnp.stack([gradient_second_gate, gradient_second_up])
    summed = lax.psum(
        (grad_a_all, grad_a_down, grad_b_all, grad_kv_all, grad_ffn_all), ("seq", "fsdp")
    )
    factor = ADAPTER_TOTAL / math.sqrt(PACK * lax.axis_size("fsdp"))
    return (
        layer_out[None],
        grad_input[None],
        summed[0] * factor,
        summed[1] * factor,
        summed[2] * factor,
        summed[3] * factor,
        summed[4] * factor,
    )


def solution(mesh):
    placed = (
        P("fsdp", "seq", None),
        P("fsdp", "seq", None),
        P("fsdp", None),
        P("fsdp", None),
        P(),
        P(),
        P("fsdp", None),
        P("fsdp", None),
        P("fsdp", None),
        P("fsdp", None),
        P("fsdp", None),
        P("fsdp", None),
        P("fsdp", None),
        P(),
        P(),
        P(),
        P(),
        P(),
    )
    return jax.shard_map(
        shards,
        mesh=mesh,
        in_specs=placed,
        out_specs=(P("fsdp", "seq", None), P("fsdp", "seq", None), P(), P(), P(), P(), P()),
        check_vma=False,
    )
```

profile of v0, /device:TPU:0, one launch (start us, length us, event | category | flops | bytes accessed | tf_op | source)
XLA Modules:
  0.0 2945.1 jit_solution(6945938635983823709)
XLA Ops:
  21.3 40.7 %all-gather.10.cloned.1.call-done = bf16[2048,512]{1,0:T(8,128)(2,1)} async-done(((bf16[256,512]{1,0:T(8,128)(2,1)}), bf16[2048,512]{1,0:T(8,128)(2,1)}) %all-gather.10.cloned.1.call-update) | async-done | bytes 2097168 | tf_op jit(solution)/shard_map/all_gather | solution.py:224
  67.3 44.5 %all-gather.12.cloned.1.call-done = bf16[2048,512]{1,0:T(8,128)(2,1)} async-done(((bf16[256,512]{1,0:T(8,128)(2,1)}), bf16[2048,512]{1,0:T(8,128)(2,1)}) %all-gather.12.cloned.1.call-update) | async-done | bytes 2097168 | tf_op jit(solution)/shard_map/all_gather | solution.py:225
  119.7 117.3 %all-gather.8.cloned.1.call-done = bf16[2048,2048]{1,0:T(8,128)(2,1)} async-done(((bf16[256,2048]{1,0:T(8,128)(2,1)}), bf16[2048,2048]{1,0:T(8,128)(2,1)}) %all-gather.8.cloned.1.call-update) | async-done | bytes 8388624 | tf_op jit(solution)/shard_map/all_gather | solution.py:223
  237.0 5.8 fusion.176
  254.2 4.6 all-to-all-start
  258.8 20.1 all-to-all-done
  282.4 33.9 %while.27 = (s32[]{:T(128)}, bf16[2,512,2,256]{3,1,0,2:T(8,128)(2,1)}, f32[2,2,4,512]{3,2,1,0:T(4,128)S(1)}, s32[2]{0:T(128)S(1)}, s32[1024]{0:T(1024)S(1)}, /*i...) while((s32[]{:T(128)}, ...), condition=%wide.region_8.9_spmd, body=%wide.region_5.8_spmd.sunk | while | flops 1125904896 | bytes 57293500 | solution.py:130
  288.2 4.3 fusion.267
  292.6 5.7 fusion.268
  305.1 4.3 fusion.267
  309.5 5.7 fusion.268
  319.7 3.8 all-to-all-start.1
  326.2 11.7 all-to-all-done.1
  342.9 18.7 all-gather.14.cloned.1.call-done
  361.6 6.1 fusion.179
  371.8 627.2 %all-gather.18.cloned.1.call-done = bf16[2048,8192]{1,0:T(8,128)(2,1)} async-done(((bf16[256,8192]{1,0:T(8,128)(2,1)}), bf16[2048,8192]{1,0:T(8,128)(2,1)}) %all-gather.18.cloned.1.call-update) | async-done | bytes 33554448 | tf_op jit(solution)/shard_map/all_gather | solution.py:269
  998.9 18.9 fusion.181
  1017.8 8.0 convolution_add_fusion.1
  1025.8 612.1 %all-gather.16.cloned.1.call-done = bf16[2048,8192]{1,0:T(8,128)(2,1)} async-done(((bf16[256,8192]{1,0:T(8,128)(2,1)}), bf16[2048,8192]{1,0:T(8,128)(2,1)}) %all-gather.16.cloned.1.call-update) | async-done | bytes 33554448 | tf_op jit(solution)/shard_map/all_gather | solution.py:268
  1638.0 19.7 fusion.180
  1657.7 8.1 convolution_add_fusion.2
  1665.8 611.4 %all-gather.20.cloned.1.call-done = bf16[8192,2048]{1,0:T(8,128)(2,1)} async-done(((bf16[1024,2048]{1,0:T(8,128)(2,1)}), bf16[8192,2048]{1,0:T(8,128)(2,1)}) %all-gather.20.cloned.1.call-update) | async-done | bytes 33554448 | tf_op jit(solution)/shard_map/all_gather | solution.py:286
  2277.2 18.5 fusion.133
  2295.7 13.0 multiply_convert_fusion
  2308.7 6.6 convolution_bitcast_fusion.1
  2321.6 16.9 fusion.183
  2338.5 17.9 convolution_add_fusion.11
  2368.1 3.5 all-to-all-start.2
  2371.6 4.2 fusion.87
  2389.3 116.1 %while.28 = (s32[]{:T(128)}, f32[1024,2,64]{0,2,1:T(8,128)S(1)}, f32[1024,2,64]{0,2,1:T(8,128)}, bf16[2,512,2,256]{3,1,0,2:T(8,128)(2,1)}, s32[2]{0:T(128)S(1)},...) while((s32[]{:T(128)}, f32[1024,2,64]{0,2,1:T(8,128)S(1)}, ...), condition=%wide.region_13.14_spmd.clone, body=%wide.region_11.13_spmd.clone.sunk | while | flops 2750018048 | bytes 175504240 | solution.py:172
  2393.0 8.2 fusion.278
  2403.1 12.1 fusion.280
  2415.2 12.0 fusion.281
  2433.5 5.1 fusion.282
  2438.6 8.1 fusion.283
  2450.7 8.2 fusion.278
  2460.9 12.1 fusion.280
  2473.0 12.0 fusion.281
  2491.3 5.1 fusion.282
  2496.4 8.1 fusion.283
  2512.0 3.6 all-to-all-start.3
  2517.1 7.8 pad_maximum_fusion
  2524.9 10.7 all-to-all-done.3
  2556.7 18.0 fusion.182
  2577.3 6.2 fusion.184
  2589.9 330.0 %all-reduce.7.cloned.1.call-done = (f32[6,2048,128]{2,1,0:T(8,128)}, f32[8192,128]{1,0:T(8,128)}, f32[3,128,2048]{2,1,0:T(8,128)}, f32[2,128,512]{2,1,0:T(8,128)}, f32[2,128,8192]{2,1,0:T(8,128)}) async-done(((f32[6,2048,128]{2,1,0:T(8,128)}, f32[8192,128]{1,0:T(8,128)}, f32[3,128,2048]{2,1,0:T(8,128)}, f32[2,128,512]{2,1,0:T(8,128)}, f32[2,128,8192]{2,1,0:T(8,128)}), (f32[6,2048,128]{2,1,0:T(8,128)}, ...) | async-done | bytes 22544400 | tf_op jit(solution)/shard_map/psum | solution.py:442
  2919.9 8.1 broadcast_multiply_fusion
  2928.0 3.5 broadcast_multiply_fusion.1
  (375 shorter events, 164.2 us)
Async XLA Ops:
  7.2 2288.5 %copy-start = (bf16[8192,128]{1,0:T(8,128)(2,1)S(1)}, bf16[8192,128]{1,0:T(8,128)(2,1)}, u32[]{:S(2)}) copy-start(bf16[8192,128]{1,0:T(8,128)(2,1)} %param.36) | copy-start | bytes 6291460
  7.2 54.9 %all-gather.10.cloned.1.call-start = ((), (), s32[]{:S(2)}) async-start(), calls=%async_computation.5 | async-start | bytes 2359296 | tf_op jit(solution)/shard_map/all_gather | solution.py:224
  7.9 103.9 %all-gather.12.cloned.1.call-start = ((), (), s32[]{:S(2)}) async-start(), calls=%async_computation.6 | async-start | bytes 2359296 | tf_op jit(solution)/shard_map/all_gather | solution.py:225
  8.7 228.3 %all-gather.8.cloned.1.call-start = ((), (), s32[]{:S(2)}) async-start(), calls=%async_computation.4 | async-start | bytes 9437184 | tf_op jit(solution)/shard_map/all_gather | solution.py:223
  9.4 352.2 %all-gather.14.cloned.1.call-start = ((), (), s32[]{:S(2)}) async-start(), calls=%async_computation.7 | async-start | bytes 9437184 | tf_op jit(solution)/shard_map/all_gather | solution.py:258
  10.0 988.9 %all-gather.18.cloned.1.call-start = ((), (), s32[]{:S(2)}) async-start(), calls=%async_computation.9 | async-start | bytes 37748736 | tf_op jit(solution)/shard_map/all_gather | solution.py:269
  10.6 1627.4 %all-gather.16.cloned.1.call-start = ((), (), s32[]{:S(2)}) async-start(), calls=%async_computation.8 | async-start | bytes 37748736 | tf_op jit(solution)/shard_map/all_gather | solution.py:268
  11.2 2266.0 %all-gather.20.cloned.1.call-start = ((), (), s32[]{:S(2)}) async-start(), calls=%async_computation.10 | async-start | bytes 37748736 | tf_op jit(solution)/shard_map/all_gather | solution.py:286
  14.9 235.4 %copy-start.50 = (f32[256,64]{0,1:T(8,128)}, f32[256,64]{0,1:T(8,128)S(1)}, u32[]{:S(2)}) copy-start(f32[256,64]{0,1:T(8,128)S(1)} %get-tuple-element.218) | copy-start | bytes 196612
  15.0 235.6 %copy-start.48 = (f32[256,64]{0,1:T(8,128)}, f32[256,64]{0,1:T(8,128)S(1)}, u32[]{:S(2)}) copy-start(f32[256,64]{0,1:T(8,128)S(1)} %get-tuple-element.217) | copy-start | bytes 196612
  15.3 221.7 %copy-start.88 = (f32[256]{0:T(256)}, f32[256]{0:T(256)S(1)}, u32[]{:S(2)}) copy-start(f32[256]{0:T(256)S(1)} %fusion.161) | copy-start | bytes 3076
  254.2 24.7 all-to-all-start
  316.2 9.9 copy-start.3
  316.3 9.9 copy-start.46
  316.3 7.2 copy-start.57
  319.7 18.2 all-to-all-start.1
  323.7 2035.8 %copy-start.86 = (f32[256]{0:T(256)}, f32[256]{0:T(256)S(1)}, u32[]{:S(2)}) copy-start(f32[256]{0:T(256)S(1)} %dynamic-slice_select_fusion) | copy-start | bytes 3076
  342.9 24.8 copy-start.16
  998.9 18.9 copy-start.25
  1638.0 19.7 copy-start.26
  2308.7 9.0 copy-start.32
  2308.7 6.6 copy-start.27
  2308.7 7.7 copy-start.34
  2338.5 17.9 copy-start.43
  2338.5 17.9 copy-start.45
  2356.4 6.6 slice-start
  2360.2 5.3 copy-start.10
  2368.1 17.9 all-to-all-start.2
  2371.6 4.2 copy-start.11
  2371.6 5.5 copy-start.33
  2383.9 5.4 copy-start.4
  2383.9 5.4 copy-start.5
  2383.9 5.4 copy-start.47
  2383.9 5.4 copy-start.82
  2433.5 5.1 copy-start.72
  2491.3 5.1 copy-start.72
  2509.2 6.4 copy-start.37
  2509.2 6.4 copy-start.63
  2509.2 6.4 copy-start.87
  2512.0 23.6 all-to-all-start.3
  2515.6 404.3 %all-reduce.7.cloned.1.call-start = ((), (), s32[]{:S(2)}) async-start(), calls=%async_computation.11 | async-start | bytes 45088768 | tf_op jit(solution)/shard_map/psum | solution.py:442
  2524.9 13.8 copy-start.51
  2536.9 4.4 copy-start.49
  2539.8 6.2 copy-start.29
  2556.7 18.0 copy-start.8
  2577.3 6.2 copy-start.40
  2919.9 8.1 copy-start.24
  2928.0 3.9 copy-start.31
  (67 other events, 149.9 us)
Sparse Core Ops, SparseCore 0:
  10.1 51.8 all-gather.9
  64.2 47.6 all-gather.11
  114.0 122.9 all-gather.7
  239.0 122.6 all-gather.13
  363.0 635.8 all-gather.17
  1000.3 637.6 all-gather.15
  1639.5 637.6 all-gather.19
  2556.8 363.0 all-reduce.6
where the time goes:
time: 2950 us
  waiting for transfers between devices  2450 us (83%)
  matrix products  309 us (10%)
  other arithmetic  78 us (3%)
  local copies, waits for them, and re-layouts  69 us (2%)
    all_gather x1, waiting for transfers between devices, shards(): lax.all_gather(up_matrix, 'fsdp', axis=0, tiled=True)  627 us
    all_gather x1, waiting for transfers between devices, shards(): lax.all_gather(gate_matrix, 'fsdp', axis=0, tiled=True)  612 us
    all_gather x1, waiting for transfers between devices, shards(): down_total = lax.all_gather(down_matrix, 'fsdp', axis=0, tiled=True)  611 us
    psum x1, waiting for transfers between devices, shards(): lax.psum((grad_a_all, grad_a_down, grad_b_all, grad_kv_all, grad_ffn_all)...  330 us
    all_gather x1, waiting for transfers between devices, shards(): lax.all_gather(query_matrix, 'fsdp', axis=0, tiled=True)  117 us
    dot_general x18, matrix products, matrix_product(): return jnp.dot(left, right, preferred_element_type=jnp.float32)  107 us
    dot_general x18, matrix products, product_right_transposed(): lax.dot_general(left, right, (((1,), (1,)), ((), ())), preferred_element_...  91.7 us
  transfers between devices with their start and end apart: 12, of which 12 were waited for; matrix products, arithmetic and copies ran while one was open for 7% of the time, Pallas kernels for 0%

commit v1 on v0

v1 whole, which is shorter than its diff:
```python
import math

import jax
import jax.numpy as jnp
from jax import lax
from jax.experimental import pallas as pl
from jax.experimental.pallas import tpu as pltpu
from jax.sharding import PartitionSpec as P

MODEL_WIDTH = 2048
HEADS = 32
KV_HEADS = 8
HEAD_DIM = 64
ADAPTER_RANK = 16
ADAPTER_TOTAL = 8
PACK = 1024
QBLOCK = 256
SPAN = ADAPTER_TOTAL * ADAPTER_RANK
GROUP = HEADS // KV_HEADS

SCORE_SCALE = 0.015625
RESIDUAL_FACTOR = 0.22
NORM_EPSILON = 1e-05
ROPE_BASE = 10000000.0
MASK_FILL = 1e30

BF16 = jnp.bfloat16
F32 = jnp.float32


def mm(left, right):
    return jnp.dot(left, right, preferred_element_type=F32)


def mm_nt(left, right):
    return lax.dot_general(left, right, (((1,), (1,)), ((), ())), preferred_element_type=F32)


def mm_tn(left, right):
    return lax.dot_general(left, right, (((0,), (0,)), ((), ())), preferred_element_type=F32)


def rms_norm(hidden, gain_vec):
    mean_square = jnp.mean(hidden * hidden, axis=-1, keepdims=True)
    return hidden * lax.rsqrt(mean_square + NORM_EPSILON) * gain_vec


def pack_tables(seq_lengths, adapter_id, token_count, adapter_count):
    slots = seq_lengths.shape[0]
    places = jnp.arange(token_count, dtype=jnp.int32)
    seq_ends = jnp.cumsum(seq_lengths)
    seq_starts = seq_ends - seq_lengths
    used_len = seq_ends[slots - 1]
    segment = jnp.sum((places[:, None] >= seq_ends[None, :]).astype(jnp.int32), axis=1)
    member = segment[:, None] == jnp.arange(slots, dtype=jnp.int32)[None, :]
    start_tok = jnp.sum(jnp.where(member, seq_starts[None, :], 0), axis=1) + jnp.where(
        segment == slots, used_len, 0
    )
    position = places - start_tok
    valid_row = segment < slots
    chosen = adapter_id[:, None] == jnp.arange(adapter_count, dtype=jnp.int32)[None, :]
    onehot = jnp.sum(jnp.where(member[:, :, None] & chosen[None, :, :], 1.0, 0.0), axis=1).astype(F32)
    return (segment, position, valid_row, onehot)


def rope_tables(position, head_size, copies):
    frequency = ROPE_BASE ** (-(jnp.arange(head_size // 2, dtype=F32) * 2.0) / head_size)
    angles = position.astype(F32)[:, None] * frequency[None, :]
    cosine, sine = jnp.cos(angles), jnp.sin(angles)
    return (jnp.tile(cosine, (1, 2 * copies)), jnp.tile(sine, (1, 2 * copies)))


def bits_down(count):
    bits, bit = [], count >> 1
    while bit:
        bits.append(bit)
        bit >>= 1
    return bits


def relative_order(count):
    order = [0]
    for bit in bits_down(count):
        order = order + [o ^ bit for o in order]
    return order


def swap(block, axis, offset):
    count = lax.axis_size(axis)
    return lax.ppermute(block, axis, [(i, i ^ offset) for i in range(count)])


def gather_relative(block, axis):
    pieces = [block]
    for bit in bits_down(lax.axis_size(axis)):
        pieces = pieces + [swap(piece, axis, bit) for piece in pieces]
    return pieces


def reduce_relative(pieces, axis):
    for bit in reversed(bits_down(lax.axis_size(axis))):
        half = len(pieces) // 2
        got = [swap(piece.astype(BF16), axis, bit) for piece in pieces[half:]]
        pieces = [mine.astype(F32) + other.astype(F32) for mine, other in zip(pieces[:half], got)]
    return pieces[0]


def cycle_of(count):
    return list(range(0, count, 2)) + list(range(count - 1, 0, -2))


class Rings:
    WINDOW = 2

    def __init__(self):
        self.count = lax.axis_size("fsdp")
        cycle = cycle_of(self.count)
        place = {device: k for k, device in enumerate(cycle)}
        table = [
            [cycle[(place[device] - k) % self.count] for k in range(self.count)]
            for device in range(self.count)
        ]
        self.owner = lax.dynamic_index_in_dim(
            jnp.array(table, jnp.int32), lax.axis_index("fsdp"), 0, keepdims=False
        )
        ahead = [(cycle[k], cycle[(k + 1) % self.count]) for k in range(self.count)]
        self.perms = (ahead, [(b, a) for a, b in ahead])
        self.sent = ([], [])

    def send(self, way, block):
        sent = self.sent[way]
        if len(sent) >= self.WINDOW:
            block, _ = lax.optimization_barrier((block, sent[-self.WINDOW]))
        got = lax.ppermute(block, "fsdp", self.perms[way])
        sent.append(got)
        return got

    def gather(self, blocks):
        half = self.count // 2
        lag = max(half // 2, 1)
        found = [{0: block} for block in blocks]
        latest = [[block, block] for block in blocks]
        for time in range(half + lag * (len(blocks) - 1)):
            for which in range(len(blocks)):
                step = time - lag * which + 1
                if not 1 <= step <= half:
                    continue
                for way in (0, 1):
                    if step == half and way != which % 2:
                        continue
                    got = self.send(way, latest[which][way])
                    latest[which][way] = got
                    found[which][step if way == 0 else self.count - step] = got
        return [[f[k] for k in range(self.count)] for f in found]


def place_blocks(pieces, counts, targets):
    rows = pieces[0].shape[0] // counts
    columns = pieces[0].shape[1]
    total = len(pieces) * counts

    def body(target_ref, *refs):
        out_ref, held, came, left = refs[-4:]
        arrivals, departures = [], []
        for i in range(len(pieces)):
            for j in range(counts):
                k = i * counts + j
                first = pl.multiple_of(target_ref[k] * rows, rows)
                arrivals.append(
                    pltpu.make_async_copy(
                        refs[i].at[pl.ds(j * rows, rows), :], held.at[k], came.at[k]
                    )
                )
                departures.append(
                    pltpu.make_async_copy(
                        held.at[k], out_ref.at[pl.ds(first, rows), :], left.at[k]
                    )
                )
        for copy in arrivals:
            copy.start()
        for arrival, departure in zip(arrivals, departures):
            arrival.wait()
            departure.start()
        for copy in departures:
            copy.wait()

    return pl.pallas_call(
        body,
        out_shape=jax.ShapeDtypeStruct((rows * total, columns), pieces[0].dtype),
        grid_spec=pltpu.PrefetchScalarGridSpec(
            num_scalar_prefetch=1,
            grid=(),
            in_specs=[pl.BlockSpec(memory_space=pl.ANY)] * len(pieces),
            out_specs=pl.BlockSpec(memory_space=pl.ANY),
            scratch_shapes=[
                pltpu.VMEM((total, rows, columns), pieces[0].dtype),
                pltpu.SemaphoreType.DMA((total,)),
                pltpu.SemaphoreType.DMA((total,)),
            ],
        ),
        cost_estimate=pl.CostEstimate(
            flops=0, transcendentals=0, bytes_accessed=4 * rows * total * columns
        ),
        name="place_blocks",
    )(targets.astype(jnp.int32), *pieces)


def half_lanes(shape):
    lane = lax.broadcasted_iota(jnp.int32, shape, 1)
    return lane % HEAD_DIM < HEAD_DIM // 2


def turn_tile(x, cosine, sine):
    quarter = HEAD_DIM // 2
    ahead = pltpu.roll(x, 2 * HEAD_DIM - quarter, 1)
    behind = pltpu.roll(x, quarter, 1)
    return x * cosine + jnp.where(half_lanes(x.shape), -ahead, behind) * sine


def dot_tn(left, right):
    return lax.dot_general(left, right, (((0,), (0,)), ((), ())), preferred_element_type=F32)


def dot_nt(left, right):
    return lax.dot_general(left, right, (((1,), (1,)), ((), ())), preferred_element_type=F32)


def allowed_pairs(seg_col, seg_row, block):
    keys = (block + 1) * QBLOCK
    shape = (keys, QBLOCK)
    key_at = lax.broadcasted_iota(jnp.int32, shape, 0)
    query_at = lax.broadcasted_iota(jnp.int32, shape, 1) + block * QBLOCK
    same = seg_col[:keys, :] == seg_row[:, block * QBLOCK : keys]
    return same & (key_at <= query_at)


def forward_body(
    blocks, slot_ref, q_ref, k_ref, v_ref, cos_ref, sin_ref, col_ref, row_ref,
    qn_ref, kn_ref, vn_ref, out_ref, lse_ref,
):
    for j in range(blocks):
        here = slice(j * QBLOCK, (j + 1) * QBLOCK)
        there = pl.ds(pl.multiple_of(slot_ref[j] * QBLOCK, QBLOCK), QBLOCK)
        cosine, sine = cos_ref[here, :], sin_ref[here, :]
        qn_ref[here, :] = turn_tile(q_ref[there, :], cosine, sine).astype(BF16)
        kn_ref[here, :] = turn_tile(k_ref[there, :], cosine, sine).astype(BF16)
        vn_ref[here, :] = v_ref[there, :].astype(BF16)
    lane = lax.broadcasted_iota(jnp.int32, (QBLOCK, 2 * HEAD_DIM), 1)
    row = lax.broadcasted_iota(jnp.int32, (2 * HEAD_DIM, QBLOCK), 0)
    for i in range(blocks):
        here = slice(i * QBLOCK, (i + 1) * QBLOCK)
        keys = (i + 1) * QBLOCK
        allowed = allowed_pairs(col_ref[...], row_ref[...], i)
        query = (qn_ref[here, :].astype(F32) * SCORE_SCALE).astype(BF16)
        outs = []
        for e in range(2):
            mine = jnp.where(lane // HEAD_DIM == e, query, jnp.zeros_like(query))
            scores = jnp.where(allowed, dot_nt(kn_ref[:keys, :], mine), -MASK_FILL)
            most = jnp.max(scores, axis=0, keepdims=True)
            exponent = jnp.exp(scores - most)
            total = jnp.sum(exponent, axis=0, keepdims=True)
            probs = (exponent * (1.0 / total)).astype(BF16)
            lse_ref[0, e : e + 1, here] = most + jnp.log(total)
            outs.append(dot_tn(vn_ref[:keys, :], probs))
        out = jnp.where(row < HEAD_DIM, outs[0], outs[1]).T
        there = pl.ds(pl.multiple_of(slot_ref[i] * QBLOCK, QBLOCK), QBLOCK)
        out_ref[there, :] = out.astype(BF16)


def backward_body(
    blocks, slot_ref, qn_ref, kn_ref, vn_ref, do_ref, lse_ref, cos_ref, sin_ref, col_ref, row_ref,
    dq_ref, dk_ref, dv_ref, dk_sum, dv_sum,
):
    pairs_per_group = GROUP // 2
    step = lax.rem(pl.program_id(0), pairs_per_group)

    @pl.when(step == 0)
    def _():
        dk_sum[...] = jnp.zeros_like(dk_sum)
        dv_sum[...] = jnp.zeros_like(dv_sum)

    lane = lax.broadcasted_iota(jnp.int32, (QBLOCK, 2 * HEAD_DIM), 1)
    row = lax.broadcasted_iota(jnp.int32, (2 * HEAD_DIM, QBLOCK), 0)
    for i in range(blocks):
        here = slice(i * QBLOCK, (i + 1) * QBLOCK)
        there = pl.ds(pl.multiple_of(slot_ref[i] * QBLOCK, QBLOCK), QBLOCK)
        keys = (i + 1) * QBLOCK
        allowed = allowed_pairs(col_ref[...], row_ref[...], i)
        query = (qn_ref[here, :].astype(F32) * SCORE_SCALE).astype(BF16)
        grad = do_ref[there, :]
        outs = []
        for e in range(2):
            mine = jnp.where(lane // HEAD_DIM == e, query, jnp.zeros_like(query))
            grad_mine = jnp.where(lane // HEAD_DIM == e, grad, jnp.zeros_like(grad))
            scores = jnp.where(allowed, dot_nt(kn_ref[:keys, :], mine), -MASK_FILL)
            probs = jnp.exp(scores - lse_ref[0, e : e + 1, here])
            grad_probs = dot_nt(vn_ref[:keys, :], grad_mine)
            delta = jnp.sum(probs * grad_probs, axis=0, keepdims=True)
            grad_scores = (probs * (grad_probs - delta)).astype(BF16)
            dv_sum[:keys, :] += jnp.dot(probs.astype(BF16), grad_mine, preferred_element_type=F32)
            dk_sum[:keys, :] += jnp.dot(grad_scores, mine, preferred_element_type=F32)
            outs.append(dot_tn(kn_ref[:keys, :], grad_scores))
        out = jnp.where(row < HEAD_DIM, outs[0], outs[1]).T * SCORE_SCALE
        out = out.astype(BF16).astype(F32)
        dq_ref[there, :] = turn_tile(out, cos_ref[here, :], -sin_ref[here, :]).astype(BF16)

    @pl.when(step == pairs_per_group - 1)
    def _():
        for j in range(blocks):
            here = slice(j * QBLOCK, (j + 1) * QBLOCK)
            there = pl.ds(pl.multiple_of(slot_ref[j] * QBLOCK, QBLOCK), QBLOCK)
            dk = dk_sum[here, :]
            dk = (dk + pltpu.roll(dk, HEAD_DIM, 1)).astype(BF16).astype(F32)
            dk_ref[there, :] = turn_tile(dk, cos_ref[here, :], -sin_ref[here, :]).astype(BF16)
            dv = dv_sum[here, :]
            dv_ref[there, :] = (dv + pltpu.roll(dv, HEAD_DIM, 1)).astype(BF16)


def attention_specs():
    tile = pl.BlockSpec((PACK, 2 * HEAD_DIM), lambda p, slot: (0, p))
    group = pl.BlockSpec((PACK, 2 * HEAD_DIM), lambda p, slot: (0, p // (GROUP // 2)))
    lse = pl.BlockSpec((1, 2, PACK), lambda p, slot: (p, 0, 0))
    table = pl.BlockSpec((PACK, 2 * HEAD_DIM), lambda p, slot: (0, 0))
    col = pl.BlockSpec((PACK, 1), lambda p, slot: (0, 0))
    row = pl.BlockSpec((1, PACK), lambda p, slot: (0, 0))
    return tile, group, lse, [table, table, col, row]


def attend_forward(slots, query, key, value, tables):
    pairs = query.shape[1] // (2 * HEAD_DIM)
    groups = key.shape[1] // (2 * HEAD_DIM)
    tile, group, lse, rest = attention_specs()
    blocks = PACK // QBLOCK
    return pl.pallas_call(
        lambda *refs: forward_body(blocks, *refs),
        grid_spec=pltpu.PrefetchScalarGridSpec(
            num_scalar_prefetch=1,
            grid=(pairs,),
            in_specs=[tile, group, group] + rest,
            out_specs=[tile, group, group, tile, lse],
        ),
        out_shape=[
            jax.ShapeDtypeStruct((PACK, pairs * 2 * HEAD_DIM), BF16),
            jax.ShapeDtypeStruct((PACK, groups * 2 * HEAD_DIM), BF16),
            jax.ShapeDtypeStruct((PACK, groups * 2 * HEAD_DIM), BF16),
            jax.ShapeDtypeStruct((PACK, pairs * 2 * HEAD_DIM), BF16),
            jax.ShapeDtypeStruct((pairs, 2, PACK), F32),
        ],
        cost_estimate=pl.CostEstimate(
            flops=4 * pairs * 2 * PACK * PACK * HEAD_DIM,
            transcendentals=pairs * PACK * PACK,
            bytes_accessed=8 * PACK * MODEL_WIDTH,
        ),
        name="attend_forward",
    )(slots, query, key, value, *tables)


def attend_backward(slots, saved, grad, log_totals, tables):
    query, key, value = saved
    pairs = query.shape[1] // (2 * HEAD_DIM)
    groups = key.shape[1] // (2 * HEAD_DIM)
    tile, group, lse, rest = attention_specs()
    blocks = PACK // QBLOCK
    return pl.pallas_call(
        lambda *refs: backward_body(blocks, *refs),
        grid_spec=pltpu.PrefetchScalarGridSpec(
            num_scalar_prefetch=1,
            grid=(pairs,),
            in_specs=[tile, group, group, tile, lse] + rest,
            out_specs=[tile, group, group],
            scratch_shapes=[pltpu.VMEM((PACK, 2 * HEAD_DIM), F32)] * 2,
        ),
        out_shape=[
            jax.ShapeDtypeStruct((PACK, pairs * 2 * HEAD_DIM), BF16),
            jax.ShapeDtypeStruct((PACK, groups * 2 * HEAD_DIM), BF16),
            jax.ShapeDtypeStruct((PACK, groups * 2 * HEAD_DIM), BF16),
        ],
        cost_estimate=pl.CostEstimate(
            flops=10 * pairs * 2 * PACK * PACK * HEAD_DIM,
            transcendentals=pairs * PACK * PACK,
            bytes_accessed=8 * PACK * MODEL_WIDTH,
        ),
        name="attend_backward",
    )(slots, query, key, value, grad, log_totals, *tables)


def reverse_bits(value, count):
    out, bit, other = 0, 1, count >> 1
    while other:
        out = out + jnp.where((value & bit) != 0, other, 0)
        bit, other = bit << 1, other >> 1
    return out


def reduce_scatter_rows(total):
    count = lax.axis_size("fsdp")
    me = lax.axis_index("fsdp")
    for bit in reversed(bits_down(count)):
        half = total.shape[0] // 2
        high = ((me & bit) != 0).astype(jnp.int32)
        keep = lax.dynamic_slice_in_dim(total, high * half, half, 0)
        give = lax.dynamic_slice_in_dim(total, (1 - high) * half, half, 0)
        got = swap(give.astype(BF16), "fsdp", bit)
        total = (keep.astype(F32) + got.astype(F32)).astype(BF16)
    return total


def share_out(total):
    count, seqs = lax.axis_size("fsdp"), lax.axis_size("seq")
    me, me_seq = lax.axis_index("fsdp"), lax.axis_index("seq")
    rows, columns = total.shape
    piece = reduce_scatter_rows(total.astype(BF16))
    for bit in bits_down(count):
        piece = jnp.concatenate([piece, swap(piece, "fsdp", bit)], axis=0)
    pieces = gather_relative(piece, "seq")
    targets = jnp.stack(
        [
            (me_seq ^ s) * count + reverse_bits(me ^ o, count)
            for s in relative_order(seqs)
            for o in relative_order(count)
        ]
    )
    return place_blocks(pieces, count, targets).reshape(seqs, rows, columns)


def shards(
    tokens,
    cotangent,
    lengths,
    sequence_adapter,
    attention_norm_gain,
    feedfwd_norm_gain,
    query_matrix,
    key_matrix,
    value_matrix,
    output_matrix,
    gate_matrix,
    up_matrix,
    down_matrix,
    adapter_first_factors,
    adapter_first_down,
    adapter_second_model,
    adapter_second_keyvalue,
    adapter_second_feedfwd,
):
    seqs, fsdps = lax.axis_size("seq"), lax.axis_size("fsdp")
    me = lax.axis_index("seq")
    order = relative_order(seqs)
    peers = [me ^ o for o in order]
    resid_in = tokens[0]
    row_count = resid_in.shape[0]
    width = MODEL_WIDTH // seqs
    kv_width = KV_HEADS * HEAD_DIM // seqs
    my_groups = KV_HEADS // seqs
    feed_units = gate_matrix.shape[1]
    unit_block = feed_units // (seqs * fsdps)
    units = feed_units // seqs
    parts = units // width

    def columns_of(array, peer, count):
        return lax.dynamic_slice_in_dim(array, peer * count, count, array.ndim - 1)

    def rows_of(array, peer):
        return lax.dynamic_slice_in_dim(array, peer * row_count, row_count, 0)

    def relative_rows(array):
        return jnp.concatenate([rows_of(array, peer) for peer in peers], axis=0)

    def blocks_of(array):
        return [array[k * row_count : (k + 1) * row_count] for k in range(seqs)]

    def exchange(pieces):
        return [p if o == 0 else swap(p, "seq", o) for o, p in zip(order, pieces)]

    def place_columns(pieces):
        rows, count = pieces[0].shape
        whole = jnp.zeros((rows, count * seqs), pieces[0].dtype)
        for peer, piece in zip(peers, pieces):
            whole = lax.dynamic_update_slice(whole, piece, (0, peer * count))
        return whole

    def my_units(matrix):
        parted = matrix.reshape(matrix.shape[0], fsdps, seqs, unit_block)
        return lax.dynamic_index_in_dim(parted, me, 2, keepdims=False).reshape(
            matrix.shape[0], units
        )

    rings = Rings()
    qkv_share = jnp.concatenate(
        [
            columns_of(query_matrix, me, width),
            columns_of(key_matrix, me, kv_width),
            columns_of(value_matrix, me, kv_width),
        ],
        axis=1,
    )
    out_share = columns_of(output_matrix, me, width)
    gate_share, up_share = my_units(gate_matrix), my_units(up_matrix)
    down_share = lax.dynamic_slice_in_dim(down_matrix, me * unit_block, unit_block, 0)
    lists = rings.gather([qkv_share, out_share, gate_share, up_share, down_share])
    qkv_mine, out_mine, gate_full, up_full, down_full = (
        place_blocks(blocks, 1, rings.owner) for blocks in lists
    )

    segment, position, valid_row, onehot = pack_tables(
        lengths[0], sequence_adapter[0], PACK, ADAPTER_TOTAL
    )
    valid_all = jnp.where(valid_row, 1.0, 0.0).astype(F32)[:, None]
    mask_all = jnp.repeat(onehot, ADAPTER_RANK, axis=1).astype(BF16)
    valid_rel = relative_rows(valid_all)
    mask_rel = relative_rows(mask_all)
    valid_col, mask_own = valid_rel[:row_count], mask_rel[:row_count]
    mask_own_three = jnp.tile(mask_own, (1, 3))
    mask_rel_two = jnp.tile(mask_rel, (1, 2))
    mask_rel_three = jnp.tile(mask_rel, (1, 3))
    cosine, sine = rope_tables(position, HEAD_DIM, 2)
    tables = (cosine, sine, segment[:, None], segment[None, :])
    slot_of = [0] * seqs
    for k, o in enumerate(order):
        slot_of[o] = k
    slot_table = jnp.array(slot_of, jnp.int32)
    sub = row_count // QBLOCK if row_count >= QBLOCK else 1
    if row_count >= QBLOCK:
        slots = jnp.stack(
            [
                slot_table[me ^ (j // sub)] * sub + j % sub
                for j in range(PACK // QBLOCK)
            ]
        )
    else:
        slots = jnp.arange(PACK // QBLOCK, dtype=jnp.int32)

    def to_kernel(array):
        if row_count >= QBLOCK:
            return array
        whole = jnp.zeros_like(array)
        for peer, piece in zip(peers, blocks_of(array)):
            whole = lax.dynamic_update_slice(whole, piece, (peer * row_count, 0))
        return whole

    def from_kernel(array):
        return array if row_count >= QBLOCK else relative_rows(array)

    hidden_in = resid_in.astype(F32)
    normed_own = rms_norm(hidden_in, attention_norm_gain).astype(BF16)
    normed_one = jnp.concatenate(gather_relative(normed_own, "seq"), axis=0)
    first_qkv = jnp.concatenate([adapter_first_factors[k] for k in range(3)], axis=1)
    low_qkv = (mm(normed_one, first_qkv) * mask_rel_three).astype(BF16)
    low_q, low_k, low_v = (low_qkv[:, k * SPAN : (k + 1) * SPAN] for k in range(3))
    second_q = [columns_of(adapter_second_model[0], peer, width) for peer in peers]
    second_k = [columns_of(adapter_second_keyvalue[0], peer, kv_width) for peer in peers]
    second_v = [columns_of(adapter_second_keyvalue[1], peer, kv_width) for peer in peers]

    def twice(rows):
        heads = [rows[:, g * HEAD_DIM : (g + 1) * HEAD_DIM] for g in range(my_groups)]
        return jnp.concatenate([h for h in heads for _ in (0, 1)], axis=1)

    projected = mm(normed_one, qkv_mine)
    query = projected[:, :width] + mm(low_q, second_q[0])
    key = projected[:, width : width + kv_width] + mm(low_k, second_k[0])
    value = projected[:, width + kv_width :] + mm(low_v, second_v[0])
    *saved, attn_heads, log_totals = attend_forward(
        slots, to_kernel(query), to_kernel(twice(key)), to_kernel(twice(value)), tables
    )
    attn_heads = from_kernel(attn_heads)
    attn_own = place_columns(exchange(blocks_of(attn_heads)))
    out_weights = gather_relative(out_mine, "seq")
    low_o = (mm(attn_own, adapter_first_factors[3]) * mask_own).astype(BF16)
    branch = place_columns([mm(attn_own, piece) for piece in out_weights]) + mm(
        low_o, adapter_second_model[1]
    )
    hidden_mid = hidden_in + RESIDUAL_FACTOR * branch
    normed_two_own = rms_norm(hidden_mid, feedfwd_norm_gain).astype(BF16)

    normed_two = jnp.concatenate(gather_relative(normed_two_own, "seq"), axis=0)
    cot_all = jnp.concatenate(gather_relative(cotangent[0], "seq"), axis=0)
    first_ffn = jnp.concatenate([adapter_first_factors[4], adapter_first_factors[5]], axis=1)
    low_ffn = (mm(normed_two, first_ffn) * mask_rel_two).astype(BF16)
    low_g, low_u = low_ffn[:, :SPAN], low_ffn[:, SPAN:]
    second_gate = my_units(adapter_second_feedfwd[0])
    second_up = my_units(adapter_second_feedfwd[1])
    gate = mm(normed_two, gate_full) + mm(low_g, second_gate)
    up = mm(normed_two, up_full) + mm(low_u, second_up)

    def swiglu(gate_arg, up_arg):
        return jax.nn.sigmoid(gate_arg) * gate_arg * up_arg

    act = swiglu(gate, up).astype(BF16)
    first_down = lax.dynamic_index_in_dim(
        adapter_first_down.reshape(fsdps, seqs, unit_block, SPAN), me, 1, keepdims=False
    ).reshape(units, SPAN)
    low_d = (mm(act, first_down) * mask_rel).astype(BF16)
    down_part = mm(act, down_full) + mm(low_d, adapter_second_model[2])
    down_sum = reduce_relative(blocks_of(down_part), "seq")
    layer_out = (valid_col * (hidden_mid + RESIDUAL_FACTOR * down_sum)).astype(BF16)

    grad_out = cotangent[0].astype(F32) * valid_col
    grad_down = (RESIDUAL_FACTOR * (cot_all.astype(F32) * valid_rel)).astype(BF16)
    grad_low_d = mm_nt(grad_down, adapter_second_model[2]).astype(BF16) * mask_rel
    grad_b_down = mm_tn(low_d, grad_down)
    grad_a_down = mm_tn(grad_low_d, act)
    grad_act = mm_nt(grad_down, down_full) + mm_nt(grad_low_d, first_down)
    _, swiglu_back = jax.vjp(swiglu, gate, up)
    grad_gate, grad_up = swiglu_back(grad_act)
    grad_gate, grad_up = grad_gate.astype(BF16), grad_up.astype(BF16)
    grad_low_ffn = (
        jnp.concatenate([mm_nt(grad_gate, second_gate), mm_nt(grad_up, second_up)], axis=1).astype(
            BF16
        )
        * mask_rel_two
    )
    grad_b_gate = mm_tn(low_g, grad_gate)
    grad_b_up = mm_tn(low_u, grad_up)
    grad_a_ffn = mm_tn(grad_low_ffn, normed_two)
    grad_normed_two = (
        mm_nt(grad_gate, gate_full) + mm_nt(grad_up, up_full) + mm_nt(grad_low_ffn, first_ffn)
    )
    grad_normed_two = reduce_relative(blocks_of(grad_normed_two), "seq")
    _, norm_two_back = jax.vjp(lambda hidden: rms_norm(hidden, feedfwd_norm_gain), hidden_mid)
    grad_mid = grad_out + norm_two_back(grad_normed_two)[0]

    grad_branch = (RESIDUAL_FACTOR * grad_mid).astype(BF16)
    grad_low_o = mm_nt(grad_branch, adapter_second_model[1]).astype(BF16) * mask_own
    grad_b_out = mm_tn(low_o, grad_branch)
    grad_a_out = mm_tn(grad_low_o, attn_own)
    grad_attn = mm_nt(grad_low_o, adapter_first_factors[3])
    for peer, piece in zip(peers, out_weights):
        grad_attn = grad_attn + mm_nt(columns_of(grad_branch, peer, width), piece)
    grad_attn = grad_attn.astype(BF16)
    grad_heads = jnp.concatenate(
        exchange([columns_of(grad_attn, peer, width) for peer in peers]), axis=0
    )
    grad_query, grad_key, grad_value = (
        from_kernel(g)
        for g in attend_backward(slots, saved, to_kernel(grad_heads), log_totals, tables)
    )

    def once(rows):
        return jnp.concatenate(
            [rows[:, 2 * g * HEAD_DIM : (2 * g + 1) * HEAD_DIM] for g in range(my_groups)], axis=1
        )

    grad_key, grad_value = once(grad_key), once(grad_value)
    grad_qkv = jnp.concatenate([grad_query, grad_key, grad_value], axis=1)
    grad_pieces = exchange(blocks_of(grad_qkv))
    qkv_weights = gather_relative(qkv_mine, "seq")
    grad_b_q = mm_tn(low_q, grad_query)
    grad_b_kv = [mm_tn(low_k, grad_key), mm_tn(low_v, grad_value)]
    low_grads = [jnp.zeros((row_count, SPAN), F32)] * 3
    for k in range(seqs):
        piece = grad_pieces[k]
        low_grads = [
            low_grads[0] + mm_nt(piece[:, :width], second_q[k]),
            low_grads[1] + mm_nt(piece[:, width : width + kv_width], second_k[k]),
            low_grads[2] + mm_nt(piece[:, width + kv_width :], second_v[k]),
        ]
    grad_low_qkv = jnp.concatenate(low_grads, axis=1).astype(BF16) * mask_own_three
    grad_low_all = jnp.concatenate(gather_relative(grad_low_qkv, "seq"), axis=0)
    grad_a_qkv = mm_tn(grad_low_all, columns_of(normed_one, me, width))
    grad_normed_one = mm_nt(grad_low_qkv, first_qkv)
    for k in range(seqs):
        grad_normed_one = grad_normed_one + mm_nt(grad_pieces[k], qkv_weights[k])
    _, norm_one_back = jax.vjp(lambda hidden: rms_norm(hidden, attention_norm_gain), hidden_in)
    grad_input = (grad_mid + norm_one_back(grad_normed_one)[0]).astype(BF16)

    factor = ADAPTER_TOTAL / math.sqrt(PACK * fsdps)

    def split_units(rows):
        return [rows[:, k * width : (k + 1) * width].astype(BF16) for k in range(parts)]

    def seq_share(rows):
        return reduce_relative(
            [columns_of(rows, peer, width) for peer in peers], "seq"
        ).astype(BF16)

    def rows_out(whole, first, count):
        return whole[:, first : first + count].transpose(1, 0, 2).reshape(count, MODEL_WIDTH)

    def units_out(whole, first):
        part = whole[:, first : first + parts * SPAN]
        part = part.reshape(seqs, parts, SPAN, fsdps // parts, unit_block)
        return part.transpose(2, 1, 3, 0, 4).reshape(SPAN, feed_units)

    early = share_out(
        jnp.concatenate(
            [seq_share(jnp.concatenate([grad_a_ffn, grad_b_down], axis=0))]
            + split_units(grad_a_down)
            + split_units(grad_b_gate)
            + split_units(grad_b_up),
            axis=0,
        )
    )
    blank = jnp.zeros((SPAN, width - 2 * kv_width), BF16)
    middle = share_out(
        jnp.concatenate(
            [
                seq_share(jnp.concatenate([grad_a_out, grad_b_out], axis=0)),
                grad_b_q.astype(BF16),
                jnp.concatenate([g.astype(BF16) for g in grad_b_kv] + [blank], axis=1),
            ],
            axis=0,
        )
    )
    late = share_out(grad_a_qkv)

    def scaled(array):
        return array.astype(F32) * factor

    a_rows = jnp.concatenate(
        [rows_out(late, 0, 3 * SPAN), rows_out(middle, 0, SPAN), rows_out(early, 0, 2 * SPAN)],
        axis=0,
    )
    base = 3 * SPAN
    b_kv = middle[:, 3 * SPAN :, : 2 * kv_width].reshape(seqs, SPAN, 2, kv_width)
    return (
        layer_out[None],
        grad_input[None],
        scaled(a_rows.reshape(6, SPAN, MODEL_WIDTH).transpose(0, 2, 1)),
        scaled(units_out(early, base).T),
        scaled(
            jnp.stack(
                [
                    rows_out(middle, 2 * SPAN, SPAN),
                    rows_out(middle, SPAN, SPAN),
                    rows_out(early, 2 * SPAN, SPAN),
                ]
            )
        ),
        scaled(b_kv.transpose(2, 1, 0, 3).reshape(2, SPAN, KV_HEADS * HEAD_DIM)),
        scaled(
            jnp.stack(
                [units_out(early, base + parts * SPAN), units_out(early, base + 2 * parts * SPAN)]
            )
        ),
    )


def solution(mesh):
    rows = P("fsdp", None)
    placed = (
        (P("fsdp", "seq", None),) * 2 + (rows,) * 2 + (P(),) * 2 + (rows,) * 7 + (P(),) * 5
    )
    return jax.shard_map(
        shards,
        mesh=mesh,
        in_specs=placed,
        out_specs=(P("fsdp", "seq", None), P("fsdp", "seq", None), P(), P(), P(), P(), P()),
        check_vma=False,
    )
```

time: 2950 us -> 949 us (0.32)
  waiting for transfers between devices: 2450 us -> 322 us
  matrix products: 309 us -> 193 us
  local copies, waits for them, and re-layouts: 69 us -> 181 us
  Pallas kernels: 0 us -> 89.7 us
  starting transfers between devices: 15.7 us -> 85.8 us
    all_gather x7 -> x0, waiting for transfers between devices: 2070 us -> none  [the longest x1 627 us: shards(): lax.all_gather(up_matrix, 'fsdp', axis=0, tiled=True)]
    psum x1 -> x0, waiting for transfers between devices: 330 us -> none  [shards(): lax.psum((grad_a_all, grad_a_down, grad_b_all, grad_kv_all, grad_ffn_all)...]
    ppermute x0 -> x101, waiting for transfers between devices: none -> 322 us  [the longest x66 162 us: swap(): return lax.ppermute(block, axis, [(i, i ^ offset) for i in range(count)])]
    dot_general x61, matrix products: 309 us -> 193 us  [the longest x31 89.3 us: mm_nt(): lax.dot_general(left, right, (((1,), (1,)), ((), ())), preferred_element_...]
    pallas_call x0 -> x10, Pallas kernels: none -> 89.7 us  [the longest x8 42.3 us: place_blocks(): pl.pallas_call(body, out_shape=jax.ShapeDtypeStruct((rows * total, column...]
    ppermute x0 -> x101, starting transfers between devices: none -> 85.8 us  [the longest x66 45.5 us: swap(): return lax.ppermute(block, axis, [(i, i ^ offset) for i in range(count)])]
    all_to_all x4 -> x0, waiting for transfers between devices: 44.5 us -> none  [the longest x1 20.1 us: shards(): lax.all_to_all(packed, 'seq', split_axis=1, concat_axis=0, tiled=True)]
  transfers between devices with their start and end apart: 12 -> 101, of which waited for: 12 -> 35; matrix products, arithmetic and copies ran while one was open for 7% -> 37% of each run, Pallas kernels for 0% -> 9%
where the time goes in v1:
time: 949 us; the launch traced here: 938 us
  waiting for transfers between devices  322 us (34%)
  matrix products  193 us (20%)
  local copies, waits for them, and re-layouts  181 us (19%)
  Pallas kernels  89.7 us (9%)
  starting transfers between devices  85.8 us (9%)
  other arithmetic  64 us (7%)
    ppermute x66, waiting for transfers between devices, swap(): return lax.ppermute(block, axis, [(i, i ^ offset) for i in range(count)])  162 us
    ppermute x35, waiting for transfers between devices, send(): got = lax.ppermute(block, 'fsdp', self.perms[way])  160 us
    dot_general x31, matrix products, mm_nt(): lax.dot_general(left, right, (((1,), (1,)), ((), ())), preferred_element_...  89.3 us
    dot_general x19, matrix products, mm(): return jnp.dot(left, right, preferred_element_type=F32)  86.1 us
    ppermute x66, starting transfers between devices, swap(): return lax.ppermute(block, axis, [(i, i ^ offset) for i in range(count)])  45.5 us
    pallas_call x8, Pallas kernels, place_blocks(): pl.pallas_call(body, out_shape=jax.ShapeDtypeStruct((rows * total, column...  42.3 us
    ppermute x35, starting transfers between devices, send(): got = lax.ppermute(block, 'fsdp', self.perms[way])  40.4 us
    unnamed x246, local copies, waits for them, and re-layouts  37.5 us
  transfers between devices with their start and end apart: 101, of which 35 were waited for; matrix products, arithmetic and copies ran while one was open for 37% of the time, Pallas kernels for 9%

profile of v1, /device:TPU:0, one launch (start us, length us, event | category | flops | bytes accessed | tf_op | source)
XLA Modules:
  0.0 938.3 jit_solution(7039759685223448001)
XLA Ops:
  11.6 7.8 reshape.286
  19.4 7.8 reshape.289
  30.5 15.2 %dynamic-slice_reduce_fusion = (bf16[256,8,256]{2,1,0:T(8,128)(2,1)}, bf16[256,8,256]{2,1,0:T(8,128)(2,1)}) fusion(bf16[256,8,4,256]{3,2,1,0:T(4,128)(2,1)} %reshape.289, s32[]{:T(128)S(6)} %select_n.493, bf16[256,8,4,256]{3,2,1,0:T(4,128)(2,1)} %reshape.286), kind=kLoop, calls=%fused_computation.83 | loop fusion | bytes 4194308 | tf_op jit(solution)/shard_map/jit(dynamic_index_in_dim)/dynamic_slice | solution.py:484
  50.1 7.8 collective-permute-done.8.refs_6_
  63.3 11.2 %collective-permute-done.16.refs_7_ = bf16[256,512]{1,0:T(8,128)(2,1)} collective-permute-done((bf16[256,512]{1,0:T(8,128)(2,1)S(1)}, bf16[256,512]{1,0:T(8,128)(2,1)}, u32[]{:S(2)}, u32[]{:S(2)}) %collective-permute-start.16) | collective-permute-done | bytes 262176 | tf_op jit(solution)/shard_map/ppermute | solution.py:134
  90.8 10.3 %collective-permute-done.14.refs_2_ = bf16[256,512]{1,0:T(8,128)(2,1)} collective-permute-done((bf16[256,512]{1,0:T(8,128)(2,1)}, bf16[256,512]{1,0:T(8,128)(2,1)}, u32[]{:S(2)}, u32[]{:S(2)}) %collective-permute-start.14) | collective-permute-done | bytes 262176 | tf_op jit(solution)/shard_map/ppermute | solution.py:134
  144.6 5.7 collective-permute-done.26.refs_1_
  158.8 14.8 %collective-permute-done.27.refs_2_ = bf16[256,2048]{1,0:T(8,128)(2,1)} collective-permute-done((bf16[256,2048]{1,0:T(8,128)(2,1)}, bf16[256,2048]{1,0:T(8,128)(2,1)}, u32[]{:S(2)}, u32[]{:S(2)}) %collective-permute-start.27) | collective-permute-done | bytes 1048608 | tf_op jit(solution)/shard_map/ppermute | solution.py:134
  175.2 23.1 %attend_forward.1 = (bf16[1024,512]{1,0:T(8,128)(2,1)}, bf16[1024,256]{1,0:T(8,128)(2,1)}, bf16[1024,256]{1,0:T(8,128)(2,1)}, bf16[1024,512]{1,0:T(8,128)(2,1)}, f32[4,2,1024]{2,1,0:T(2,128)}) custom-call(s32[4]{0:T(128)} %pad_add_fusion.refs_0_, f32[1024,512]{1,0:T(8,128)} %slice_add_fusion.4.refs_1_, f32[1024,256]{1,0:T(8,128)} %pad_maximum_fusion.4.refs_2_, ...), custom_call_target="tpu_custom_call" | custom-call | flops 2147483648 | bytes 16777216 | tf_op jit(solution)/shard_map/attend_forward/pallas_call | solution.py:334
  201.8 5.9 collective-permute-done.10
  222.7 12.3 %collective-permute-done.33.refs_1_ = bf16[256,2048]{1,0:T(8,128)(2,1)} collective-permute-done((bf16[256,2048]{1,0:T(8,128)(2,1)}, bf16[256,2048]{1,0:T(8,128)(2,1)}, u32[]{:S(2)}, u32[]{:S(2)}) %collective-permute-start.33) | collective-permute-done | bytes 1048608 | tf_op jit(solution)/shard_map/ppermute | solution.py:134
  236.5 5.5 collective-permute-done.32.refs_5_
  243.5 20.8 %collective-permute-done.36.refs_7_ = bf16[256,2048]{1,0:T(8,128)(2,1)} collective-permute-done((bf16[256,2048]{1,0:T(8,128)(2,1)}, bf16[256,2048]{1,0:T(8,128)(2,1)}, u32[]{:S(2)}, u32[]{:S(2)}) %collective-permute-start.36) | collective-permute-done | bytes 1048608 | tf_op jit(solution)/shard_map/ppermute | solution.py:134
  276.2 13.5 %collective-permute-done.34.refs_2_ = bf16[256,2048]{1,0:T(8,128)(2,1)S(1)} collective-permute-done((bf16[256,2048]{1,0:T(8,128)(2,1)}, bf16[256,2048]{1,0:T(8,128)(2,1)S(1)}, u32[]{:S(2)}, u32[]{:S(2)}) %collective-permute-start.34) | collective-permute-done | bytes 1048608 | tf_op jit(solution)/shard_map/ppermute | solution.py:134
  300.4 15.3 %collective-permute-done.35.refs_3_ = bf16[256,2048]{1,0:T(8,128)(2,1)S(1)} collective-permute-done((bf16[256,2048]{1,0:T(8,128)(2,1)S(1)}, bf16[256,2048]{1,0:T(8,128)(2,1)S(1)}, u32[]{:S(2)}, u32[]{:S(2)}) %collective-permute-start.35) | collective-permute-done | bytes 1048608 | tf_op jit(solution)/shard_map/ppermute | solution.py:134
  317.2 19.5 %collective-permute-done.40.refs_1_ = bf16[256,2048]{1,0:T(8,128)(2,1)} collective-permute-done((bf16[256,2048]{1,0:T(8,128)(2,1)}, bf16[256,2048]{1,0:T(8,128)(2,1)}, u32[]{:S(2)}, u32[]{:S(2)}) %collective-permute-start.40) | collective-permute-done | bytes 1048608 | tf_op jit(solution)/shard_map/ppermute | solution.py:134
  352.1 8.4 collective-permute-done.23
  366.0 4.7 fusion.222
  370.6 7.1 place_blocks.10
  380.0 19.2 %collective-permute-done.45.refs_6_ = bf16[256,2048]{1,0:T(8,128)(2,1)} collective-permute-done((bf16[256,2048]{1,0:T(8,128)(2,1)}, bf16[256,2048]{1,0:T(8,128)(2,1)}, u32[]{:S(2)}, u32[]{:S(2)}) %collective-permute-start.45) | collective-permute-done | bytes 1048608 | tf_op jit(solution)/shard_map/ppermute | solution.py:134
  399.6 7.1 place_blocks.11
  413.7 14.5 %convolution_add_fusion.2 = f32[1024,2048]{1,0:T(8,128)} fusion(f32[1024,2048]{1,0:T(8,128)S(1)} %fusion.104, bf16[2048,2048]{1,0:T(8,128)(2,1)} %place_blocks.11, bf16[256,2048]{1,0:T(8,128)(2,1)} %collective-permute-done.25, bf16[256,2048]{1,0:T(8,128)(2,1)} %collective-permute-done.24, bf16[256,2048]{1,0:T(8,128)(2,1)} %collective-permute-done.23, ...), kind=kOutput, calls=%fused_computation.30 | convolution fusion | flops 8608808960 | bytes 29360128 | tf_op jit(solution)/shard_map/dot_general | solution.py:32
  436.5 7.1 place_blocks.12
  443.6 15.8 %convolution_add_fusion = f32[1024,2048]{1,0:T(8,128)} fusion(f32[1024,2048]{1,0:T(8,128)} %fusion.222, bf16[1024,2048]{1,0:T(8,128)(2,1)} %copy-done.6, bf16[2048,2048]{1,0:T(8,128)(2,1)} %place_blocks.12), kind=kOutput, calls=%fused_computation.28 | convolution fusion | flops 8592031744 | bytes 29360128 | tf_op jit(solution)/shard_map/dot_general | solution.py:36
  459.4 22.6 %fusion.2 = (bf16[1024,2048]{1,0:T(8,128)(2,1)}, bf16[1024,2048]{1,0:T(8,128)(2,1)}, bf16[1024,2048]{1,0:T(8,128)(2,1)S(1)}) fusion(f32[1024,2048]{1,0:T(8,128)} %convolution_add_fusion, f32[1024,2048]{1,0:T(8,128)} %convolution_add_fusion.2, f32[1024,2048]{1,0:T(8,128)} %fusion.107, bf16[2048,2048]{1,0:T(8,128)(2,1)} %place_blocks.10, ...), kind=kOutput, calls=%fused_computation.3 | convolution fusion | flops 8642363392 | bytes 50331648 | tf_op jit(solution)/shard_map/dot_general | solution.py:32
  490.7 13.8 %fusion.223 = f32[1024,2048]{1,0:T(8,128)} fusion(bf16[1024,2048]{1,0:T(8,128)(2,1)S(1)} %copy-done.26, bf16[2048,2048]{1,0:T(8,128)(2,1)} %place_blocks.11), kind=kOutput, calls=%fused_computation.400 | convolution fusion | flops 8589934592 | bytes 20971520 | tf_op jit(solution)/shard_map/dot_general | solution.py:36
  505.8 4.7 fusion.57
  514.6 14.0 %fusion.220 = (bf16[1024,2048]{1,0:T(8,128)(2,1)}, f32[1024,2048]{1,0:T(8,128)}) fusion(f32[1024,2048]{1,0:T(8,128)S(1)} %fusion.71, bf16[1024,2048]{1,0:T(8,128)(2,1)S(1)} %copy-done.22, bf16[2048,2048]{1,0:T(8,128)(2,1)} %place_blocks.12), kind=kOutput, calls=%fused_computation.397 | convolution fusion | flops 8594128896 | bytes 33554432 | tf_op jit(solution)/shard_map/dot_general | solution.py:32
  531.7 19.1 %fusion.219 = (bf16[1024,2048]{1,0:T(8,128)(2,1)}, f32[1024,2048]{1,0:T(8,128)}) fusion(f32[1024,2048]{1,0:T(8,128)} %fusion.57, f32[1024,2048]{1,0:T(8,128)} %fusion.223, bf16[1024,2048]{1,0:T(8,128)(2,1)} %get-tuple-element.108, bf16[2048,2048]{1,0:T(8,128)(2,1)} %place_blocks.10), kind=kOutput, calls=%fused_computation.396 | convolution fusion | flops 8596226048 | bytes 41943040 | tf_op jit(solution)/shard_map/dot_general | solution.py:36
  561.6 6.4 collective-permute-done.91
  577.8 15.3 %collective-permute-done.92 = bf16[960,512]{1,0:T(8,128)(2,1)S(1)} collective-permute-done((bf16[960,512]{1,0:T(8,128)(2,1)S(1)}, bf16[960,512]{1,0:T(8,128)(2,1)S(1)}, u32[]{:S(2)}, u32[]{:S(2)}) %collective-permute-start.92) | collective-permute-done | bytes 983072 | tf_op jit(solution)/shard_map/ppermute | solution.py:90
  603.6 16.7 %collective-permute-done.49 = bf16[256,2048]{1,0:T(8,128)(2,1)} collective-permute-done((bf16[256,2048]{1,0:T(8,128)(2,1)}, bf16[256,2048]{1,0:T(8,128)(2,1)}, u32[]{:S(2)}, u32[]{:S(2)}) %collective-permute-start.49) | collective-permute-done | bytes 1048608 | tf_op jit(solution)/shard_map/ppermute | solution.py:90
  620.3 5.4 multiply_convert_fusion.3
  653.3 24.4 %attend_backward.1 = (bf16[1024,512]{1,0:T(8,128)(2,1)}, bf16[1024,256]{1,0:T(8,128)(2,1)}, bf16[1024,256]{1,0:T(8,128)(2,1)}) custom-call(s32[4]{0:T(128)} %pad_add_fusion.refs_0_, bf16[1024,512]{1,0:T(8,128)(2,1)} %get-tuple-element.78.refs_1_, bf16[1024,256]{1,0:T(8,128)(2,1)} %get-tuple-element.79.refs_2_, bf16[1024,256]{1,0:T(8,128)(2,1)} %get-tuple-element.80.refs_3_, ...), custom_call_target="tpu_custom_call" | custom-call | flops 5368709120 | bytes 16777216 | tf_op jit(solution)/shard_map/attend_backward/pallas_call | solution.py:364
  698.4 15.5 %collective-permute-done.61 = bf16[256,768]{1,0:T(8,128)(2,1)S(1)} collective-permute-done((bf16[256,768]{1,0:T(8,128)(2,1)S(1)}, bf16[256,768]{1,0:T(8,128)(2,1)S(1)}, u32[]{:S(2)}, u32[]{:S(2)}) %collective-permute-start.61) | collective-permute-done | bytes 393248 | tf_op jit(solution)/shard_map/ppermute | solution.py:90
  717.9 9.9 %collective-permute-done.95 = bf16[240,512]{1,0:T(8,128)(2,1)S(1)} collective-permute-done((bf16[240,512]{1,0:T(8,128)(2,1)S(1)}, bf16[240,512]{1,0:T(8,128)(2,1)S(1)}, u32[]{:S(2)}, u32[]{:S(2)}) %collective-permute-start.95) | collective-permute-done | bytes 245792 | tf_op jit(solution)/shard_map/ppermute | solution.py:90
  730.9 12.0 %collective-permute-done.81 = bf16[128,512]{1,0:T(8,128)(2,1)S(1)} collective-permute-done((bf16[128,512]{1,0:T(8,128)(2,1)S(1)}, bf16[128,512]{1,0:T(8,128)(2,1)S(1)}, u32[]{:S(2)}, u32[]{:S(2)}) %collective-permute-start.81) | collective-permute-done | bytes 131104 | tf_op jit(solution)/shard_map/ppermute | solution.py:90
  754.1 13.0 %collective-permute-done.97 = bf16[960,512]{1,0:T(8,128)(2,1)S(1)} collective-permute-done((bf16[960,512]{1,0:T(8,128)(2,1)S(1)}, bf16[960,512]{1,0:T(8,128)(2,1)S(1)}, u32[]{:S(2)}, u32[]{:S(2)}) %collective-permute-start.97) | collective-permute-done | bytes 983072 | tf_op jit(solution)/shard_map/ppermute | solution.py:90
  791.0 23.5 %collective-permute-done.98.refs_1_ = bf16[1920,512]{1,0:T(8,128)(2,1)} collective-permute-done((bf16[1920,512]{1,0:T(8,128)(2,1)}, bf16[1920,512]{1,0:T(8,128)(2,1)}, u32[]{:S(2)}, u32[]{:S(2)}) %collective-permute-start.98) | collective-permute-done | bytes 1966112 | tf_op jit(solution)/shard_map/ppermute | solution.py:90
  820.0 5.3 collective-permute-done.73
  829.3 6.9 collective-permute-done.74.refs_1_
  854.9 7.6 place_blocks.15
  862.5 4.5 fusion.206
  903.1 6.6 copy.149
  909.6 6.6 copy.157
  916.2 5.9 reshape.305
  922.0 7.2 copy.150
  929.3 6.8 convert_multiply_fusion
  (612 shorter events, 381.3 us)
Async XLA Ops:
  4.4 41.6 %collective-permute-start.7 = (bf16[256,768]{1,0:T(8,128)(2,1)S(1)}, bf16[256,768]{1,0:T(8,128)(2,1)}, u32[]{:S(2)}, u32[]{:S(2)}) collective-permute-start(bf16[256,768]{1,0:T(8,128)(2,1)S(1)} %pad_maximum_fusion.15.refs_0_), channel_id=1, source_target_pairs={{2,0},{4,2},{6,4},{7,6},{5,7},{3,5},{1,3},{0,1},{10,8},{12,10},{14... | collective-permute-start | bytes 1179656 | tf_op jit(solution)/shard_map/ppermute | solution.py:134
  7.4 40.8 %collective-permute-start.3 = (bf16[256,768]{1,0:T(8,128)(2,1)S(1)}, bf16[256,768]{1,0:T(8,128)(2,1)}, u32[]{:S(2)}, u32[]{:S(2)}) collective-permute-start(bf16[256,768]{1,0:T(8,128)(2,1)S(1)} %pad_maximum_fusion.15.refs_0_), channel_id=1, source_target_pairs={{0,2},{2,4},{4,6},{6,7},{7,5},{5,3},{3,1},{1,0},{8,10},{10,12},{12... | collective-permute-start | bytes 1179656 | tf_op jit(solution)/shard_map/ppermute | solution.py:134
  9.7 66.4 %collective-permute-start = (bf16[256,2048]{1,0:T(8,128)(2,1)}, bf16[256,2048]{1,0:T(8,128)(2,1)}, u32[]{:S(2)}, u32[]{:S(2)}) collective-permute-start(bf16[256,2048]{1,0:T(8,128)(2,1)} %fusion.14), channel_id=1, source_target_pairs={{0,16},{8,24},{16,0},{24,8},{1,17},{9,25},{17,1},{25,9},{2,18},{10... | collective-permute-start | bytes 3145736 | tf_op jit(solution)/shard_map/ppermute | solution.py:90
  11.6 124.0 %collective-permute-start.1 = (bf16[256,2048]{1,0:T(8,128)(2,1)}, bf16[256,2048]{1,0:T(8,128)(2,1)}, u32[]{:S(2)}, u32[]{:S(2)}) collective-permute-start(bf16[256,2048]{1,0:T(8,128)(2,1)} %fusion.14), channel_id=1, source_target_pairs={{0,8},{8,0},{16,24},{24,16},{1,9},{9,1},{17,25},{25,17},{2,10},{10... | collective-permute-start | bytes 3145736 | tf_op jit(solution)/shard_map/ppermute | solution.py:90
  76.1 59.5 %collective-permute-start.2 = (bf16[256,2048]{1,0:T(8,128)(2,1)}, bf16[256,2048]{1,0:T(8,128)(2,1)}, u32[]{:S(2)}, u32[]{:S(2)}) collective-permute-start(bf16[256,2048]{1,0:T(8,128)(2,1)} %collective-permute-done), channel_id=1, source_target_pairs={{0,8},{8,0},{16,24},{24,16},{1,9},{9,1},{17,25},{25,17},{2,10},{10... | collective-permute-start | bytes 3145736 | tf_op jit(solution)/shard_map/ppermute | solution.py:90
  101.1 30.0 %collective-permute-start.15 = (bf16[256,512]{1,0:T(8,128)(2,1)}, bf16[256,512]{1,0:T(8,128)(2,1)}, u32[]{:S(2)}, u32[]{:S(2)}) collective-permute-start(bf16[256,512]{1,0:T(8,128)(2,1)} %collective-permute-done.14.refs_2_), channel_id=1, source_target_pairs={{0,2},{2,4},{4,6},{6,7},{7,5},{5,3},{3,1},{1,0},{8,10},{10,12},{12... | collective-permute-start | bytes 786440 | tf_op jit(solution)/shard_map/ppermute | solution.py:134
  102.7 29.1 %collective-permute-start.19 = (bf16[256,512]{1,0:T(8,128)(2,1)}, bf16[256,512]{1,0:T(8,128)(2,1)}, u32[]{:S(2)}, u32[]{:S(2)}) collective-permute-start(bf16[256,512]{1,0:T(8,128)(2,1)} %collective-permute-done.18.refs_5_), channel_id=1, source_target_pairs={{2,0},{4,2},{6,4},{7,6},{5,7},{3,5},{1,3},{0,1},{10,8},{12,10},{14... | collective-permute-start | bytes 786440 | tf_op jit(solution)/shard_map/ppermute | solution.py:134
  135.0 81.3 %collective-permute-start.20 = (bf16[2048,512]{1,0:T(8,128)(2,1)}, bf16[2048,512]{1,0:T(8,128)(2,1)}, u32[]{:S(2)}, u32[]{:S(2)}) collective-permute-start(bf16[2048,512]{1,0:T(8,128)(2,1)} %place_blocks.9), channel_id=1, source_target_pairs={{0,16},{8,24},{16,0},{24,8},{1,17},{9,25},{17,1},{25,9},{2,18},{10... | collective-permute-start | bytes 6291464 | tf_op jit(solution)/shard_map/ppermute | solution.py:90
  135.6 130.3 %collective-permute-start.21 = (bf16[2048,512]{1,0:T(8,128)(2,1)}, bf16[2048,512]{1,0:T(8,128)(2,1)}, u32[]{:S(2)}, u32[]{:S(2)}) collective-permute-start(bf16[2048,512]{1,0:T(8,128)(2,1)} %place_blocks.9), channel_id=1, source_target_pairs={{0,8},{8,0},{16,24},{24,16},{1,9},{9,1},{17,25},{25,17},{2,10},{10... | collective-permute-start | bytes 6291464 | tf_op jit(solution)/shard_map/ppermute | solution.py:90
  155.3 52.4 %collective-permute-start.31 = (bf16[256,2048]{1,0:T(8,128)(2,1)}, bf16[256,2048]{1,0:T(8,128)(2,1)}, u32[]{:S(2)}, u32[]{:S(2)}) collective-permute-start(bf16[256,2048]{1,0:T(8,128)(2,1)} %collective-permute-done.30.refs_7_), channel_id=1, source_target_pairs={{2,0},{4,2},{6,4},{7,6},{5,7},{3,5},{1,3},{0,1},{10,8},{12,10},{14... | collective-permute-start | bytes 3145736 | tf_op jit(solution)/shard_map/ppermute | solution.py:134
  173.6 44.2 %collective-permute-start.28 = (bf16[256,2048]{1,0:T(8,128)(2,1)}, bf16[256,2048]{1,0:T(8,128)(2,1)}, u32[]{:S(2)}, u32[]{:S(2)}) collective-permute-start(bf16[256,2048]{1,0:T(8,128)(2,1)} %collective-permute-done.27.refs_2_), channel_id=1, source_target_pairs={{0,2},{2,4},{4,6},{6,7},{7,5},{5,3},{3,1},{1,0},{8,10},{10,12},{12... | collective-permute-start | bytes 3145736 | tf_op jit(solution)/shard_map/ppermute | solution.py:134
  215.6 26.3 %collective-permute-start.32 = (bf16[256,2048]{1,0:T(8,128)(2,1)}, bf16[256,2048]{1,0:T(8,128)(2,1)}, u32[]{:S(2)}, u32[]{:S(2)}) collective-permute-start(bf16[256,2048]{1,0:T(8,128)(2,1)} %collective-permute-done.31.refs_6_), channel_id=1, source_target_pairs={{2,0},{4,2},{6,4},{7,6},{5,7},{3,5},{1,3},{0,1},{10,8},{12,10},{14... | collective-permute-start | bytes 3145736 | tf_op jit(solution)/shard_map/ppermute | solution.py:134
  216.3 48.1 %collective-permute-start.36 = (bf16[256,2048]{1,0:T(8,128)(2,1)}, bf16[256,2048]{1,0:T(8,128)(2,1)}, u32[]{:S(2)}, u32[]{:S(2)}) collective-permute-start(bf16[256,2048]{1,0:T(8,128)(2,1)} %bitcast.113.refs_0_), channel_id=1, source_target_pairs={{2,0},{4,2},{6,4},{7,6},{5,7},{3,5},{1,3},{0,1},{10,8},{12,10},{14... | collective-permute-start | bytes 3145736 | tf_op jit(solution)/shard_map/ppermute | solution.py:134
  217.8 75.1 %collective-permute-start.22 = (bf16[2048,512]{1,0:T(8,128)(2,1)}, bf16[2048,512]{1,0:T(8,128)(2,1)}, u32[]{:S(2)}, u32[]{:S(2)}) collective-permute-start(bf16[2048,512]{1,0:T(8,128)(2,1)} %collective-permute-done.20), channel_id=1, source_target_pairs={{0,8},{8,0},{16,24},{24,16},{1,9},{9,1},{17,25},{25,17},{2,10},{10... | collective-permute-start | bytes 6291464 | tf_op jit(solution)/shard_map/ppermute | solution.py:90
  234.9 40.7 %collective-permute-start.50 = (bf16[256,2048]{1,0:T(8,128)(2,1)}, bf16[256,2048]{1,0:T(8,128)(2,1)}, u32[]{:S(2)}, u32[]{:S(2)}) collective-permute-start(bf16[256,2048]{1,0:T(8,128)(2,1)} %bitcast.33), channel_id=1, source_target_pairs={{0,16},{8,24},{16,0},{24,8},{1,17},{9,25},{17,1},{25,9},{2,18},{10... | collective-permute-start | bytes 3145736 | tf_op jit(solution)/shard_map/ppermute | solution.py:90
  241.9 33.8 %collective-permute-start.29 = (bf16[256,2048]{1,0:T(8,128)(2,1)}, bf16[256,2048]{1,0:T(8,128)(2,1)S(1)}, u32[]{:S(2)}, u32[]{:S(2)}) collective-permute-start(bf16[256,2048]{1,0:T(8,128)(2,1)} %collective-permute-done.28.refs_3_), channel_id=1, source_target_pairs={{0,2},{2,4},{4,6},{6,7},{7,5},{5,3},{3,1},{1,0},{8,10},{10,12},{12... | collective-permute-start | bytes 3145736 | tf_op jit(solution)/shard_map/ppermute | solution.py:134
  275.6 75.5 %collective-permute-start.51 = (bf16[256,2048]{1,0:T(8,128)(2,1)}, bf16[256,2048]{1,0:T(8,128)(2,1)}, u32[]{:S(2)}, u32[]{:S(2)}) collective-permute-start(bf16[256,2048]{1,0:T(8,128)(2,1)} %bitcast.33), channel_id=1, source_target_pairs={{0,8},{8,0},{16,24},{24,16},{1,9},{9,1},{17,25},{25,17},{2,10},{10... | collective-permute-start | bytes 3145736 | tf_op jit(solution)/shard_map/ppermute | solution.py:90
  275.7 75.8 %collective-permute-start.52 = (bf16[256,2048]{1,0:T(8,128)(2,1)}, bf16[256,2048]{1,0:T(8,128)(2,1)}, u32[]{:S(2)}, u32[]{:S(2)}) collective-permute-start(bf16[256,2048]{1,0:T(8,128)(2,1)} %collective-permute-done.50), channel_id=1, source_target_pairs={{0,8},{8,0},{16,24},{24,16},{1,9},{9,1},{17,25},{25,17},{2,10},{10... | collective-permute-start | bytes 3145736 | tf_op jit(solution)/shard_map/ppermute | solution.py:90
  291.3 45.4 %collective-permute-start.40 = (bf16[256,2048]{1,0:T(8,128)(2,1)}, bf16[256,2048]{1,0:T(8,128)(2,1)}, u32[]{:S(2)}, u32[]{:S(2)}) collective-permute-start(bf16[256,2048]{1,0:T(8,128)(2,1)} %constant_dynamic-slice_fusion.14.refs_0_), channel_id=1, source_target_pairs={{0,2},{2,4},{4,6},{6,7},{7,5},{5,3},{3,1},{1,0},{8,10},{10,12},{12... | collective-permute-start | bytes 3145736 | tf_op jit(solution)/shard_map/ppermute | solution.py:134
  292.8 56.6 %collective-permute-start.38 = (bf16[256,2048]{1,0:T(8,128)(2,1)}, bf16[256,2048]{1,0:T(8,128)(2,1)}, u32[]{:S(2)}, u32[]{:S(2)}) collective-permute-start(bf16[256,2048]{1,0:T(8,128)(2,1)} %collective-permute-done.37.refs_6_), channel_id=1, source_target_pairs={{2,0},{4,2},{6,4},{7,6},{5,7},{3,5},{1,3},{0,1},{10,8},{12,10},{14... | collective-permute-start | bytes 3145736 | tf_op jit(solution)/shard_map/ppermute | solution.py:134
  316.7 32.8 %collective-permute-start.44 = (bf16[256,2048]{1,0:T(8,128)(2,1)}, bf16[256,2048]{1,0:T(8,128)(2,1)}, u32[]{:S(2)}, u32[]{:S(2)}) collective-permute-start(bf16[256,2048]{1,0:T(8,128)(2,1)} %constant_dynamic-slice_fusion.14.refs_0_), channel_id=1, source_target_pairs={{2,0},{4,2},{6,4},{7,6},{5,7},{3,5},{1,3},{0,1},{10,8},{12,10},{14... | collective-permute-start | bytes 3145736 | tf_op jit(solution)/shard_map/ppermute | solution.py:134
  349.4 57.3 %collective-permute-start.24 = (bf16[256,2048]{1,0:T(8,128)(2,1)}, bf16[256,2048]{1,0:T(8,128)(2,1)}, u32[]{:S(2)}, u32[]{:S(2)}) collective-permute-start(bf16[256,2048]{1,0:T(8,128)(2,1)} %multiply_convert_fusion.4), channel_id=1, source_target_pairs={{0,8},{8,0},{16,24},{24,16},{1,9},{9,1},{17,25},{25,17},{2,10},{10... | collective-permute-start | bytes 3145736 | tf_op jit(solution)/shard_map/ppermute | solution.py:90
  349.5 28.3 %collective-permute-start.41 = (bf16[256,2048]{1,0:T(8,128)(2,1)}, bf16[256,2048]{1,0:T(8,128)(2,1)}, u32[]{:S(2)}, u32[]{:S(2)}) collective-permute-start(bf16[256,2048]{1,0:T(8,128)(2,1)} %collective-permute-done.40.refs_1_), channel_id=1, source_target_pairs={{0,2},{2,4},{4,6},{6,7},{7,5},{5,3},{3,1},{1,0},{8,10},{10,12},{12... | collective-permute-start | bytes 3145736 | tf_op jit(solution)/shard_map/ppermute | solution.py:134
  351.1 27.2 %collective-permute-start.39 = (bf16[256,2048]{1,0:T(8,128)(2,1)}, bf16[256,2048]{1,0:T(8,128)(2,1)}, u32[]{:S(2)}, u32[]{:S(2)}) collective-permute-start(bf16[256,2048]{1,0:T(8,128)(2,1)} %collective-permute-done.38.refs_5_), channel_id=1, source_target_pairs={{2,0},{4,2},{6,4},{7,6},{5,7},{3,5},{1,3},{0,1},{10,8},{12,10},{14... | collective-permute-start | bytes 3145736 | tf_op jit(solution)/shard_map/ppermute | solution.py:134
  351.6 47.6 %collective-permute-start.45 = (bf16[256,2048]{1,0:T(8,128)(2,1)}, bf16[256,2048]{1,0:T(8,128)(2,1)}, u32[]{:S(2)}, u32[]{:S(2)}) collective-permute-start(bf16[256,2048]{1,0:T(8,128)(2,1)} %collective-permute-done.44.refs_7_), channel_id=1, source_target_pairs={{2,0},{4,2},{6,4},{7,6},{5,7},{3,5},{1,3},{0,1},{10,8},{12,10},{14... | collective-permute-start | bytes 3145736 | tf_op jit(solution)/shard_map/ppermute | solution.py:134
  360.4 46.3 %collective-permute-start.25 = (bf16[256,2048]{1,0:T(8,128)(2,1)}, bf16[256,2048]{1,0:T(8,128)(2,1)}, u32[]{:S(2)}, u32[]{:S(2)}) collective-permute-start(bf16[256,2048]{1,0:T(8,128)(2,1)} %collective-permute-done.23), channel_id=1, source_target_pairs={{0,8},{8,0},{16,24},{24,16},{1,9},{9,1},{17,25},{25,17},{2,10},{10... | collective-permute-start | bytes 3145736 | tf_op jit(solution)/shard_map/ppermute | solution.py:90
  377.8 219.3 %collective-permute-start.62 = (bf16[2048,768]{1,0:T(8,128)(2,1)}, bf16[2048,768]{1,0:T(8,128)(2,1)}, u32[]{:S(2)}, u32[]{:S(2)}) collective-permute-start(bf16[2048,768]{1,0:T(8,128)(2,1)} %place_blocks.8), channel_id=1, source_target_pairs={{0,16},{8,24},{16,0},{24,8},{1,17},{9,25},{17,1},{25,9},{2,18},{10... | collective-permute-start | bytes 9437192 | tf_op jit(solution)/shard_map/ppermute | solution.py:90
  378.4 33.2 %collective-permute-start.42 = (bf16[256,2048]{1,0:T(8,128)(2,1)}, bf16[256,2048]{1,0:T(8,128)(2,1)}, u32[]{:S(2)}, u32[]{:S(2)}) collective-permute-start(bf16[256,2048]{1,0:T(8,128)(2,1)} %collective-permute-done.41.refs_2_), channel_id=1, source_target_pairs={{0,2},{2,4},{4,6},{6,7},{7,5},{5,3},{3,1},{1,0},{8,10},{10,12},{12... | collective-permute-start | bytes 3145736 | tf_op jit(solution)/shard_map/ppermute | solution.py:134
  399.1 33.6 %collective-permute-start.46 = (bf16[256,2048]{1,0:T(8,128)(2,1)}, bf16[256,2048]{1,0:T(8,128)(2,1)}, u32[]{:S(2)}, u32[]{:S(2)}) collective-permute-start(bf16[256,2048]{1,0:T(8,128)(2,1)} %collective-permute-done.45.refs_6_), channel_id=1, source_target_pairs={{2,0},{4,2},{6,4},{7,6},{5,7},{3,5},{1,3},{0,1},{10,8},{12,10},{14... | collective-permute-start | bytes 3145736 | tf_op jit(solution)/shard_map/ppermute | solution.py:134
  514.0 41.0 %collective-permute-start.90 = (bf16[384,512]{1,0:T(8,128)(2,1)S(1)}, bf16[384,512]{1,0:T(8,128)(2,1)}, u32[]{:S(2)}, u32[]{:S(2)}) collective-permute-start(bf16[384,512]{1,0:T(8,128)(2,1)S(1)} %get-tuple-element.120), channel_id=1, source_target_pairs={{0,8},{8,0},{16,24},{24,16},{1,9},{9,1},{17,25},{25,17},{2,10},{10... | collective-permute-start | bytes 1179656 | tf_op jit(solution)/shard_map/ppermute | solution.py:90
  514.1 47.4 %collective-permute-start.89 = (bf16[384,512]{1,0:T(8,128)(2,1)S(1)}, bf16[384,512]{1,0:T(8,128)(2,1)S(1)}, u32[]{:S(2)}, u32[]{:S(2)}) collective-permute-start(bf16[384,512]{1,0:T(8,128)(2,1)S(1)} %get-tuple-element.119), channel_id=1, source_target_pairs={{0,8},{8,0},{16,24},{24,16},{1,9},{9,1},{17,25},{25,17},{2,10},{10... | collective-permute-start | bytes 1179656 | tf_op jit(solution)/shard_map/ppermute | solution.py:90
  531.7 43.0 %collective-permute-start.48 = (bf16[256,2048]{1,0:T(8,128)(2,1)}, bf16[256,2048]{1,0:T(8,128)(2,1)}, u32[]{:S(2)}, u32[]{:S(2)}) collective-permute-start(bf16[256,2048]{1,0:T(8,128)(2,1)} %get-tuple-element.116), channel_id=1, source_target_pairs={{0,8},{8,0},{16,24},{24,16},{1,9},{9,1},{17,25},{25,17},{2,10},{10... | collective-permute-start | bytes 3145736 | tf_op jit(solution)/shard_map/ppermute | solution.py:90
  561.5 35.7 %collective-permute-start.53 = (bf16[256,2048]{1,0:T(8,128)(2,1)}, bf16[256,2048]{1,0:T(8,128)(2,1)S(1)}, u32[]{:S(2)}, u32[]{:S(2)}) collective-permute-start(bf16[256,2048]{1,0:T(8,128)(2,1)} %get-tuple-element.113), channel_id=1, source_target_pairs={{0,8},{8,0},{16,24},{24,16},{1,9},{9,1},{17,25},{25,17},{2,10},{10... | collective-permute-start | bytes 3145736 | tf_op jit(solution)/shard_map/ppermute | solution.py:90
  573.2 26.3 %collective-permute-start.55 = (bf16[256,2048]{1,0:T(8,128)(2,1)}, bf16[256,2048]{1,0:T(8,128)(2,1)}, u32[]{:S(2)}, u32[]{:S(2)}) collective-permute-start(bf16[256,2048]{1,0:T(8,128)(2,1)} %fusion.16), channel_id=1, source_target_pairs={{0,16},{8,24},{16,0},{24,8},{1,17},{9,25},{17,1},{25,9},{2,18},{10... | collective-permute-start | bytes 3145736 | tf_op jit(solution)/shard_map/ppermute | solution.py:90
  574.7 28.9 %collective-permute-start.47 = (bf16[256,2048]{1,0:T(8,128)(2,1)}, bf16[256,2048]{1,0:T(8,128)(2,1)}, u32[]{:S(2)}, u32[]{:S(2)}) collective-permute-start(bf16[256,2048]{1,0:T(8,128)(2,1)} %get-tuple-element.115), channel_id=1, source_target_pairs={{0,8},{8,0},{16,24},{24,16},{1,9},{9,1},{17,25},{25,17},{2,10},{10... | collective-permute-start | bytes 3145736 | tf_op jit(solution)/shard_map/ppermute | solution.py:90
  593.1 27.2 %collective-permute-start.49 = (bf16[256,2048]{1,0:T(8,128)(2,1)}, bf16[256,2048]{1,0:T(8,128)(2,1)}, u32[]{:S(2)}, u32[]{:S(2)}) collective-permute-start(bf16[256,2048]{1,0:T(8,128)(2,1)} %fusion.19), channel_id=1, source_target_pairs={{0,16},{8,24},{16,0},{24,8},{1,17},{9,25},{17,1},{25,9},{2,18},{10... | collective-permute-start | bytes 3145736 | tf_op jit(solution)/shard_map/ppermute | solution.py:90
  597.1 173.3 %collective-permute-start.63 = (bf16[2048,768]{1,0:T(8,128)(2,1)}, bf16[2048,768]{1,0:T(8,128)(2,1)}, u32[]{:S(2)}, u32[]{:S(2)}) collective-permute-start(bf16[2048,768]{1,0:T(8,128)(2,1)} %place_blocks.8), channel_id=1, source_target_pairs={{0,8},{8,0},{16,24},{24,16},{1,9},{9,1},{17,25},{25,17},{2,10},{10... | collective-permute-start | bytes 9437192 | tf_op jit(solution)/shard_map/ppermute | solution.py:90
  597.2 217.4 %collective-permute-start.64 = (bf16[2048,768]{1,0:T(8,128)(2,1)}, bf16[2048,768]{1,0:T(8,128)(2,1)}, u32[]{:S(2)}, u32[]{:S(2)}) collective-permute-start(bf16[2048,768]{1,0:T(8,128)(2,1)} %collective-permute-done.62), channel_id=1, source_target_pairs={{0,8},{8,0},{16,24},{24,16},{1,9},{9,1},{17,25},{25,17},{2,10},{10... | collective-permute-start | bytes 9437192 | tf_op jit(solution)/shard_map/ppermute | solution.py:90
  599.5 41.6 %collective-permute-start.93 = (bf16[480,512]{1,0:T(8,128)(2,1)S(1)}, bf16[480,512]{1,0:T(8,128)(2,1)S(1)}, u32[]{:S(2)}, u32[]{:S(2)}) collective-permute-start(bf16[480,512]{1,0:T(8,128)(2,1)S(1)} %constant_dynamic-slice_fusion.1), channel_id=1, source_target_pairs={{0,2},{1,3},{2,0},{3,1},{4,6},{5,7},{6,4},{7,5},{8,10},{9,11},{10,... | collective-permute-start | bytes 1474568 | tf_op jit(solution)/shard_map/ppermute | solution.py:90
  646.2 35.1 %collective-permute-start.78 = (bf16[256,512]{1,0:T(8,128)(2,1)S(1)}, bf16[256,512]{1,0:T(8,128)(2,1)S(1)}, u32[]{:S(2)}, u32[]{:S(2)}) collective-permute-start(bf16[256,512]{1,0:T(8,128)(2,1)S(1)} %get-tuple-element.131), channel_id=1, source_target_pairs={{0,8},{8,0},{16,24},{24,16},{1,9},{9,1},{17,25},{25,17},{2,10},{10... | collective-permute-start | bytes 786440 | tf_op jit(solution)/shard_map/ppermute | solution.py:90
  646.2 49.7 %collective-permute-start.77 = (bf16[256,512]{1,0:T(8,128)(2,1)}, bf16[256,512]{1,0:T(8,128)(2,1)}, u32[]{:S(2)}, u32[]{:S(2)}) collective-permute-start(bf16[256,512]{1,0:T(8,128)(2,1)} %get-tuple-element.130), channel_id=1, source_target_pairs={{0,8},{8,0},{16,24},{24,16},{1,9},{9,1},{17,25},{25,17},{2,10},{10... | collective-permute-start | bytes 786440 | tf_op jit(solution)/shard_map/ppermute | solution.py:90
  649.7 43.6 %collective-permute-start.94 = (bf16[240,512]{1,0:T(8,128)(2,1)}, bf16[240,512]{1,0:T(8,128)(2,1)}, u32[]{:S(2)}, u32[]{:S(2)}) collective-permute-start(bf16[240,512]{1,0:T(8,128)(2,1)} %constant_dynamic-slice_fusion), channel_id=1, source_target_pairs={{0,4},{1,5},{2,6},{3,7},{4,0},{5,1},{6,2},{7,3},{8,12},{9,13},{10,... | collective-permute-start | bytes 737288 | tf_op jit(solution)/shard_map/ppermute | solution.py:90
  717.8 30.1 %collective-permute-start.65 = (bf16[256,384]{0,1:T(8,128)(2,1)S(1)}, bf16[256,384]{0,1:T(8,128)(2,1)S(1)}, u32[]{:S(2)}, u32[]{:S(2)}) collective-permute-start(bf16[256,384]{0,1:T(8,128)(2,1)S(1)} %maximum_multiply_fusion), channel_id=1, source_target_pairs={{0,16},{8,24},{16,0},{24,8},{1,17},{9,25},{17,1},{25,9},{2,18},{10... | collective-permute-start | bytes 589832 | tf_op jit(solution)/shard_map/ppermute | solution.py:90
  768.5 46.0 %collective-permute-start.98 = (bf16[1920,512]{1,0:T(8,128)(2,1)}, bf16[1920,512]{1,0:T(8,128)(2,1)}, u32[]{:S(2)}, u32[]{:S(2)}) collective-permute-start(bf16[1920,512]{1,0:T(8,128)(2,1)} %pad_maximum_fusion.2.refs_0_), channel_id=1, source_target_pairs={{0,16},{8,24},{16,0},{24,8},{1,17},{9,25},{17,1},{25,9},{2,18},{10... | collective-permute-start | bytes 5898248 | tf_op jit(solution)/shard_map/ppermute | solution.py:90
  786.8 40.4 %collective-permute-start.86 = (bf16[512,512]{1,0:T(8,128)(2,1)S(1)}, bf16[512,512]{1,0:T(8,128)(2,1)S(1)}, u32[]{:S(2)}, u32[]{:S(2)}) collective-permute-start(bf16[512,512]{1,0:T(8,128)(2,1)S(1)} %pad_maximum_fusion.13.refs_0_), channel_id=1, source_target_pairs={{0,16},{8,24},{16,0},{24,8},{1,17},{9,25},{17,1},{25,9},{2,18},{10... | collective-permute-start | bytes 1572872 | tf_op jit(solution)/shard_map/ppermute | solution.py:90
  790.9 27.0 %collective-permute-start.72 = (bf16[96,512]{1,0:T(8,128)(2,1)S(1)}, bf16[96,512]{1,0:T(8,128)(2,1)S(1)}, u32[]{:S(2)}, u32[]{:S(2)}) collective-permute-start(bf16[96,512]{1,0:T(8,128)(2,1)S(1)} %pad_maximum_fusion.21), channel_id=1, source_target_pairs={{0,2},{1,3},{2,0},{3,1},{4,6},{5,7},{6,4},{7,5},{8,10},{9,11},{10,... | collective-permute-start | bytes 294920 | tf_op jit(solution)/shard_map/ppermute | solution.py:90
  791.0 63.9 %collective-permute-start.99 = (bf16[1920,512]{1,0:T(8,128)(2,1)}, bf16[1920,512]{1,0:T(8,128)(2,1)}, u32[]{:S(2)}, u32[]{:S(2)}) collective-permute-start(bf16[1920,512]{1,0:T(8,128)(2,1)} %pad_maximum_fusion.2.refs_0_), channel_id=1, source_target_pairs={{0,8},{8,0},{16,24},{24,16},{1,9},{9,1},{17,25},{25,17},{2,10},{10... | collective-permute-start | bytes 5898248 | tf_op jit(solution)/shard_map/ppermute | solution.py:90
  814.6 40.3 %collective-permute-start.100 = (bf16[1920,512]{1,0:T(8,128)(2,1)}, bf16[1920,512]{1,0:T(8,128)(2,1)}, u32[]{:S(2)}, u32[]{:S(2)}) collective-permute-start(bf16[1920,512]{1,0:T(8,128)(2,1)} %collective-permute-done.98.refs_1_), channel_id=1, source_target_pairs={{0,8},{8,0},{16,24},{24,16},{1,9},{9,1},{17,25},{25,17},{2,10},{10... | collective-permute-start | bytes 5898248 | tf_op jit(solution)/shard_map/ppermute | solution.py:90
  (165 other events, 3053.7 us)

commit v2 on v1

--- a/solution.py
+++ b/solution.py
@@ -110,7 +110,7 @@
 
 
 class Rings:
-    WINDOW = 2
+    WINDOW = 3
 
     def __init__(self):
         self.count = lax.axis_size("fsdp")
@@ -135,14 +135,13 @@
         sent.append(got)
         return got
 
-    def gather(self, blocks):
+    def gather(self, blocks, starts):
         half = self.count // 2
-        lag = max(half // 2, 1)
         found = [{0: block} for block in blocks]
         latest = [[block, block] for block in blocks]
-        for time in range(half + lag * (len(blocks) - 1)):
+        for time in range(1, half + max(starts) + 1):
             for which in range(len(blocks)):
-                step = time - lag * which + 1
+                step = time - starts[which]
                 if not 1 <= step <= half:
                     continue
                 for way in (0, 1):
@@ -203,6 +202,124 @@
         ),
         name="place_blocks",
     )(targets.astype(jnp.int32), *pieces)
+
+
+def after(value, *others):
+    return lax.optimization_barrier((value, others))[0]
+
+
+def take_units(matrices, peer, seqs, runs, unit_block):
+    if unit_block % 128:
+        return [
+            lax.dynamic_index_in_dim(
+                m.reshape(m.shape[0], runs, seqs, unit_block), peer, 2, keepdims=False
+            ).reshape(m.shape[0], runs * unit_block)
+            for m in matrices
+        ]
+
+    def body(peer_ref, *refs):
+        for source, target in zip(refs[: len(matrices)], refs[len(matrices) :]):
+            target[...] = source[...]
+
+    return pl.pallas_call(
+        body,
+        grid_spec=pltpu.PrefetchScalarGridSpec(
+            num_scalar_prefetch=1,
+            grid=(runs,),
+            in_specs=[
+                pl.BlockSpec((m.shape[0], unit_block), lambda f, at: (0, f * seqs + at[0]))
+                for m in matrices
+            ],
+            out_specs=[
+                pl.BlockSpec((m.shape[0], unit_block), lambda f, at: (0, f)) for m in matrices
+            ],
+        ),
+        out_shape=[
+            jax.ShapeDtypeStruct((m.shape[0], runs * unit_block), m.dtype) for m in matrices
+        ],
+        name="take_units",
+    )(peer.astype(jnp.int32)[None], *matrices)
+
+
+def finish_units(whole, first, parts, runs, unit_block, factor):
+    seqs, _, columns = whole.shape
+    feed_units = seqs * runs * unit_block
+    per = runs // parts
+
+    def body(down_ref, gate_ref, up_ref, a_ref, b_ref):
+        for s in range(seqs):
+            here = slice(s * unit_block, (s + 1) * unit_block)
+            a_ref[here, :] = down_ref[s].astype(F32).T * factor
+            b_ref[0, :, here] = gate_ref[s].astype(F32) * factor
+            b_ref[1, :, here] = up_ref[s].astype(F32) * factor
+
+    def part(which):
+        base = first // SPAN + which * parts
+        return pl.BlockSpec((seqs, SPAN, unit_block), lambda k, g: (0, base + k, g))
+
+    return pl.pallas_call(
+        body,
+        grid=(parts, per),
+        in_specs=[part(0), part(1), part(2)],
+        out_specs=[
+            pl.BlockSpec((seqs * unit_block, SPAN), lambda k, g: (k * per + g, 0)),
+            pl.BlockSpec((2, SPAN, seqs * unit_block), lambda k, g: (0, 0, k * per + g)),
+        ],
+        out_shape=[
+            jax.ShapeDtypeStruct((feed_units, SPAN), F32),
+            jax.ShapeDtypeStruct((2, SPAN, feed_units), F32),
+        ],
+        name="finish_units",
+    )(whole, whole, whole)
+
+
+def finish_model(early, middle, factor):
+    seqs, _, columns = early.shape
+
+    def body(early_ref, middle_ref, a_ref, b_ref):
+        a_ref[0] = middle_ref[0, :SPAN].astype(F32).T * factor
+        a_ref[1] = early_ref[0, :SPAN].astype(F32).T * factor
+        a_ref[2] = early_ref[0, SPAN : 2 * SPAN].astype(F32).T * factor
+        b_ref[0] = middle_ref[0, 2 * SPAN :].astype(F32) * factor
+        b_ref[1] = middle_ref[0, SPAN : 2 * SPAN].astype(F32) * factor
+        b_ref[2] = early_ref[0, 2 * SPAN :].astype(F32) * factor
+
+    spec = pl.BlockSpec((1, 3 * SPAN, columns), lambda s: (s, 0, 0))
+    return pl.pallas_call(
+        body,
+        grid=(seqs,),
+        in_specs=[spec, spec],
+        out_specs=[
+            pl.BlockSpec((3, columns, SPAN), lambda s: (1, s, 0)),
+            pl.BlockSpec((3, SPAN, columns), lambda s: (0, 0, s)),
+        ],
+        out_shape=[
+            jax.ShapeDtypeStruct((6, MODEL_WIDTH, SPAN), F32),
+            jax.ShapeDtypeStruct((3, SPAN, MODEL_WIDTH), F32),
+        ],
+        name="finish_model",
+    )(early, middle)
+
+
+def finish_late(late, a_all, factor):
+    seqs, _, columns = late.shape
+
+    def body(late_ref, held_ref, a_ref):
+        for j in range(3):
+            a_ref[j] = late_ref[0, j * SPAN : (j + 1) * SPAN].astype(F32).T * factor
+
+    return pl.pallas_call(
+        body,
+        grid=(seqs,),
+        in_specs=[
+            pl.BlockSpec((1, 3 * SPAN, columns), lambda s: (s, 0, 0)),
+            pl.BlockSpec(memory_space=pl.ANY),
+        ],
+        out_specs=pl.BlockSpec((3, columns, SPAN), lambda s: (0, s, 0)),
+        out_shape=jax.ShapeDtypeStruct(a_all.shape, F32),
+        input_output_aliases={1: 0},
+        name="finish_late",
+    )(late, a_all)
 
 
 def half_lanes(shape):
@@ -479,12 +596,6 @@
             whole = lax.dynamic_update_slice(whole, piece, (0, peer * count))
         return whole
 
-    def my_units(matrix):
-        parted = matrix.reshape(matrix.shape[0], fsdps, seqs, unit_block)
-        return lax.dynamic_index_in_dim(parted, me, 2, keepdims=False).reshape(
-            matrix.shape[0], units
-        )
-
     rings = Rings()
     qkv_share = jnp.concatenate(
         [
@@ -495,11 +606,25 @@
         axis=1,
     )
     out_share = columns_of(output_matrix, me, width)
-    gate_share, up_share = my_units(gate_matrix), my_units(up_matrix)
+    gate_share, up_share = take_units([gate_matrix, up_matrix], me, seqs, fsdps, unit_block)
     down_share = lax.dynamic_slice_in_dim(down_matrix, me * unit_block, unit_block, 0)
-    lists = rings.gather([qkv_share, out_share, gate_share, up_share, down_share])
-    qkv_mine, out_mine, gate_full, up_full, down_full = (
-        place_blocks(blocks, 1, rings.owner) for blocks in lists
+    half_block = unit_block // 2
+    lists = rings.gather(
+        [
+            qkv_share,
+            out_share,
+            gate_share,
+            up_share,
+            down_share[:half_block],
+            down_share[half_block:],
+        ],
+        [0, 0, 3, 4, 7, 7],
+    )
+    qkv_mine, out_mine, gate_full, up_full = (
+        place_blocks(blocks, 1, rings.owner) for blocks in lists[:4]
+    )
+    down_full = place_blocks(
+        lists[4] + lists[5], 1, jnp.concatenate([rings.owner * 2, rings.owner * 2 + 1])
     )
 
     segment, position, valid_row, onehot = pack_tables(
@@ -577,8 +702,10 @@
     first_ffn = jnp.concatenate([adapter_first_factors[4], adapter_first_factors[5]], axis=1)
     low_ffn = (mm(normed_two, first_ffn) * mask_rel_two).astype(BF16)
     low_g, low_u = low_ffn[:, :SPAN], low_ffn[:, SPAN:]
-    second_gate = my_units(adapter_second_feedfwd[0])
-    second_up = my_units(adapter_second_feedfwd[1])
+    (second_ffn,) = take_units(
+        [adapter_second_feedfwd.reshape(2 * SPAN, feed_units)], me, seqs, fsdps, unit_block
+    )
+    second_gate, second_up = second_ffn[:SPAN], second_ffn[SPAN:]
     gate = mm(normed_two, gate_full) + mm(low_g, second_gate)
     up = mm(normed_two, up_full) + mm(low_u, second_up)
 
@@ -589,16 +716,9 @@
     first_down = lax.dynamic_index_in_dim(
         adapter_first_down.reshape(fsdps, seqs, unit_block, SPAN), me, 1, keepdims=False
     ).reshape(units, SPAN)
-    low_d = (mm(act, first_down) * mask_rel).astype(BF16)
-    down_part = mm(act, down_full) + mm(low_d, adapter_second_model[2])
-    down_sum = reduce_relative(blocks_of(down_part), "seq")
-    layer_out = (valid_col * (hidden_mid + RESIDUAL_FACTOR * down_sum)).astype(BF16)
-
     grad_out = cotangent[0].astype(F32) * valid_col
     grad_down = (RESIDUAL_FACTOR * (cot_all.astype(F32) * valid_rel)).astype(BF16)
     grad_low_d = mm_nt(grad_down, adapter_second_model[2]).astype(BF16) * mask_rel
-    grad_b_down = mm_tn(low_d, grad_down)
-    grad_a_down = mm_tn(grad_low_d, act)
     grad_act = mm_nt(grad_down, down_full) + mm_nt(grad_low_d, first_down)
     _, swiglu_back = jax.vjp(swiglu, gate, up)
     grad_gate, grad_up = swiglu_back(grad_act)
@@ -609,13 +729,21 @@
         )
         * mask_rel_two
     )
+    grad_normed_two = (
+        mm_nt(grad_gate, gate_full) + mm_nt(grad_up, up_full) + mm_nt(grad_low_ffn, first_ffn)
+    )
+    act, grad_gate, grad_up = after((act, grad_gate, grad_up), grad_normed_two)
+    grad_normed_two = reduce_relative(blocks_of(grad_normed_two), "seq")
+    low_d = (mm(act, first_down) * mask_rel).astype(BF16)
+    down_part = mm(act, down_full) + mm(low_d, adapter_second_model[2])
+    down_sum = reduce_relative(blocks_of(down_part), "seq")
+    layer_out = (valid_col * (hidden_mid + RESIDUAL_FACTOR * down_sum)).astype(BF16)
+
+    grad_b_down = mm_tn(low_d, grad_down)
+    grad_a_down = mm_tn(grad_low_d, act)
     grad_b_gate = mm_tn(low_g, grad_gate)
     grad_b_up = mm_tn(low_u, grad_up)
     grad_a_ffn = mm_tn(grad_low_ffn, normed_two)
-    grad_normed_two = (
-        mm_nt(grad_gate, gate_full) + mm_nt(grad_up, up_full) + mm_nt(grad_low_ffn, first_ffn)
-    )
-    grad_normed_two = reduce_relative(blocks_of(grad_normed_two), "seq")
     _, norm_two_back = jax.vjp(lambda hidden: rms_norm(hidden, feedfwd_norm_gain), hidden_mid)
     grad_mid = grad_out + norm_two_back(grad_normed_two)[0]
 
@@ -673,9 +801,6 @@
             [columns_of(rows, peer, width) for peer in peers], "seq"
         ).astype(BF16)
 
-    def rows_out(whole, first, count):
-        return whole[:, first : first + count].transpose(1, 0, 2).reshape(count, MODEL_WIDTH)
-
     def units_out(whole, first):
         part = whole[:, first : first + parts * SPAN]
         part = part.reshape(seqs, parts, SPAN, fsdps // parts, unit_block)
@@ -706,32 +831,26 @@
     def scaled(array):
         return array.astype(F32) * factor
 
-    a_rows = jnp.concatenate(
-        [rows_out(late, 0, 3 * SPAN), rows_out(middle, 0, SPAN), rows_out(early, 0, 2 * SPAN)],
-        axis=0,
-    )
     base = 3 * SPAN
     b_kv = middle[:, 3 * SPAN :, : 2 * kv_width].reshape(seqs, SPAN, 2, kv_width)
+    if unit_block % 128 == 0:
+        a_down, b_ffn = finish_units(early, base, parts, fsdps, unit_block, factor)
+    else:
+        a_down = scaled(units_out(early, base).T)
+        b_ffn = scaled(
+            jnp.stack(
+                [units_out(early, base + parts * SPAN), units_out(early, base + 2 * parts * SPAN)]
+            )
+        )
+    a_all, b_model = finish_model(early, middle, factor)
     return (
         layer_out[None],
         grad_input[None],
-        scaled(a_rows.reshape(6, SPAN, MODEL_WIDTH).transpose(0, 2, 1)),
-        scaled(units_out(early, base).T),
-        scaled(
-            jnp.stack(
-                [
-                    rows_out(middle, 2 * SPAN, SPAN),
-                    rows_out(middle, SPAN, SPAN),
-                    rows_out(early, 2 * SPAN, SPAN),
-                ]
-            )
-        ),
+        finish_late(late, a_all, factor),
+        a_down,
+        b_model,
         scaled(b_kv.transpose(2, 1, 0, 3).reshape(2, SPAN, KV_HEADS * HEAD_DIM)),
-        scaled(
-            jnp.stack(
-                [units_out(early, base + parts * SPAN), units_out(early, base + 2 * parts * SPAN)]
-            )
-        ),
+        b_ffn,
     )
 
 

time: 949 us -> 805 us (0.85)
  local copies, waits for them, and re-layouts: 181 us -> 68.8 us
  waiting for transfers between devices: 322 us -> 262 us
  Pallas kernels: 89.7 us -> 119 us
  starting transfers between devices: 85.8 us -> 105 us
  other arithmetic: 64 us -> 46.7 us
    ppermute x35 -> x42, waiting for transfers between devices: 160 us -> 104 us  [send(): got = lax.ppermute(block, 'fsdp', self.perms[way])]
    reshape x7 -> x0, local copies, waits for them, and re-layouts: 31.4 us -> none  [the longest x2 15.6 us: my_units(): parted = matrix.reshape(matrix.shape[0], fsdps, seqs, unit_block)]
    pallas_call x0 -> x5, Pallas kernels: none -> 29.6 us  [the longest x2 11 us: take_units(): pl.pallas_call(body, grid_spec=pltpu.PrefetchScalarGridSpec(num_scalar_pr...]
    unnamed x246 -> x215, local copies, waits for them, and re-layouts: 37.5 us -> 13.5 us
    mul x6 -> x3, local copies, waits for them, and re-layouts: 21.4 us -> 1.62 us  [scaled(): return array.astype(F32) * factor]
    ppermute x35 -> x42, starting transfers between devices: 40.4 us -> 59.4 us  [send(): got = lax.ppermute(block, 'fsdp', self.perms[way])]
    dynamic_slice x3 -> x0, local copies, waits for them, and re-layouts: 19 us -> none  [the longest x2 16.7 us: my_units(): lax.dynamic_index_in_dim(parted, me, 2, keepdims=False)]
    mul x5 -> x1, other arithmetic: 17.3 us -> 1.01 us  [scaled(): return array.astype(F32) * factor]
  transfers between devices with their start and end apart: 101 -> 108, of which waited for: 35 -> 39; matrix products, arithmetic and copies ran while one was open for 37% -> 37% of each run, Pallas kernels for 9% -> 12%
where the time goes in v2:
time: 805 us; the launch traced here: 794 us
  waiting for transfers between devices  262 us (33%)
  matrix products  189 us (23%)
  Pallas kernels  119 us (15%)
  starting transfers between devices  105 us (13%)
  local copies, waits for them, and re-layouts  68.8 us (9%)
  other arithmetic  46.7 us (6%)
    ppermute x66, waiting for transfers between devices, swap(): return lax.ppermute(block, axis, [(i, i ^ offset) for i in range(count)])  159 us
    ppermute x42, waiting for transfers between devices, send(): got = lax.ppermute(block, 'fsdp', self.perms[way])  104 us
    dot_general x31, matrix products, mm_nt(): lax.dot_general(left, right, (((1,), (1,)), ((), ())), preferred_element_...  96.2 us
    dot_general x19, matrix products, mm(): return jnp.dot(left, right, preferred_element_type=F32)  81.6 us
    ppermute x42, starting transfers between devices, send(): got = lax.ppermute(block, 'fsdp', self.perms[way])  59.4 us
    ppermute x66, starting transfers between devices, swap(): return lax.ppermute(block, axis, [(i, i ^ offset) for i in range(count)])  45.6 us
    pallas_call x8, Pallas kernels, place_blocks(): pl.pallas_call(body, out_shape=jax.ShapeDtypeStruct((rows * total, column...  42.4 us
    pallas_call x1, Pallas kernels, attend_backward(): pl.pallas_call(lambda *refs: backward_body(blocks, *refs), grid_spec=pltp...  24.4 us
  transfers between devices with their start and end apart: 108, of which 39 were waited for; matrix products, arithmetic and copies ran while one was open for 37% of the time, Pallas kernels for 12%

profile of v2, /device:TPU:0, one launch (start us, length us, event | category | flops | bytes accessed | tf_op | source)
XLA Modules:
  0.0 794.5 jit_solution(9521655018367096287)
XLA Ops:
  25.1 7.1 collective-permute-done.4.refs_2_
  34.3 3.6 collective-permute-done
  51.0 4.4 collective-permute-done.18.refs_5_
  77.8 5.8 take_units.2
  107.5 4.0 collective-permute-done.31.refs_7_
  119.3 23.0 %attend_forward.1 = (bf16[1024,512]{1,0:T(8,128)(2,1)}, bf16[1024,256]{1,0:T(8,128)(2,1)}, bf16[1024,256]{1,0:T(8,128)(2,1)}, bf16[1024,512]{1,0:T(8,128)(2,1)}, f32[4,2,1024]{2,1,0:T(2,128)}) custom-call(s32[4]{0:T(128)} %pad_add_fusion.refs_0_, f32[1024,512]{1,0:T(8,128)} %slice_add_fusion.4.refs_1_, f32[1024,256]{1,0:T(8,128)} %pad_maximum_fusion.4.refs_2_, ...), custom_call_target="tpu_custom_call" | custom-call | flops 2147483648 | bytes 16777216 | tf_op jit(solution)/shard_map/attend_forward/pallas_call | solution.py:451
  145.7 9.0 %collective-permute-done.32.refs_6_ = bf16[256,2048]{1,0:T(8,128)(2,1)} collective-permute-done((bf16[256,2048]{1,0:T(8,128)(2,1)}, bf16[256,2048]{1,0:T(8,128)(2,1)}, u32[]{:S(2)}, u32[]{:S(2)}) %collective-permute-start.32) | collective-permute-done | bytes 1048608 | tf_op jit(solution)/shard_map/ppermute | solution.py:134
  167.9 4.3 collective-permute-done.15
  192.3 11.0 %collective-permute-done.28.refs_3_ = bf16[256,2048]{1,0:T(8,128)(2,1)S(1)} collective-permute-done((bf16[256,2048]{1,0:T(8,128)(2,1)}, bf16[256,2048]{1,0:T(8,128)(2,1)S(1)}, u32[]{:S(2)}, u32[]{:S(2)}) %collective-permute-start.28) | collective-permute-done | bytes 1048608 | tf_op jit(solution)/shard_map/ppermute | solution.py:134
  208.4 20.0 %collective-permute-done.38.refs_5_ = bf16[256,2048]{1,0:T(8,128)(2,1)} collective-permute-done((bf16[256,2048]{1,0:T(8,128)(2,1)}, bf16[256,2048]{1,0:T(8,128)(2,1)}, u32[]{:S(2)}, u32[]{:S(2)}) %collective-permute-start.38) | collective-permute-done | bytes 1048608 | tf_op jit(solution)/shard_map/ppermute | solution.py:134
  236.6 6.6 collective-permute-done.43.refs_1_
  247.5 11.8 %collective-permute-done.30.refs_4_ = bf16[256,2048]{1,0:T(8,128)(2,1)S(1)} collective-permute-done((bf16[256,2048]{1,0:T(8,128)(2,1)S(1)}, bf16[256,2048]{1,0:T(8,128)(2,1)S(1)}, u32[]{:S(2)}, u32[]{:S(2)}) %collective-permute-start.30) | collective-permute-done | bytes 1048608 | tf_op jit(solution)/shard_map/ppermute | solution.py:134
  261.7 5.2 take_units.3
  268.2 5.8 collective-permute-done.51.refs_15_
  278.5 8.7 %collective-permute-done.44.refs_2_ = bf16[128,2048]{1,0:T(8,128)(2,1)} collective-permute-done((bf16[128,2048]{1,0:T(8,128)(2,1)}, bf16[128,2048]{1,0:T(8,128)(2,1)}, u32[]{:S(2)}, u32[]{:S(2)}) %collective-permute-start.44) | collective-permute-done | bytes 524320 | tf_op jit(solution)/shard_map/ppermute | solution.py:134
  287.2 9.8 %collective-permute-start.50 = (bf16[128,2048]{1,0:T(8,128)(2,1)}, bf16[128,2048]{1,0:T(8,128)(2,1)}, u32[]{:S(2)}, u32[]{:S(2)}) collective-permute-start(bf16[128,2048]{1,0:T(8,128)(2,1)} %copy-done.60), channel_id=1, source_target_pairs={{2,0},{4,2},{6,4},{7,6},{5,7},{3,5},{1,3},{0,1},{10,8},{12,10},{14... | collective-permute-start | bytes 1572872 | tf_op jit(solution)/shard_map/ppermute | solution.py:134
  309.2 4.6 fusion.224
  313.8 7.1 place_blocks.10
  321.7 4.1 collective-permute-done.47.refs_10_
  327.7 7.1 place_blocks.11
  340.6 4.5 fusion.79
  346.3 15.7 %convolution_add_fusion.2 = f32[1024,2048]{1,0:T(8,128)} fusion(f32[1024,2048]{1,0:T(8,128)} %fusion.79, bf16[2048,2048]{1,0:T(8,128)(2,1)} %place_blocks.11, bf16[256,2048]{1,0:T(8,128)(2,1)} %collective-permute-done.25, bf16[256,2048]{1,0:T(8,128)(2,1)} %collective-permute-done.24, bf16[256,2048]{1,0:T(8,128)(2,1)} %collective-permute-done.23, ...), kind=kOutput, calls=%fused_computation.27 | convolution fusion | flops 8608808960 | bytes 29360128 | tf_op jit(solution)/shard_map/dot_general | solution.py:32
  362.0 14.7 %convolution_add_fusion.3 = f32[1024,2048]{1,0:T(8,128)} fusion(f32[1024,2048]{1,0:T(8,128)S(1)} %fusion.82, bf16[2048,2048]{1,0:T(8,128)(2,1)} %place_blocks.10, bf16[256,2048]{1,0:T(8,128)(2,1)} %collective-permute-done.25, bf16[256,2048]{1,0:T(8,128)(2,1)} %collective-permute-done.24, bf16[256,2048]{1,0:T(8,128)(2,1)} %collective-permute-done.23, ...), kind=kOutput, calls=%fused_computation.28 | convolution fusion | flops 8608808960 | bytes 29360128 | tf_op jit(solution)/shard_map/dot_general | solution.py:32
  376.7 7.3 place_blocks.12
  383.9 22.5 %multiply_convert_fusion = (bf16[1024,2048]{1,0:T(8,128)(2,1)}, bf16[1024,2048]{1,0:T(8,128)(2,1)}, bf16[1024,2048]{1,0:T(8,128)(2,1)}) fusion(f32[1024,2048]{1,0:T(8,128)} %convolution_add_fusion.3, f32[1024,2048]{1,0:T(8,128)} %convolution_add_fusion.2, f32[1024,2048]{1,0:T(8,128)} %fusion.224, bf16[1024,2048]{1,0:T(8,128)(2,1)} %copy-done.6, ...), kind=kOutput, calls=%fused_computation.5 | convolution fusion | flops 8625586176 | bytes 50331648 | tf_op jit(solution)/shard_map/dot_general | solution.py:36
  406.5 14.7 %fusion.225 = f32[1024,2048]{1,0:T(8,128)} fusion(bf16[1024,2048]{1,0:T(8,128)(2,1)} %get-tuple-element.108, bf16[2048,2048]{1,0:T(8,128)(2,1)} %place_blocks.11), kind=kOutput, calls=%fused_computation.392 | convolution fusion | flops 8589934592 | bytes 20971520 | tf_op jit(solution)/shard_map/dot_general | solution.py:36
  424.6 4.5 fusion.57
  429.2 19.4 %fusion.221 = (bf16[1024,2048]{1,0:T(8,128)(2,1)}, f32[1024,2048]{1,0:T(8,128)}) fusion(f32[1024,2048]{1,0:T(8,128)} %fusion.57, f32[1024,2048]{1,0:T(8,128)} %fusion.225, bf16[1024,2048]{1,0:T(8,128)(2,1)} %get-tuple-element.107, bf16[2048,2048]{1,0:T(8,128)(2,1)} %place_blocks.10), kind=kOutput, calls=%fused_computation.388 | convolution fusion | flops 8596226048 | bytes 41943040 | tf_op jit(solution)/shard_map/dot_general | solution.py:36
  448.6 3.6 fusion.26
  455.8 13.5 %fusion.222 = (bf16[1024,2048]{1,0:T(8,128)(2,1)}, f32[1024,2048]{1,0:T(8,128)}) fusion(f32[1024,2048]{1,0:T(8,128)S(1)} %fusion.70, bf16[1024,2048]{1,0:T(8,128)(2,1)} %get-tuple-element.99, bf16[2048,2048]{1,0:T(8,128)(2,1)S(1)} %bitcast.222), kind=kOutput, calls=%fused_computation.389 | convolution fusion | flops 8594128896 | bytes 33554432 | tf_op jit(solution)/shard_map/dot_general | solution.py:32
  483.4 7.3 collective-permute-done.86
  499.3 16.1 %collective-permute-done.87 = bf16[960,512]{1,0:T(8,128)(2,1)S(1)} collective-permute-done((bf16[960,512]{1,0:T(8,128)(2,1)S(1)}, bf16[960,512]{1,0:T(8,128)(2,1)S(1)}, u32[]{:S(2)}, u32[]{:S(2)}) %collective-permute-start.87) | collective-permute-done | bytes 983072 | tf_op jit(solution)/shard_map/ppermute | solution.py:90
  526.4 16.4 %collective-permute-done.59 = bf16[256,2048]{1,0:T(8,128)(2,1)} collective-permute-done((bf16[256,2048]{1,0:T(8,128)(2,1)}, bf16[256,2048]{1,0:T(8,128)(2,1)}, u32[]{:S(2)}, u32[]{:S(2)}) %collective-permute-start.59) | collective-permute-done | bytes 1048608 | tf_op jit(solution)/shard_map/ppermute | solution.py:90
  542.8 5.4 multiply_convert_fusion.3
  575.2 24.4 %attend_backward.1 = (bf16[1024,512]{1,0:T(8,128)(2,1)}, bf16[1024,256]{1,0:T(8,128)(2,1)}, bf16[1024,256]{1,0:T(8,128)(2,1)}) custom-call(s32[4]{0:T(128)} %pad_add_fusion.refs_0_, bf16[1024,512]{1,0:T(8,128)(2,1)} %get-tuple-element.100.refs_1_, bf16[1024,256]{1,0:T(8,128)(2,1)} %get-tuple-element.101.refs_2_, ...), custom_call_target="tpu_custom_call" | custom-call | flops 5368709120 | bytes 16777216 | tf_op jit(solution)/shard_map/attend_backward/pallas_call | solution.py:481
  604.4 3.8 concatenate.120
  616.5 4.7 collective-permute-done.98
  622.6 15.5 %collective-permute-done.68 = bf16[256,768]{1,0:T(8,128)(2,1)S(1)} collective-permute-done((bf16[256,768]{1,0:T(8,128)(2,1)S(1)}, bf16[256,768]{1,0:T(8,128)(2,1)S(1)}, u32[]{:S(2)}, u32[]{:S(2)}) %collective-permute-start.68) | collective-permute-done | bytes 393248 | tf_op jit(solution)/shard_map/ppermute | solution.py:90
  642.1 10.1 %collective-permute-done.90 = bf16[240,512]{1,0:T(8,128)(2,1)S(1)} collective-permute-done((bf16[240,512]{1,0:T(8,128)(2,1)S(1)}, bf16[240,512]{1,0:T(8,128)(2,1)S(1)}, u32[]{:S(2)}, u32[]{:S(2)}) %collective-permute-start.90) | collective-permute-done | bytes 245792 | tf_op jit(solution)/shard_map/ppermute | solution.py:90
  655.3 11.0 %collective-permute-done.91 = bf16[480,512]{1,0:T(8,128)(2,1)S(1)} collective-permute-done((bf16[480,512]{1,0:T(8,128)(2,1)S(1)}, bf16[480,512]{1,0:T(8,128)(2,1)S(1)}, u32[]{:S(2)}, u32[]{:S(2)}) %collective-permute-start.91) | collective-permute-done | bytes 491552 | tf_op jit(solution)/shard_map/ppermute | solution.py:90
  674.2 15.2 %collective-permute-done.92 = bf16[960,512]{1,0:T(8,128)(2,1)S(1)} collective-permute-done((bf16[960,512]{1,0:T(8,128)(2,1)S(1)}, bf16[960,512]{1,0:T(8,128)(2,1)S(1)}, u32[]{:S(2)}, u32[]{:S(2)}) %collective-permute-start.92) | collective-permute-done | bytes 983072 | tf_op jit(solution)/shard_map/ppermute | solution.py:90
  713.8 16.3 %collective-permute-done.93.refs_1_ = bf16[1920,512]{1,0:T(8,128)(2,1)} collective-permute-done((bf16[1920,512]{1,0:T(8,128)(2,1)}, bf16[1920,512]{1,0:T(8,128)(2,1)}, u32[]{:S(2)}, u32[]{:S(2)}) %collective-permute-start.93) | collective-permute-done | bytes 1966112 | tf_op jit(solution)/shard_map/ppermute | solution.py:90
  738.7 9.3 %collective-permute-done.105.refs_1_ = bf16[512,512]{1,0:T(8,128)(2,1)S(1)} collective-permute-done((bf16[512,512]{1,0:T(8,128)(2,1)S(1)}, bf16[512,512]{1,0:T(8,128)(2,1)S(1)}, u32[]{:S(2)}, u32[]{:S(2)}) %collective-permute-start.105) | collective-permute-done | bytes 524320 | tf_op jit(solution)/shard_map/ppermute | solution.py:90
  748.5 7.4 collective-permute-done.81.refs_1_
  767.8 7.6 place_blocks.14
  775.4 5.2 finish_model.1
  780.6 9.2 %finish_units.1 = (f32[8192,128]{1,0:T(8,128)}, f32[2,128,8192]{2,1,0:T(8,128)}) custom-call(bf16[4,1920,512]{2,1,0:T(8,128)(2,1)} %bitcast.216, bf16[4,1920,512]{2,1,0:T(8,128)(2,1)} %bitcast.217, bf16[4,1920,512]{2,1,0:T(8,128)(2,1)} %bitcast.218), custom_call_target="tpu_custom_call" | custom-call | tf_op jit(solution)/shard_map/finish_units/pallas_call | solution.py:260
  789.8 4.3 finish_late.1
  (574 shorter events, 318.8 us)
Async XLA Ops:
  25.0 70.5 %collective-permute-start.1 = (bf16[256,2048]{1,0:T(8,128)(2,1)}, bf16[256,2048]{1,0:T(8,128)(2,1)}, u32[]{:S(2)}, u32[]{:S(2)}) collective-permute-start(bf16[256,2048]{1,0:T(8,128)(2,1)} %fusion.14), channel_id=1, source_target_pairs={{0,8},{8,0},{16,24},{24,16},{1,9},{9,1},{17,25},{25,17},{2,10},{10... | collective-permute-start | bytes 3145736 | tf_op jit(solution)/shard_map/ppermute | solution.py:90
  37.8 59.2 %collective-permute-start.2 = (bf16[256,2048]{1,0:T(8,128)(2,1)}, bf16[256,2048]{1,0:T(8,128)(2,1)}, u32[]{:S(2)}, u32[]{:S(2)}) collective-permute-start(bf16[256,2048]{1,0:T(8,128)(2,1)} %collective-permute-done), channel_id=1, source_target_pairs={{0,8},{8,0},{16,24},{24,16},{1,9},{9,1},{17,25},{25,17},{2,10},{10... | collective-permute-start | bytes 3145736 | tf_op jit(solution)/shard_map/ppermute | solution.py:90
  48.7 41.6 %collective-permute-start.8 = (bf16[256,768]{1,0:T(8,128)(2,1)}, bf16[256,768]{1,0:T(8,128)(2,1)}, u32[]{:S(2)}, u32[]{:S(2)}) collective-permute-start(bf16[256,768]{1,0:T(8,128)(2,1)} %collective-permute-done.6.refs_3_), channel_id=1, source_target_pairs={{0,2},{2,4},{4,6},{6,7},{7,5},{5,3},{3,1},{1,0},{8,10},{10,12},{12... | collective-permute-start | bytes 1179656 | tf_op jit(solution)/shard_map/ppermute | solution.py:134
  55.4 31.4 %collective-permute-start.16 = (bf16[256,512]{1,0:T(8,128)(2,1)}, bf16[256,512]{1,0:T(8,128)(2,1)}, u32[]{:S(2)}, u32[]{:S(2)}) collective-permute-start(bf16[256,512]{1,0:T(8,128)(2,1)} %copy-done.70), channel_id=1, source_target_pairs={{0,2},{2,4},{4,6},{6,7},{7,5},{5,3},{3,1},{1,0},{8,10},{10,12},{12... | collective-permute-start | bytes 786440 | tf_op jit(solution)/shard_map/ppermute | solution.py:134
  57.1 28.1 %collective-permute-start.19 = (bf16[256,512]{1,0:T(8,128)(2,1)}, bf16[256,512]{1,0:T(8,128)(2,1)}, u32[]{:S(2)}, u32[]{:S(2)}) collective-permute-start(bf16[256,512]{1,0:T(8,128)(2,1)} %collective-permute-done.18.refs_5_), channel_id=1, source_target_pairs={{2,0},{4,2},{6,4},{7,6},{5,7},{3,5},{1,3},{0,1},{10,8},{12,10},{14... | collective-permute-start | bytes 786440 | tf_op jit(solution)/shard_map/ppermute | solution.py:134
  85.2 26.3 %collective-permute-start.31 = (bf16[256,2048]{1,0:T(8,128)(2,1)}, bf16[256,2048]{1,0:T(8,128)(2,1)}, u32[]{:S(2)}, u32[]{:S(2)}) collective-permute-start(bf16[256,2048]{1,0:T(8,128)(2,1)} %get-tuple-element.76.refs_0_), channel_id=1, source_target_pairs={{2,0},{4,2},{6,4},{7,6},{5,7},{3,5},{1,3},{0,1},{10,8},{12,10},{14... | collective-permute-start | bytes 3145736 | tf_op jit(solution)/shard_map/ppermute | solution.py:134
  90.3 52.1 %collective-permute-start.36 = (bf16[256,2048]{1,0:T(8,128)(2,1)}, bf16[256,2048]{1,0:T(8,128)(2,1)}, u32[]{:S(2)}, u32[]{:S(2)}) collective-permute-start(bf16[256,2048]{1,0:T(8,128)(2,1)} %get-tuple-element.81.refs_0_), channel_id=1, source_target_pairs={{2,0},{4,2},{6,4},{7,6},{5,7},{3,5},{1,3},{0,1},{10,8},{12,10},{14... | collective-permute-start | bytes 3145736 | tf_op jit(solution)/shard_map/ppermute | solution.py:134
  95.4 62.8 %collective-permute-start.20 = (bf16[2048,512]{1,0:T(8,128)(2,1)}, bf16[2048,512]{1,0:T(8,128)(2,1)}, u32[]{:S(2)}, u32[]{:S(2)}) collective-permute-start(bf16[2048,512]{1,0:T(8,128)(2,1)} %place_blocks.9), channel_id=1, source_target_pairs={{0,16},{8,24},{16,0},{24,8},{1,17},{9,25},{17,1},{25,9},{2,18},{10... | collective-permute-start | bytes 6291464 | tf_op jit(solution)/shard_map/ppermute | solution.py:90
  97.0 59.2 %collective-permute-start.29 = (bf16[256,2048]{1,0:T(8,128)(2,1)}, bf16[256,2048]{1,0:T(8,128)(2,1)}, u32[]{:S(2)}, u32[]{:S(2)}) collective-permute-start(bf16[256,2048]{1,0:T(8,128)(2,1)} %get-tuple-element.81.refs_0_), channel_id=1, source_target_pairs={{0,2},{2,4},{4,6},{6,7},{7,5},{5,3},{3,1},{1,0},{8,10},{10,12},{12... | collective-permute-start | bytes 3145736 | tf_op jit(solution)/shard_map/ppermute | solution.py:134
  111.6 43.1 %collective-permute-start.32 = (bf16[256,2048]{1,0:T(8,128)(2,1)}, bf16[256,2048]{1,0:T(8,128)(2,1)}, u32[]{:S(2)}, u32[]{:S(2)}) collective-permute-start(bf16[256,2048]{1,0:T(8,128)(2,1)} %collective-permute-done.31.refs_7_), channel_id=1, source_target_pairs={{2,0},{4,2},{6,4},{7,6},{5,7},{3,5},{1,3},{0,1},{10,8},{12,10},{14... | collective-permute-start | bytes 3145736 | tf_op jit(solution)/shard_map/ppermute | solution.py:134
  113.2 44.6 %collective-permute-start.27 = (bf16[256,2048]{1,0:T(8,128)(2,1)}, bf16[256,2048]{1,0:T(8,128)(2,1)}, u32[]{:S(2)}, u32[]{:S(2)}) collective-permute-start(bf16[256,2048]{1,0:T(8,128)(2,1)} %collective-permute-done.26.refs_1_), channel_id=1, source_target_pairs={{0,2},{2,4},{4,6},{6,7},{7,5},{5,3},{3,1},{1,0},{8,10},{10,12},{12... | collective-permute-start | bytes 3145736 | tf_op jit(solution)/shard_map/ppermute | solution.py:134
  142.4 61.3 %collective-permute-start.21 = (bf16[2048,512]{1,0:T(8,128)(2,1)}, bf16[2048,512]{1,0:T(8,128)(2,1)}, u32[]{:S(2)}, u32[]{:S(2)}) collective-permute-start(bf16[2048,512]{1,0:T(8,128)(2,1)} %place_blocks.9), channel_id=1, source_target_pairs={{0,8},{8,0},{16,24},{24,16},{1,9},{9,1},{17,25},{25,17},{2,10},{10... | collective-permute-start | bytes 6291464 | tf_op jit(solution)/shard_map/ppermute | solution.py:90
  157.7 26.3 %collective-permute-start.34 = (bf16[256,2048]{1,0:T(8,128)(2,1)}, bf16[256,2048]{1,0:T(8,128)(2,1)}, u32[]{:S(2)}, u32[]{:S(2)}) collective-permute-start(bf16[256,2048]{1,0:T(8,128)(2,1)} %collective-permute-done.29.refs_1_), channel_id=1, source_target_pairs={{0,2},{2,4},{4,6},{6,7},{7,5},{5,3},{3,1},{1,0},{8,10},{10,12},{12... | collective-permute-start | bytes 3145736 | tf_op jit(solution)/shard_map/ppermute | solution.py:134
  158.3 71.7 %collective-permute-start.22 = (bf16[2048,512]{1,0:T(8,128)(2,1)}, bf16[2048,512]{1,0:T(8,128)(2,1)}, u32[]{:S(2)}, u32[]{:S(2)}) collective-permute-start(bf16[2048,512]{1,0:T(8,128)(2,1)} %collective-permute-done.20), channel_id=1, source_target_pairs={{0,8},{8,0},{16,24},{24,16},{1,9},{9,1},{17,25},{25,17},{2,10},{10... | collective-permute-start | bytes 6291464 | tf_op jit(solution)/shard_map/ppermute | solution.py:90
  172.1 31.2 %collective-permute-start.28 = (bf16[256,2048]{1,0:T(8,128)(2,1)}, bf16[256,2048]{1,0:T(8,128)(2,1)S(1)}, u32[]{:S(2)}, u32[]{:S(2)}) collective-permute-start(bf16[256,2048]{1,0:T(8,128)(2,1)} %collective-permute-done.27.refs_2_), channel_id=1, source_target_pairs={{0,2},{2,4},{4,6},{6,7},{7,5},{5,3},{3,1},{1,0},{8,10},{10,12},{12... | collective-permute-start | bytes 3145736 | tf_op jit(solution)/shard_map/ppermute | solution.py:134
  179.6 27.2 %collective-permute-start.33 = (bf16[256,2048]{1,0:T(8,128)(2,1)}, bf16[256,2048]{1,0:T(8,128)(2,1)S(1)}, u32[]{:S(2)}, u32[]{:S(2)}) collective-permute-start(bf16[256,2048]{1,0:T(8,128)(2,1)} %collective-permute-done.32.refs_6_), channel_id=1, source_target_pairs={{2,0},{4,2},{6,4},{7,6},{5,7},{3,5},{1,3},{0,1},{10,8},{12,10},{14... | collective-permute-start | bytes 3145736 | tf_op jit(solution)/shard_map/ppermute | solution.py:134
  184.1 44.3 %collective-permute-start.38 = (bf16[256,2048]{1,0:T(8,128)(2,1)}, bf16[256,2048]{1,0:T(8,128)(2,1)}, u32[]{:S(2)}, u32[]{:S(2)}) collective-permute-start(bf16[256,2048]{1,0:T(8,128)(2,1)} %collective-permute-done.37.refs_6_), channel_id=1, source_target_pairs={{2,0},{4,2},{6,4},{7,6},{5,7},{3,5},{1,3},{0,1},{10,8},{12,10},{14... | collective-permute-start | bytes 3145736 | tf_op jit(solution)/shard_map/ppermute | solution.py:134
  203.3 32.7 %collective-permute-start.40 = (bf16[256,2048]{1,0:T(8,128)(2,1)}, bf16[256,2048]{1,0:T(8,128)(2,1)}, u32[]{:S(2)}, u32[]{:S(2)}) collective-permute-start(bf16[256,2048]{1,0:T(8,128)(2,1)} %bitcast.27), channel_id=1, source_target_pairs={{0,16},{8,24},{16,0},{24,8},{1,17},{9,25},{17,1},{25,9},{2,18},{10... | collective-permute-start | bytes 3145736 | tf_op jit(solution)/shard_map/ppermute | solution.py:90
  203.7 41.0 %collective-permute-start.35 = (bf16[256,2048]{1,0:T(8,128)(2,1)}, bf16[256,2048]{1,0:T(8,128)(2,1)}, u32[]{:S(2)}, u32[]{:S(2)}) collective-permute-start(bf16[256,2048]{1,0:T(8,128)(2,1)} %collective-permute-done.34.refs_2_), channel_id=1, source_target_pairs={{0,2},{2,4},{4,6},{6,7},{7,5},{5,3},{3,1},{1,0},{8,10},{10,12},{12... | collective-permute-start | bytes 3145736 | tf_op jit(solution)/shard_map/ppermute | solution.py:134
  206.7 29.4 %collective-permute-start.49 = (bf16[128,2048]{1,0:T(8,128)(2,1)S(1)}, bf16[128,2048]{1,0:T(8,128)(2,1)S(1)}, u32[]{:S(2)}, u32[]{:S(2)}) collective-permute-start(bf16[128,2048]{1,0:T(8,128)(2,1)S(1)} %get-tuple-element.91.refs_0_), channel_id=1, source_target_pairs={{2,0},{4,2},{6,4},{7,6},{5,7},{3,5},{1,3},{0,1},{10,8},{12,10},{14... | collective-permute-start | bytes 1572872 | tf_op jit(solution)/shard_map/ppermute | solution.py:134
  230.0 29.4 %collective-permute-start.30 = (bf16[256,2048]{1,0:T(8,128)(2,1)S(1)}, bf16[256,2048]{1,0:T(8,128)(2,1)S(1)}, u32[]{:S(2)}, u32[]{:S(2)}) collective-permute-start(bf16[256,2048]{1,0:T(8,128)(2,1)S(1)} %collective-permute-done.28.refs_3_), channel_id=1, source_target_pairs={{0,2},{2,4},{4,6},{6,7},{7,5},{5,3},{3,1},{1,0},{8,10},{10,12},{12... | collective-permute-start | bytes 3145736 | tf_op jit(solution)/shard_map/ppermute | solution.py:134
  236.0 41.9 %collective-permute-start.41 = (bf16[256,2048]{1,0:T(8,128)(2,1)}, bf16[256,2048]{1,0:T(8,128)(2,1)}, u32[]{:S(2)}, u32[]{:S(2)}) collective-permute-start(bf16[256,2048]{1,0:T(8,128)(2,1)} %bitcast.27), channel_id=1, source_target_pairs={{0,8},{8,0},{16,24},{24,16},{1,9},{9,1},{17,25},{25,17},{2,10},{10... | collective-permute-start | bytes 3145736 | tf_op jit(solution)/shard_map/ppermute | solution.py:90
  236.1 41.8 %collective-permute-start.42 = (bf16[256,2048]{1,0:T(8,128)(2,1)}, bf16[256,2048]{1,0:T(8,128)(2,1)}, u32[]{:S(2)}, u32[]{:S(2)}) collective-permute-start(bf16[256,2048]{1,0:T(8,128)(2,1)} %collective-permute-done.40), channel_id=1, source_target_pairs={{0,8},{8,0},{16,24},{24,16},{1,9},{9,1},{17,25},{25,17},{2,10},{10... | collective-permute-start | bytes 3145736 | tf_op jit(solution)/shard_map/ppermute | solution.py:90
  243.2 33.1 %collective-permute-start.39 = (bf16[256,2048]{1,0:T(8,128)(2,1)}, bf16[256,2048]{1,0:T(8,128)(2,1)S(1)}, u32[]{:S(2)}, u32[]{:S(2)}) collective-permute-start(bf16[256,2048]{1,0:T(8,128)(2,1)} %collective-permute-done.38.refs_5_), channel_id=1, source_target_pairs={{2,0},{4,2},{6,4},{7,6},{5,7},{3,5},{1,3},{0,1},{10,8},{12,10},{14... | collective-permute-start | bytes 3145736 | tf_op jit(solution)/shard_map/ppermute | solution.py:134
  244.7 29.3 %collective-permute-start.51 = (bf16[128,2048]{1,0:T(8,128)(2,1)}, bf16[128,2048]{1,0:T(8,128)(2,1)}, u32[]{:S(2)}, u32[]{:S(2)}) collective-permute-start(bf16[128,2048]{1,0:T(8,128)(2,1)} %get-tuple-element.93.refs_8_), channel_id=1, source_target_pairs={{2,0},{4,2},{6,4},{7,6},{5,7},{3,5},{1,3},{0,1},{10,8},{12,10},{14... | collective-permute-start | bytes 1572872 | tf_op jit(solution)/shard_map/ppermute | solution.py:134
  260.3 36.6 %collective-permute-start.23 = (bf16[256,2048]{1,0:T(8,128)(2,1)}, bf16[256,2048]{1,0:T(8,128)(2,1)}, u32[]{:S(2)}, u32[]{:S(2)}) collective-permute-start(bf16[256,2048]{1,0:T(8,128)(2,1)} %multiply_convert_fusion.4), channel_id=1, source_target_pairs={{0,16},{8,24},{16,0},{24,8},{1,17},{9,25},{17,1},{25,9},{2,18},{10... | collective-permute-start | bytes 3145736 | tf_op jit(solution)/shard_map/ppermute | solution.py:90
  277.9 58.6 %collective-permute-start.24 = (bf16[256,2048]{1,0:T(8,128)(2,1)}, bf16[256,2048]{1,0:T(8,128)(2,1)}, u32[]{:S(2)}, u32[]{:S(2)}) collective-permute-start(bf16[256,2048]{1,0:T(8,128)(2,1)} %multiply_convert_fusion.4), channel_id=1, source_target_pairs={{0,8},{8,0},{16,24},{24,16},{1,9},{9,1},{17,25},{25,17},{2,10},{10... | collective-permute-start | bytes 3145736 | tf_op jit(solution)/shard_map/ppermute | solution.py:90
  297.0 40.0 %collective-permute-start.25 = (bf16[256,2048]{1,0:T(8,128)(2,1)}, bf16[256,2048]{1,0:T(8,128)(2,1)}, u32[]{:S(2)}, u32[]{:S(2)}) collective-permute-start(bf16[256,2048]{1,0:T(8,128)(2,1)} %collective-permute-done.23), channel_id=1, source_target_pairs={{0,8},{8,0},{16,24},{24,16},{1,9},{9,1},{17,25},{25,17},{2,10},{10... | collective-permute-start | bytes 3145736 | tf_op jit(solution)/shard_map/ppermute | solution.py:90
  306.8 28.0 %collective-permute-start.55 = (bf16[128,2048]{1,0:T(8,128)(2,1)S(1)}, bf16[128,2048]{1,0:T(8,128)(2,1)}, u32[]{:S(2)}, u32[]{:S(2)}) collective-permute-start(bf16[128,2048]{1,0:T(8,128)(2,1)S(1)} %collective-permute-done.54.refs_14_), channel_id=1, source_target_pairs={{2,0},{4,2},{6,4},{7,6},{5,7},{3,5},{1,3},{0,1},{10,8},{12,10},{14... | collective-permute-start | bytes 1572872 | tf_op jit(solution)/shard_map/ppermute | solution.py:134
  320.9 198.0 %collective-permute-start.69 = (bf16[2048,768]{1,0:T(8,128)(2,1)}, bf16[2048,768]{1,0:T(8,128)(2,1)}, u32[]{:S(2)}, u32[]{:S(2)}) collective-permute-start(bf16[2048,768]{1,0:T(8,128)(2,1)} %place_blocks.8), channel_id=1, source_target_pairs={{0,16},{8,24},{16,0},{24,8},{1,17},{9,25},{17,1},{25,9},{2,18},{10... | collective-permute-start | bytes 9437192 | tf_op jit(solution)/shard_map/ppermute | solution.py:90
  325.8 50.8 %collective-permute-start.48 = (bf16[128,2048]{1,0:T(8,128)(2,1)}, bf16[128,2048]{1,0:T(8,128)(2,1)}, u32[]{:S(2)}, u32[]{:S(2)}) collective-permute-start(bf16[128,2048]{1,0:T(8,128)(2,1)} %collective-permute-done.46.refs_3_), channel_id=1, source_target_pairs={{0,2},{2,4},{4,6},{6,7},{7,5},{5,3},{3,1},{1,0},{8,10},{10,12},{12... | collective-permute-start | bytes 1572872 | tf_op jit(solution)/shard_map/ppermute | solution.py:134
  334.9 41.8 %collective-permute-start.53 = (bf16[128,2048]{1,0:T(8,128)(2,1)}, bf16[128,2048]{1,0:T(8,128)(2,1)}, u32[]{:S(2)}, u32[]{:S(2)}) collective-permute-start(bf16[128,2048]{1,0:T(8,128)(2,1)} %collective-permute-done.47.refs_10_), channel_id=1, source_target_pairs={{0,2},{2,4},{4,6},{6,7},{7,5},{5,3},{3,1},{1,0},{8,10},{10,12},{12... | collective-permute-start | bytes 1572872 | tf_op jit(solution)/shard_map/ppermute | solution.py:134
  336.5 40.1 %collective-permute-start.52 = (bf16[128,2048]{1,0:T(8,128)(2,1)}, bf16[128,2048]{1,0:T(8,128)(2,1)}, u32[]{:S(2)}, u32[]{:S(2)}) collective-permute-start(bf16[128,2048]{1,0:T(8,128)(2,1)} %collective-permute-done.50.refs_6_), channel_id=1, source_target_pairs={{2,0},{4,2},{6,4},{7,6},{5,7},{3,5},{1,3},{0,1},{10,8},{12,10},{14... | collective-permute-start | bytes 1572872 | tf_op jit(solution)/shard_map/ppermute | solution.py:134
  337.0 39.7 %collective-permute-start.56 = (bf16[128,2048]{1,0:T(8,128)(2,1)}, bf16[128,2048]{1,0:T(8,128)(2,1)}, u32[]{:S(2)}, u32[]{:S(2)}) collective-permute-start(bf16[128,2048]{1,0:T(8,128)(2,1)} %collective-permute-done.55.refs_13_), channel_id=1, source_target_pairs={{2,0},{4,2},{6,4},{7,6},{5,7},{3,5},{1,3},{0,1},{10,8},{12,10},{14... | collective-permute-start | bytes 1572872 | tf_op jit(solution)/shard_map/ppermute | solution.py:134
  483.3 35.7 %collective-permute-start.60 = (bf16[256,2048]{1,0:T(8,128)(2,1)}, bf16[256,2048]{1,0:T(8,128)(2,1)S(1)}, u32[]{:S(2)}, u32[]{:S(2)}) collective-permute-start(bf16[256,2048]{1,0:T(8,128)(2,1)} %get-tuple-element.118), channel_id=1, source_target_pairs={{0,8},{8,0},{16,24},{24,16},{1,9},{9,1},{17,25},{25,17},{2,10},{10... | collective-permute-start | bytes 3145736 | tf_op jit(solution)/shard_map/ppermute | solution.py:90
  496.0 26.3 %collective-permute-start.62 = (bf16[256,2048]{1,0:T(8,128)(2,1)}, bf16[256,2048]{1,0:T(8,128)(2,1)}, u32[]{:S(2)}, u32[]{:S(2)}) collective-permute-start(bf16[256,2048]{1,0:T(8,128)(2,1)} %fusion.16), channel_id=1, source_target_pairs={{0,16},{8,24},{16,0},{24,8},{1,17},{9,25},{17,1},{25,9},{2,18},{10... | collective-permute-start | bytes 3145736 | tf_op jit(solution)/shard_map/ppermute | solution.py:90
  496.4 30.0 %collective-permute-start.57 = (bf16[256,2048]{1,0:T(8,128)(2,1)}, bf16[256,2048]{1,0:T(8,128)(2,1)}, u32[]{:S(2)}, u32[]{:S(2)}) collective-permute-start(bf16[256,2048]{1,0:T(8,128)(2,1)} %get-tuple-element.120), channel_id=1, source_target_pairs={{0,8},{8,0},{16,24},{24,16},{1,9},{9,1},{17,25},{25,17},{2,10},{10... | collective-permute-start | bytes 3145736 | tf_op jit(solution)/shard_map/ppermute | solution.py:90
  515.4 27.4 %collective-permute-start.59 = (bf16[256,2048]{1,0:T(8,128)(2,1)}, bf16[256,2048]{1,0:T(8,128)(2,1)}, u32[]{:S(2)}, u32[]{:S(2)}) collective-permute-start(bf16[256,2048]{1,0:T(8,128)(2,1)} %fusion.19), channel_id=1, source_target_pairs={{0,16},{8,24},{16,0},{24,8},{1,17},{9,25},{17,1},{25,9},{2,18},{10... | collective-permute-start | bytes 3145736 | tf_op jit(solution)/shard_map/ppermute | solution.py:90
  518.9 184.3 %collective-permute-start.70 = (bf16[2048,768]{1,0:T(8,128)(2,1)}, bf16[2048,768]{1,0:T(8,128)(2,1)}, u32[]{:S(2)}, u32[]{:S(2)}) collective-permute-start(bf16[2048,768]{1,0:T(8,128)(2,1)} %place_blocks.8), channel_id=1, source_target_pairs={{0,8},{8,0},{16,24},{24,16},{1,9},{9,1},{17,25},{25,17},{2,10},{10... | collective-permute-start | bytes 9437192 | tf_op jit(solution)/shard_map/ppermute | solution.py:90
  519.0 215.7 %collective-permute-start.71 = (bf16[2048,768]{1,0:T(8,128)(2,1)}, bf16[2048,768]{1,0:T(8,128)(2,1)}, u32[]{:S(2)}, u32[]{:S(2)}) collective-permute-start(bf16[2048,768]{1,0:T(8,128)(2,1)} %collective-permute-done.69), channel_id=1, source_target_pairs={{0,8},{8,0},{16,24},{24,16},{1,9},{9,1},{17,25},{25,17},{2,10},{10... | collective-permute-start | bytes 9437192 | tf_op jit(solution)/shard_map/ppermute | solution.py:90
  522.4 40.4 %collective-permute-start.88 = (bf16[480,512]{1,0:T(8,128)(2,1)S(1)}, bf16[480,512]{1,0:T(8,128)(2,1)S(1)}, u32[]{:S(2)}, u32[]{:S(2)}) collective-permute-start(bf16[480,512]{1,0:T(8,128)(2,1)S(1)} %constant_dynamic-slice_fusion.5), channel_id=1, source_target_pairs={{0,2},{1,3},{2,0},{3,1},{4,6},{5,7},{6,4},{7,5},{8,10},{9,11},{10,... | collective-permute-start | bytes 1474568 | tf_op jit(solution)/shard_map/ppermute | solution.py:90
  568.8 41.7 %collective-permute-start.97 = (bf16[256,512]{1,0:T(8,128)(2,1)}, bf16[256,512]{1,0:T(8,128)(2,1)}, u32[]{:S(2)}, u32[]{:S(2)}) collective-permute-start(bf16[256,512]{1,0:T(8,128)(2,1)} %get-tuple-element.133), channel_id=1, source_target_pairs={{0,8},{8,0},{16,24},{24,16},{1,9},{9,1},{17,25},{25,17},{2,10},{10... | collective-permute-start | bytes 786440 | tf_op jit(solution)/shard_map/ppermute | solution.py:90
  568.8 46.9 %collective-permute-start.96 = (bf16[256,512]{1,0:T(8,128)(2,1)}, bf16[256,512]{1,0:T(8,128)(2,1)}, u32[]{:S(2)}, u32[]{:S(2)}) collective-permute-start(bf16[256,512]{1,0:T(8,128)(2,1)} %get-tuple-element.132), channel_id=1, source_target_pairs={{0,8},{8,0},{16,24},{24,16},{1,9},{9,1},{17,25},{25,17},{2,10},{10... | collective-permute-start | bytes 786440 | tf_op jit(solution)/shard_map/ppermute | solution.py:90
  571.4 42.5 %collective-permute-start.89 = (bf16[240,512]{1,0:T(8,128)(2,1)}, bf16[240,512]{1,0:T(8,128)(2,1)}, u32[]{:S(2)}, u32[]{:S(2)}) collective-permute-start(bf16[240,512]{1,0:T(8,128)(2,1)} %constant_dynamic-slice_fusion.4), channel_id=1, source_target_pairs={{0,4},{1,5},{2,6},{3,7},{4,0},{5,1},{6,2},{7,3},{8,12},{9,13},{10,... | collective-permute-start | bytes 737288 | tf_op jit(solution)/shard_map/ppermute | solution.py:90
  641.7 28.2 %collective-permute-start.72 = (bf16[256,384]{0,1:T(8,128)(2,1)S(1)}, bf16[256,384]{0,1:T(8,128)(2,1)S(1)}, u32[]{:S(2)}, u32[]{:S(2)}) collective-permute-start(bf16[256,384]{0,1:T(8,128)(2,1)S(1)} %maximum_multiply_fusion), channel_id=1, source_target_pairs={{0,16},{8,24},{16,0},{24,8},{1,17},{9,25},{17,1},{25,9},{2,18},{10... | collective-permute-start | bytes 589832 | tf_op jit(solution)/shard_map/ppermute | solution.py:90
  690.8 39.3 %collective-permute-start.93 = (bf16[1920,512]{1,0:T(8,128)(2,1)}, bf16[1920,512]{1,0:T(8,128)(2,1)}, u32[]{:S(2)}, u32[]{:S(2)}) collective-permute-start(bf16[1920,512]{1,0:T(8,128)(2,1)} %pad_maximum_fusion.2.refs_0_), channel_id=1, source_target_pairs={{0,16},{8,24},{16,0},{24,8},{1,17},{9,25},{17,1},{25,9},{2,18},{10... | collective-permute-start | bytes 5898248 | tf_op jit(solution)/shard_map/ppermute | solution.py:90
  713.8 53.9 %collective-permute-start.94 = (bf16[1920,512]{1,0:T(8,128)(2,1)}, bf16[1920,512]{1,0:T(8,128)(2,1)}, u32[]{:S(2)}, u32[]{:S(2)}) collective-permute-start(bf16[1920,512]{1,0:T(8,128)(2,1)} %pad_maximum_fusion.2.refs_0_), channel_id=1, source_target_pairs={{0,8},{8,0},{16,24},{24,16},{1,9},{9,1},{17,25},{25,17},{2,10},{10... | collective-permute-start | bytes 5898248 | tf_op jit(solution)/shard_map/ppermute | solution.py:90
  730.1 37.7 %collective-permute-start.95 = (bf16[1920,512]{1,0:T(8,128)(2,1)}, bf16[1920,512]{1,0:T(8,128)(2,1)}, u32[]{:S(2)}, u32[]{:S(2)}) collective-permute-start(bf16[1920,512]{1,0:T(8,128)(2,1)} %collective-permute-done.93.refs_1_), channel_id=1, source_target_pairs={{0,8},{8,0},{16,24},{24,16},{1,9},{9,1},{17,25},{25,17},{2,10},{10... | collective-permute-start | bytes 5898248 | tf_op jit(solution)/shard_map/ppermute | solution.py:90
  (160 other events, 2224.4 us)

commit v3 on v2

--- a/solution.py
+++ b/solution.py
@@ -90,19 +90,34 @@
     return lax.ppermute(block, axis, [(i, i ^ offset) for i in range(count)])
 
 
-def gather_relative(block, axis):
+def gather_relative(block, axis, last=()):
     pieces = [block]
     for bit in bits_down(lax.axis_size(axis)):
+        if bit == 1:
+            pieces[-1] = after(pieces[-1], *last)
         pieces = pieces + [swap(piece, axis, bit) for piece in pieces]
     return pieces
 
 
-def reduce_relative(pieces, axis):
+def reduce_relative(pieces, axis, last=()):
     for bit in reversed(bits_down(lax.axis_size(axis))):
         half = len(pieces) // 2
-        got = [swap(piece.astype(BF16), axis, bit) for piece in pieces[half:]]
+        given = [piece.astype(BF16) for piece in pieces[half:]]
+        if half == 1:
+            given = [after(given[0], *last)]
+        got = [swap(piece, axis, bit) for piece in given]
         pieces = [mine.astype(F32) + other.astype(F32) for mine, other in zip(pieces[:half], got)]
     return pieces[0]
+
+
+def reduce_halves(keep, give, axis):
+    bits = list(reversed(bits_down(lax.axis_size(axis))))
+    for bit in bits:
+        got = swap(give, axis, bit)
+        total = keep.astype(F32) + got.astype(F32)
+        half = total.shape[0] // 2
+        keep, give = total[:half], total[half:].astype(BF16)
+    return total
 
 
 def cycle_of(count):
@@ -273,22 +288,27 @@
     )(whole, whole, whole)
 
 
-def finish_model(early, middle, factor):
-    seqs, _, columns = early.shape
-
-    def body(early_ref, middle_ref, a_ref, b_ref):
-        a_ref[0] = middle_ref[0, :SPAN].astype(F32).T * factor
-        a_ref[1] = early_ref[0, :SPAN].astype(F32).T * factor
-        a_ref[2] = early_ref[0, SPAN : 2 * SPAN].astype(F32).T * factor
-        b_ref[0] = middle_ref[0, 2 * SPAN :].astype(F32) * factor
-        b_ref[1] = middle_ref[0, SPAN : 2 * SPAN].astype(F32) * factor
-        b_ref[2] = early_ref[0, 2 * SPAN :].astype(F32) * factor
-
-    spec = pl.BlockSpec((1, 3 * SPAN, columns), lambda s: (s, 0, 0))
+def finish_model(whole, factor):
+    seqs, _, columns = whole.shape
+
+    def body(shared_ref, heads_ref, a_ref, b_ref):
+        def rows(k):
+            return shared_ref[0, k * SPAN : (k + 1) * SPAN].astype(F32) * factor
+
+        a_ref[0] = rows(3).T
+        a_ref[1] = rows(0).T
+        a_ref[2] = rows(1).T
+        b_ref[0] = heads_ref[0].astype(F32) * factor
+        b_ref[1] = rows(4)
+        b_ref[2] = rows(2)
+
     return pl.pallas_call(
         body,
         grid=(seqs,),
-        in_specs=[spec, spec],
+        in_specs=[
+            pl.BlockSpec((1, 5 * SPAN, columns), lambda s: (s, 0, 0)),
+            pl.BlockSpec((1, SPAN, columns), lambda s: (s, 5, 0)),
+        ],
         out_specs=[
             pl.BlockSpec((3, columns, SPAN), lambda s: (1, s, 0)),
             pl.BlockSpec((3, SPAN, columns), lambda s: (0, 0, s)),
@@ -298,7 +318,7 @@
             jax.ShapeDtypeStruct((3, SPAN, MODEL_WIDTH), F32),
         ],
         name="finish_model",
-    )(early, middle)
+    )(whole, whole)
 
 
 def finish_late(late, a_all, factor):
@@ -385,26 +405,31 @@
 
 
 def backward_body(
-    blocks, slot_ref, qn_ref, kn_ref, vn_ref, do_ref, lse_ref, cos_ref, sin_ref, col_ref, row_ref,
-    dq_ref, dk_ref, dv_ref, dk_sum, dv_sum,
+    blocks, groups, slot_ref, qn_ref, kn_ref, vn_ref, do_ref, lse_ref, cos_ref, sin_ref, col_ref,
+    row_ref, out_ref, dk_sum, dv_sum,
 ):
     pairs_per_group = GROUP // 2
-    step = lax.rem(pl.program_id(0), pairs_per_group)
+    pair = pl.program_id(0)
+    step = lax.rem(pair, pairs_per_group)
+    two = 2 * HEAD_DIM
 
     @pl.when(step == 0)
     def _():
         dk_sum[...] = jnp.zeros_like(dk_sum)
         dv_sum[...] = jnp.zeros_like(dv_sum)
 
-    lane = lax.broadcasted_iota(jnp.int32, (QBLOCK, 2 * HEAD_DIM), 1)
-    row = lax.broadcasted_iota(jnp.int32, (2 * HEAD_DIM, QBLOCK), 0)
+    lane = lax.broadcasted_iota(jnp.int32, (QBLOCK, two), 1)
+    row = lax.broadcasted_iota(jnp.int32, (two, QBLOCK), 0)
+
+    def place(j):
+        return pl.ds(pl.multiple_of(slot_ref[j] * QBLOCK, QBLOCK), QBLOCK)
+
     for i in range(blocks):
         here = slice(i * QBLOCK, (i + 1) * QBLOCK)
-        there = pl.ds(pl.multiple_of(slot_ref[i] * QBLOCK, QBLOCK), QBLOCK)
         keys = (i + 1) * QBLOCK
         allowed = allowed_pairs(col_ref[...], row_ref[...], i)
         query = (qn_ref[here, :].astype(F32) * SCORE_SCALE).astype(BF16)
-        grad = do_ref[there, :]
+        grad = do_ref[place(i), :]
         outs = []
         for e in range(2):
             mine = jnp.where(lane // HEAD_DIM == e, query, jnp.zeros_like(query))
@@ -419,18 +444,28 @@
             outs.append(dot_tn(kn_ref[:keys, :], grad_scores))
         out = jnp.where(row < HEAD_DIM, outs[0], outs[1]).T * SCORE_SCALE
         out = out.astype(BF16).astype(F32)
-        dq_ref[there, :] = turn_tile(out, cos_ref[here, :], -sin_ref[here, :]).astype(BF16)
-
-    @pl.when(step == pairs_per_group - 1)
-    def _():
-        for j in range(blocks):
-            here = slice(j * QBLOCK, (j + 1) * QBLOCK)
-            there = pl.ds(pl.multiple_of(slot_ref[j] * QBLOCK, QBLOCK), QBLOCK)
-            dk = dk_sum[here, :]
-            dk = (dk + pltpu.roll(dk, HEAD_DIM, 1)).astype(BF16).astype(F32)
-            dk_ref[there, :] = turn_tile(dk, cos_ref[here, :], -sin_ref[here, :]).astype(BF16)
-            dv = dv_sum[here, :]
-            dv_ref[there, :] = (dv + pltpu.roll(dv, HEAD_DIM, 1)).astype(BF16)
+        out_ref[place(i), pl.ds(pl.multiple_of(pair * two, two), two)] = turn_tile(
+            out, cos_ref[here, :], -sin_ref[here, :]
+        ).astype(BF16)
+
+    width = groups * GROUP * HEAD_DIM
+    for g in range(groups):
+
+        @pl.when(pair == (g + 1) * pairs_per_group - 1)
+        def _(g=g):
+            for j in range(blocks):
+                here = slice(j * QBLOCK, (j + 1) * QBLOCK)
+                dk = dk_sum[here, :]
+                dk = (dk + pltpu.roll(dk, HEAD_DIM, 1)).astype(BF16).astype(F32)
+                dk = turn_tile(dk, cos_ref[here, :], -sin_ref[here, :]).astype(BF16)
+                dv = dv_sum[here, :]
+                dv = (dv + pltpu.roll(dv, HEAD_DIM, 1)).astype(BF16)
+                for base, values in ((width, dk), (width + groups * HEAD_DIM, dv)):
+                    first = base + g * HEAD_DIM
+                    tile = slice(first // two * two, first // two * two + two)
+                    half = first // HEAD_DIM % 2
+                    old = out_ref[place(j), tile]
+                    out_ref[place(j), tile] = jnp.where(lane // HEAD_DIM == half, values, old)
 
 
 def attention_specs():
@@ -478,27 +513,88 @@
     groups = key.shape[1] // (2 * HEAD_DIM)
     tile, group, lse, rest = attention_specs()
     blocks = PACK // QBLOCK
+    columns = pairs * 2 * HEAD_DIM + groups * 2 * HEAD_DIM
     return pl.pallas_call(
-        lambda *refs: backward_body(blocks, *refs),
+        lambda *refs: backward_body(blocks, groups, *refs),
         grid_spec=pltpu.PrefetchScalarGridSpec(
             num_scalar_prefetch=1,
             grid=(pairs,),
             in_specs=[tile, group, group, tile, lse] + rest,
-            out_specs=[tile, group, group],
+            out_specs=pl.BlockSpec((PACK, columns), lambda p, slot: (0, 0)),
             scratch_shapes=[pltpu.VMEM((PACK, 2 * HEAD_DIM), F32)] * 2,
         ),
-        out_shape=[
-            jax.ShapeDtypeStruct((PACK, pairs * 2 * HEAD_DIM), BF16),
-            jax.ShapeDtypeStruct((PACK, groups * 2 * HEAD_DIM), BF16),
-            jax.ShapeDtypeStruct((PACK, groups * 2 * HEAD_DIM), BF16),
-        ],
-        cost_estimate=pl.CostEstimate(
-            flops=10 * pairs * 2 * PACK * PACK * HEAD_DIM,
-            transcendentals=pairs * PACK * PACK,
-            bytes_accessed=8 * PACK * MODEL_WIDTH,
-        ),
+        out_shape=jax.ShapeDtypeStruct((PACK, columns), BF16),
+        cost_estimate=pl.CostEstimate(flops=0, transcendentals=0, bytes_accessed=0),
         name="attend_backward",
     )(slots, query, key, value, grad, log_totals, *tables)
+
+
+def tile_of(count):
+    return 256 if count % 256 == 0 else 128
+
+
+def gate_grads(grad_down, down, grad_low, first_down, gate, up):
+    tokens, units = gate.shape
+    tile = tile_of(units)
+
+    def body(gd_ref, down_ref, gl_ref, fd_ref, gate_ref, up_ref, gg_ref, gu_ref):
+        grad_act = dot_nt(gd_ref[...], down_ref[...]) + dot_nt(gl_ref[...], fd_ref[...])
+        gate_here = gate_ref[...]
+        share = jax.nn.sigmoid(gate_here)
+        gu_ref[...] = (grad_act * share * gate_here).astype(BF16)
+        gg_ref[...] = (
+            grad_act * up_ref[...] * share * (1.0 + gate_here * (1.0 - share))
+        ).astype(BF16)
+
+    def whole(array):
+        return pl.BlockSpec(array.shape, lambda t: (0, 0))
+
+    def rows(array):
+        return pl.BlockSpec((tile, array.shape[1]), lambda t: (t, 0))
+
+    cols = pl.BlockSpec((tokens, tile), lambda t: (0, t))
+    return pl.pallas_call(
+        body,
+        grid=(units // tile,),
+        in_specs=[whole(grad_down), rows(down), whole(grad_low), rows(first_down), cols, cols],
+        out_specs=[cols, cols],
+        out_shape=[jax.ShapeDtypeStruct((tokens, units), BF16)] * 2,
+        cost_estimate=pl.CostEstimate(
+            flops=2 * tokens * units * MODEL_WIDTH,
+            transcendentals=tokens * units,
+            bytes_accessed=12 * tokens * units + 2 * units * MODEL_WIDTH,
+        ),
+        name="gate_grads",
+    )(grad_down, down, grad_low, first_down, gate, up)
+
+
+def sum_products(lefts, rights):
+    tokens, outs = lefts[0].shape[0], rights[0].shape[0]
+    tile = tile_of(outs)
+    count = len(lefts)
+
+    def body(*refs):
+        total = dot_nt(refs[0][...], refs[count][...])
+        for k in range(1, count):
+            total = total + dot_nt(refs[k][...], refs[count + k][...])
+        refs[-2][...] = total[: tokens // 2].astype(BF16)
+        refs[-1][...] = total[tokens // 2 :].astype(BF16)
+
+    half = pl.BlockSpec((tokens // 2, tile), lambda t: (0, t))
+    return pl.pallas_call(
+        body,
+        grid=(outs // tile,),
+        in_specs=[pl.BlockSpec(a.shape, lambda t: (0, 0)) for a in lefts]
+        + [pl.BlockSpec((tile, b.shape[1]), lambda t: (t, 0)) for b in rights],
+        out_specs=[half, half],
+        out_shape=[jax.ShapeDtypeStruct((tokens // 2, outs), BF16)] * 2,
+        cost_estimate=pl.CostEstimate(
+            flops=sum(2 * tokens * outs * a.shape[1] for a in lefts),
+            transcendentals=0,
+            bytes_accessed=2 * sum(a.size for a in [*lefts, *rights]) + 2 * tokens * outs,
+        ),
+        name="sum_products",
+    )(*lefts, *rights)
 
 
 def reverse_bits(value, count):
@@ -509,27 +605,35 @@
     return out
 
 
+def scatter_step(total, bit):
+    half = total.shape[0] // 2
+    high = ((lax.axis_index("fsdp") & bit) != 0).astype(jnp.int32)
+    keep = lax.dynamic_slice_in_dim(total, high * half, half, 0)
+    give = lax.dynamic_slice_in_dim(total, (1 - high) * half, half, 0)
+    got = swap(give, "fsdp", bit)
+    return (keep.astype(F32) + got.astype(F32)).astype(BF16)
+
+
 def reduce_scatter_rows(total):
-    count = lax.axis_size("fsdp")
-    me = lax.axis_index("fsdp")
-    for bit in reversed(bits_down(count)):
-        half = total.shape[0] // 2
-        high = ((me & bit) != 0).astype(jnp.int32)
-        keep = lax.dynamic_slice_in_dim(total, high * half, half, 0)
-        give = lax.dynamic_slice_in_dim(total, (1 - high) * half, half, 0)
-        got = swap(give.astype(BF16), "fsdp", bit)
-        total = (keep.astype(F32) + got.astype(F32)).astype(BF16)
+    for bit in reversed(bits_down(lax.axis_size("fsdp"))):
+        total = scatter_step(total, bit)
     return total
 
 
-def share_out(total):
+def widen(piece, bit):
+    return jnp.concatenate([piece, swap(piece, "fsdp", bit)], axis=0)
+
+
+def share_out(piece):
+    for bit in bits_down(lax.axis_size("fsdp")):
+        piece = widen(piece, bit)
+    return piece
+
+
+def settle(pieces):
     count, seqs = lax.axis_size("fsdp"), lax.axis_size("seq")
     me, me_seq = lax.axis_index("fsdp"), lax.axis_index("seq")
-    rows, columns = total.shape
-    piece = reduce_scatter_rows(total.astype(BF16))
-    for bit in bits_down(count):
-        piece = jnp.concatenate([piece, swap(piece, "fsdp", bit)], axis=0)
-    pieces = gather_relative(piece, "seq")
+    rows, columns = pieces[0].shape
     targets = jnp.stack(
         [
             (me_seq ^ s) * count + reverse_bits(me ^ o, count)
@@ -605,8 +709,8 @@
         ],
         axis=1,
     )
+    gate_share, up_share = take_units([gate_matrix, up_matrix], me, seqs, fsdps, unit_block)
     out_share = columns_of(output_matrix, me, width)
-    gate_share, up_share = take_units([gate_matrix, up_matrix], me, seqs, fsdps, unit_block)
     down_share = lax.dynamic_slice_in_dim(down_matrix, me * unit_block, unit_block, 0)
     half_block = unit_block // 2
     lists = rings.gather(
@@ -618,13 +722,10 @@
             down_share[:half_block],
             down_share[half_block:],
         ],
-        [0, 0, 3, 4, 7, 7],
+        [0, 0, 2, 3, 5, 6],
     )
     qkv_mine, out_mine, gate_full, up_full = (
         place_blocks(blocks, 1, rings.owner) for blocks in lists[:4]
-    )
-    down_full = place_blocks(
-        lists[4] + lists[5], 1, jnp.concatenate([rings.owner * 2, rings.owner * 2 + 1])
     )
 
     segment, position, valid_row, onehot = pack_tables(
@@ -672,9 +773,9 @@
     first_qkv = jnp.concatenate([adapter_first_factors[k] for k in range(3)], axis=1)
     low_qkv = (mm(normed_one, first_qkv) * mask_rel_three).astype(BF16)
     low_q, low_k, low_v = (low_qkv[:, k * SPAN : (k + 1) * SPAN] for k in range(3))
-    second_q = [columns_of(adapter_second_model[0], peer, width) for peer in peers]
-    second_k = [columns_of(adapter_second_keyvalue[0], peer, kv_width) for peer in peers]
-    second_v = [columns_of(adapter_second_keyvalue[1], peer, kv_width) for peer in peers]
+    second_q = [columns_of(adapter_second_model[0], me, width)]
+    second_k = [columns_of(adapter_second_keyvalue[0], me, kv_width)]
+    second_v = [columns_of(adapter_second_keyvalue[1], me, kv_width)]
 
     def twice(rows):
         heads = [rows[:, g * HEAD_DIM : (g + 1) * HEAD_DIM] for g in range(my_groups)]
@@ -713,36 +814,45 @@
         return jax.nn.sigmoid(gate_arg) * gate_arg * up_arg
 
     act = swiglu(gate, up).astype(BF16)
+    down_full = place_blocks(
+        lists[4] + lists[5], 1, jnp.concatenate([rings.owner * 2, rings.owner * 2 + 1])
+    )
     first_down = lax.dynamic_index_in_dim(
         adapter_first_down.reshape(fsdps, seqs, unit_block, SPAN), me, 1, keepdims=False
     ).reshape(units, SPAN)
     grad_out = cotangent[0].astype(F32) * valid_col
     grad_down = (RESIDUAL_FACTOR * (cot_all.astype(F32) * valid_rel)).astype(BF16)
     grad_low_d = mm_nt(grad_down, adapter_second_model[2]).astype(BF16) * mask_rel
-    grad_act = mm_nt(grad_down, down_full) + mm_nt(grad_low_d, first_down)
-    _, swiglu_back = jax.vjp(swiglu, gate, up)
-    grad_gate, grad_up = swiglu_back(grad_act)
-    grad_gate, grad_up = grad_gate.astype(BF16), grad_up.astype(BF16)
+    grad_gate, grad_up = gate_grads(grad_down, down_full, grad_low_d, first_down, gate, up)
     grad_low_ffn = (
         jnp.concatenate([mm_nt(grad_gate, second_gate), mm_nt(grad_up, second_up)], axis=1).astype(
             BF16
         )
         * mask_rel_two
     )
-    grad_normed_two = (
-        mm_nt(grad_gate, gate_full) + mm_nt(grad_up, up_full) + mm_nt(grad_low_ffn, first_ffn)
-    )
-    act, grad_gate, grad_up = after((act, grad_gate, grad_up), grad_normed_two)
-    grad_normed_two = reduce_relative(blocks_of(grad_normed_two), "seq")
+    keep, give = sum_products(
+        [grad_gate, grad_up, grad_low_ffn], [gate_full, up_full, first_ffn]
+    )
+    act, late_gate, late_up = after((act, grad_gate, grad_up), give)
+    grad_normed_two = reduce_halves(keep, give, "seq")
+    grad_a_down = mm_tn(grad_low_d, act)
+    grad_b_gate = mm_tn(low_g, late_gate)
+    grad_b_up = mm_tn(low_u, late_up)
+
+    def split_units(rows):
+        return [rows[:, k * width : (k + 1) * width].astype(BF16) for k in range(parts)]
+
+    unit_grads = jnp.concatenate(
+        split_units(grad_a_down) + split_units(grad_b_gate) + split_units(grad_b_up), axis=0
+    )
+    act = after(act, unit_grads)
+    unit_bits = list(reversed(bits_down(fsdps)))
+    unit_sums = scatter_step(unit_grads, unit_bits[0])
+    grad_normed_two, unit_sums = after((grad_normed_two, unit_sums))
+    unit_sums = scatter_step(unit_sums, unit_bits[1])
     low_d = (mm(act, first_down) * mask_rel).astype(BF16)
     down_part = mm(act, down_full) + mm(low_d, adapter_second_model[2])
-    down_sum = reduce_relative(blocks_of(down_part), "seq")
-    layer_out = (valid_col * (hidden_mid + RESIDUAL_FACTOR * down_sum)).astype(BF16)
-
     grad_b_down = mm_tn(low_d, grad_down)
-    grad_a_down = mm_tn(grad_low_d, act)
-    grad_b_gate = mm_tn(low_g, grad_gate)
-    grad_b_up = mm_tn(low_u, grad_up)
     grad_a_ffn = mm_tn(grad_low_ffn, normed_two)
     _, norm_two_back = jax.vjp(lambda hidden: rms_norm(hidden, feedfwd_norm_gain), hidden_mid)
     grad_mid = grad_out + norm_two_back(grad_normed_two)[0]
@@ -751,98 +861,101 @@
     grad_low_o = mm_nt(grad_branch, adapter_second_model[1]).astype(BF16) * mask_own
     grad_b_out = mm_tn(low_o, grad_branch)
     grad_a_out = mm_tn(grad_low_o, attn_own)
-    grad_attn = mm_nt(grad_low_o, adapter_first_factors[3])
-    for peer, piece in zip(peers, out_weights):
-        grad_attn = grad_attn + mm_nt(columns_of(grad_branch, peer, width), piece)
+    grad_attn = mm_nt(grad_low_o, adapter_first_factors[3]) + mm_nt(
+        jnp.concatenate([columns_of(grad_branch, peer, width) for peer in peers], axis=1),
+        jnp.concatenate(out_weights, axis=1),
+    )
     grad_attn = grad_attn.astype(BF16)
     grad_heads = jnp.concatenate(
         exchange([columns_of(grad_attn, peer, width) for peer in peers]), axis=0
     )
-    grad_query, grad_key, grad_value = (
-        from_kernel(g)
-        for g in attend_backward(slots, saved, to_kernel(grad_heads), log_totals, tables)
-    )
-
-    def once(rows):
-        return jnp.concatenate(
-            [rows[:, 2 * g * HEAD_DIM : (2 * g + 1) * HEAD_DIM] for g in range(my_groups)], axis=1
-        )
-
-    grad_key, grad_value = once(grad_key), once(grad_value)
-    grad_qkv = jnp.concatenate([grad_query, grad_key, grad_value], axis=1)
-    grad_pieces = exchange(blocks_of(grad_qkv))
-    qkv_weights = gather_relative(qkv_mine, "seq")
+    grad_heads, unit_sums = after((grad_heads, unit_sums))
+    for bit in unit_bits[2:]:
+        unit_sums = scatter_step(unit_sums, bit)
+    down_sum = reduce_relative(blocks_of(down_part), "seq", [grad_heads])
+    shared_terms = jnp.concatenate([grad_a_ffn, grad_b_down, grad_a_out, grad_b_out], axis=0)
+    shared_sum = reduce_relative(
+        [columns_of(shared_terms, peer, width) for peer in peers], "seq", [grad_heads]
+    ).astype(BF16)
+    grad_qkv = from_kernel(
+        attend_backward(slots, saved, to_kernel(grad_heads), log_totals, tables)
+    )
+    grad_qkv, unit_sums = after((grad_qkv, unit_sums), shared_sum, down_sum)
+    grad_query = grad_qkv[:, :width]
+    grad_key = grad_qkv[:, width : width + kv_width]
+    grad_value = grad_qkv[:, width + kv_width :]
+    low_part = jnp.concatenate(
+        [
+            mm_nt(grad_query, second_q[0]),
+            mm_nt(grad_key, second_k[0]),
+            mm_nt(grad_value, second_v[0]),
+        ],
+        axis=1,
+    ).astype(BF16)
+    grad_low_qkv = reduce_halves(low_part[: PACK // 2], low_part[PACK // 2 :], "seq")
+    grad_low_qkv = grad_low_qkv.astype(BF16) * mask_own_three
+    wide_bits = bits_down(fsdps)
+    unit_sums = widen(unit_sums, wide_bits[0])
+    grad_low_qkv, unit_sums = after((grad_low_qkv, unit_sums))
+    grad_low_all = jnp.concatenate(gather_relative(grad_low_qkv, "seq"), axis=0)
+    for bit in wide_bits[1:-1]:
+        unit_sums = widen(unit_sums, bit)
+    grad_low_all, unit_sums = after((grad_low_all, unit_sums))
+    grad_a_qkv = mm_tn(grad_low_all, columns_of(normed_one, me, width))
     grad_b_q = mm_tn(low_q, grad_query)
     grad_b_kv = [mm_tn(low_k, grad_key), mm_tn(low_v, grad_value)]
-    low_grads = [jnp.zeros((row_count, SPAN), F32)] * 3
-    for k in range(seqs):
-        piece = grad_pieces[k]
-        low_grads = [
-            low_grads[0] + mm_nt(piece[:, :width], second_q[k]),
-            low_grads[1] + mm_nt(piece[:, width : width + kv_width], second_k[k]),
-            low_grads[2] + mm_nt(piece[:, width + kv_width :], second_v[k]),
-        ]
-    grad_low_qkv = jnp.concatenate(low_grads, axis=1).astype(BF16) * mask_own_three
-    grad_low_all = jnp.concatenate(gather_relative(grad_low_qkv, "seq"), axis=0)
-    grad_a_qkv = mm_tn(grad_low_all, columns_of(normed_one, me, width))
-    grad_normed_one = mm_nt(grad_low_qkv, first_qkv)
-    for k in range(seqs):
-        grad_normed_one = grad_normed_one + mm_nt(grad_pieces[k], qkv_weights[k])
+    keep_one, give_one = sum_products([grad_qkv], [qkv_mine])
+    grad_normed_one = reduce_halves(keep_one, after(give_one, grad_low_all), "seq")
+    grad_normed_one = grad_normed_one + mm_nt(grad_low_qkv, first_qkv)
+    layer_out = (valid_col * (hidden_mid + RESIDUAL_FACTOR * down_sum)).astype(BF16)
     _, norm_one_back = jax.vjp(lambda hidden: rms_norm(hidden, attention_norm_gain), hidden_in)
     grad_input = (grad_mid + norm_one_back(grad_normed_one)[0]).astype(BF16)
 
     factor = ADAPTER_TOTAL / math.sqrt(PACK * fsdps)
-
-    def split_units(rows):
-        return [rows[:, k * width : (k + 1) * width].astype(BF16) for k in range(parts)]
-
-    def seq_share(rows):
-        return reduce_relative(
-            [columns_of(rows, peer, width) for peer in peers], "seq"
-        ).astype(BF16)
 
     def units_out(whole, first):
         part = whole[:, first : first + parts * SPAN]
         part = part.reshape(seqs, parts, SPAN, fsdps // parts, unit_block)
         return part.transpose(2, 1, 3, 0, 4).reshape(SPAN, feed_units)
 
-    early = share_out(
-        jnp.concatenate(
-            [seq_share(jnp.concatenate([grad_a_ffn, grad_b_down], axis=0))]
-            + split_units(grad_a_down)
-            + split_units(grad_b_gate)
-            + split_units(grad_b_up),
-            axis=0,
+    late_sums = scatter_step(grad_a_qkv.astype(BF16), unit_bits[0])
+    unit_sums = widen(unit_sums, wide_bits[-1])
+    late_sums, unit_sums = after((late_sums, unit_sums), grad_normed_one)
+    for bit in unit_bits[1:]:
+        late_sums = scatter_step(late_sums, bit)
+    unit_pieces = gather_relative(unit_sums, "seq")
+    early = settle(unit_pieces)
+    blank = jnp.zeros((SPAN, width - 2 * kv_width), BF16)
+    middle_sums = share_out(
+        reduce_scatter_rows(
+            jnp.concatenate(
+                [
+                    shared_sum,
+                    grad_b_q.astype(BF16),
+                    jnp.concatenate([g.astype(BF16) for g in grad_b_kv] + [blank], axis=1),
+                ],
+                axis=0,
+            )
         )
     )
-    blank = jnp.zeros((SPAN, width - 2 * kv_width), BF16)
-    middle = share_out(
-        jnp.concatenate(
-            [
-                seq_share(jnp.concatenate([grad_a_out, grad_b_out], axis=0)),
-                grad_b_q.astype(BF16),
-                jnp.concatenate([g.astype(BF16) for g in grad_b_kv] + [blank], axis=1),
-            ],
-            axis=0,
-        )
-    )
-    late = share_out(grad_a_qkv)
-
     def scaled(array):
         return array.astype(F32) * factor
 
-    base = 3 * SPAN
-    b_kv = middle[:, 3 * SPAN :, : 2 * kv_width].reshape(seqs, SPAN, 2, kv_width)
     if unit_block % 128 == 0:
-        a_down, b_ffn = finish_units(early, base, parts, fsdps, unit_block, factor)
+        a_down, b_ffn = finish_units(early, 0, parts, fsdps, unit_block, factor)
     else:
-        a_down = scaled(units_out(early, base).T)
+        a_down = scaled(units_out(early, 0).T)
         b_ffn = scaled(
             jnp.stack(
-                [units_out(early, base + parts * SPAN), units_out(early, base + 2 * parts * SPAN)]
+                [units_out(early, parts * SPAN), units_out(early, 2 * parts * SPAN)]
             )
         )
-    a_all, b_model = finish_model(early, middle, factor)
+    middle_pieces = gather_relative(middle_sums, "seq", [a_down])
+    middle = settle(middle_pieces)
+    b_kv = middle[:, 6 * SPAN :, : 2 * kv_width].reshape(seqs, SPAN, 2, kv_width)
+    a_all, b_model = finish_model(middle, factor)
+    late_sums = share_out(late_sums)
+    late = settle(gather_relative(late_sums, "seq", [b_model]))
     return (
         layer_out[None],
         grad_input[None],

time: 805 us -> 785 us (0.975)
  matrix products: 189 us -> 123 us
  Pallas kernels: 119 us -> 174 us
  starting transfers between devices: 105 us -> 89.6 us
  waiting for transfers between devices: 262 us -> 274 us
  local copies, waits for them, and re-layouts: 68.8 us -> 60.5 us
    dot_general x31 -> x10, matrix products: 96.2 us -> 21.3 us  [mm_nt(): lax.dot_general(left, right, (((1,), (1,)), ((), ())), preferred_element_...]
    pallas_call x2 -> x5, Pallas kernels: 29.6 us -> 84 us  [the longest x2 34.5 us: sum_products(): pl.pallas_call(body, grid=(outs // tile,), in_specs=[pl.BlockSpec(a.shape...]
    ppermute x42, waiting for transfers between devices: 104 us -> 148 us  [send(): got = lax.ppermute(block, 'fsdp', self.perms[way])]
    ppermute x66 -> x60, waiting for transfers between devices: 159 us -> 126 us  [swap(): return lax.ppermute(block, axis, [(i, i ^ offset) for i in range(count)])]
    ppermute x42, starting transfers between devices: 59.4 us -> 48.5 us  [send(): got = lax.ppermute(block, 'fsdp', self.perms[way])]
    ppermute x66 -> x60, starting transfers between devices: 45.6 us -> 41.1 us  [swap(): return lax.ppermute(block, axis, [(i, i ^ offset) for i in range(count)])]
  transfers between devices with their start and end apart: 108 -> 102, of which waited for: 39 -> 42; matrix products, arithmetic and copies ran while one was open for 37% -> 21% of each run, Pallas kernels for 12% -> 16%
where the time goes in v3:
time: 785 us; the launch traced here: 777 us
  waiting for transfers between devices  274 us (35%)
  Pallas kernels  174 us (22%)
  matrix products  123 us (16%)
  starting transfers between devices  89.6 us (11%)
  local copies, waits for them, and re-layouts  60.5 us (8%)
  other arithmetic  52.5 us (7%)
    ppermute x42, waiting for transfers between devices, send(): got = lax.ppermute(block, 'fsdp', self.perms[way])  148 us
    ppermute x60, waiting for transfers between devices, swap(): return lax.ppermute(block, axis, [(i, i ^ offset) for i in range(count)])  126 us
    dot_general x19, matrix products, mm(): return jnp.dot(left, right, preferred_element_type=F32)  85.1 us
    ppermute x42, starting transfers between devices, send(): got = lax.ppermute(block, 'fsdp', self.perms[way])  48.5 us
    pallas_call x8, Pallas kernels, place_blocks(): pl.pallas_call(body, out_shape=jax.ShapeDtypeStruct((rows * total, column...  42.3 us
    ppermute x60, starting transfers between devices, swap(): return lax.ppermute(block, axis, [(i, i ^ offset) for i in range(count)])  41.1 us
    pallas_call x2, Pallas kernels, sum_products(): pl.pallas_call(body, grid=(outs // tile,), in_specs=[pl.BlockSpec(a.shape...  34.5 us
    pallas_call x1, Pallas kernels, attend_backward(): pl.pallas_call(lambda *refs: backward_body(blocks, groups, *refs), grid_s...  24.9 us
  transfers between devices with their start and end apart: 102, of which 42 were waited for; matrix products, arithmetic and copies ran while one was open for 21% of the time, Pallas kernels for 16%

profile of v3, /device:TPU:0, one launch (start us, length us, event | category | flops | bytes accessed | tf_op | source)
XLA Modules:
  0.0 776.9 jit_solution(15772920634372903557)
XLA Ops:
  24.9 7.2 collective-permute-done.9.refs_6_
  40.4 5.9 take_units.2
  113.9 23.1 %attend_forward.1 = (bf16[1024,512]{1,0:T(8,128)(2,1)}, bf16[1024,256]{1,0:T(8,128)(2,1)}, bf16[1024,256]{1,0:T(8,128)(2,1)}, bf16[1024,512]{1,0:T(8,128)(2,1)}, f32[4,2,1024]{2,1,0:T(2,128)}) custom-call(s32[4]{0:T(128)} %pad_add_fusion.refs_0_, f32[1024,512]{1,0:T(8,128)} %slice_add_fusion.4.refs_1_, f32[1024,256]{1,0:T(8,128)} %pad_maximum_fusion.5.refs_2_, ...), custom_call_target="tpu_custom_call" | custom-call | flops 2147483648 | bytes 16777216 | tf_op jit(solution)/shard_map/attend_forward/pallas_call | solution.py:486
  142.1 4.6 collective-permute-done.12
  150.0 13.8 %collective-permute-done.36.refs_7_ = bf16[256,2048]{1,0:T(8,128)(2,1)} collective-permute-done((bf16[256,2048]{1,0:T(8,128)(2,1)S(1)}, bf16[256,2048]{1,0:T(8,128)(2,1)}, u32[]{:S(2)}, u32[]{:S(2)}) %collective-permute-start.36) | collective-permute-done | bytes 1048608 | tf_op jit(solution)/shard_map/ppermute | solution.py:149
  163.9 8.9 %collective-permute-done.29.refs_1_ = bf16[256,2048]{1,0:T(8,128)(2,1)} collective-permute-done((bf16[256,2048]{1,0:T(8,128)(2,1)S(1)}, bf16[256,2048]{1,0:T(8,128)(2,1)}, u32[]{:S(2)}, u32[]{:S(2)}) %collective-permute-start.29) | collective-permute-done | bytes 1048608 | tf_op jit(solution)/shard_map/ppermute | solution.py:149
  175.6 19.7 %collective-permute-done.28.refs_3_ = bf16[256,2048]{1,0:T(8,128)(2,1)} collective-permute-done((bf16[256,2048]{1,0:T(8,128)(2,1)}, bf16[256,2048]{1,0:T(8,128)(2,1)}, u32[]{:S(2)}, u32[]{:S(2)}) %collective-permute-start.28) | collective-permute-done | bytes 1048608 | tf_op jit(solution)/shard_map/ppermute | solution.py:149
  205.0 12.7 %collective-permute-done.34.refs_2_ = bf16[256,2048]{1,0:T(8,128)(2,1)} collective-permute-done((bf16[256,2048]{1,0:T(8,128)(2,1)}, bf16[256,2048]{1,0:T(8,128)(2,1)}, u32[]{:S(2)}, u32[]{:S(2)}) %collective-permute-start.34) | collective-permute-done | bytes 1048608 | tf_op jit(solution)/shard_map/ppermute | solution.py:149
  231.5 16.6 %collective-permute-done.48.refs_7_ = bf16[128,2048]{1,0:T(8,128)(2,1)S(1)} collective-permute-done((bf16[128,2048]{1,0:T(8,128)(2,1)S(1)}, bf16[128,2048]{1,0:T(8,128)(2,1)S(1)}, u32[]{:S(2)}, u32[]{:S(2)}) %collective-permute-start.48) | collective-permute-done | bytes 524320 | tf_op jit(solution)/shard_map/ppermute | solution.py:149
  259.5 6.7 collective-permute-done.53.refs_15_
  269.0 5.7 collective-permute-done.35.refs_3_
  276.4 20.6 %collective-permute-done.49.refs_6_ = bf16[128,2048]{1,0:T(8,128)(2,1)} collective-permute-done((bf16[128,2048]{1,0:T(8,128)(2,1)S(1)}, bf16[128,2048]{1,0:T(8,128)(2,1)}, u32[]{:S(2)}, u32[]{:S(2)}) %collective-permute-start.49) | collective-permute-done | bytes 524320 | tf_op jit(solution)/shard_map/ppermute | solution.py:149
  299.4 6.8 collective-permute-done.46.refs_9_
  306.8 7.0 collective-permute-done.45.refs_3_
  328.2 5.3 take_units.3
  345.6 7.1 place_blocks.10.refs_3_
  352.7 7.2 place_blocks.11.refs_4_
  360.6 7.3 place_blocks.12.down_ref
  372.7 4.5 fusion.52
  377.1 14.5 %convolution_add_fusion.2.gate_ref = f32[1024,2048]{1,0:T(8,128)} fusion(f32[1024,2048]{1,0:T(8,128)S(1)} %fusion.55, bf16[2048,2048]{1,0:T(8,128)(2,1)} %place_blocks.10.refs_3_, bf16[256,2048]{1,0:T(8,128)(2,1)} %collective-permute-done.25, bf16[256,2048]{1,0:T(8,128)(2,1)} %collective-permute-done.24, bf16[256,2048]{1,0:T(8,128)(2,1)} %collective-permute-done.23, ...), kind=kOutput, calls=%fused_computation.22 | convolution fusion | flops 8608808960 | bytes 29360128 | tf_op jit(solution)/shard_map/dot_general | solution.py:32
  391.6 20.2 %multiply_convert_fusion.1 = (bf16[1024,2048]{1,0:T(8,128)(2,1)}, f32[1024,2048]{1,0:T(8,128)}) fusion(f32[1024,2048]{1,0:T(8,128)} %convolution_add_fusion.2.gate_ref, f32[1024,2048]{1,0:T(8,128)} %fusion.52, bf16[2048,2048]{1,0:T(8,128)(2,1)} %place_blocks.11.refs_4_, bf16[256,2048]{1,0:T(8,128)(2,1)} %collective-permute-done.25, ...), kind=kOutput, calls=%fused_computation.9 | convolution fusion | flops 8621391872 | bytes 41943040 | tf_op jit(solution)/shard_map/dot_general | solution.py:32
  411.8 19.4 %gate_grads.1 = (bf16[1024,2048]{1,0:T(8,128)(2,1)}, bf16[1024,2048]{1,0:T(8,128)(2,1)}) custom-call(bf16[1024,2048]{1,0:T(8,128)(2,1)} %copy-done.6, bf16[2048,2048]{1,0:T(8,128)(2,1)} %place_blocks.12.down_ref, bf16[1024,128]{1,0:T(8,128)(2,1)} %fusion.27.gl_ref, bf16[2048,128]{1,0:T(8,128)(2,1)} %bitcast.187, ...), custom_call_target="tpu_custom_call" | custom-call | flops 8589934592 | bytes 33554432 | tf_op jit(solution)/shard_map/gate_grads/pallas_call | solution.py:556
  437.0 25.7 %sum_products.2 = (bf16[512,2048]{1,0:T(8,128)(2,1)}, bf16[512,2048]{1,0:T(8,128)(2,1)}) custom-call(bf16[1024,2048]{1,0:T(8,128)(2,1)} %get-tuple-element.124.refs_0_, bf16[1024,2048]{1,0:T(8,128)(2,1)} %get-tuple-element.125.refs_1_, bf16[1024,256]{1,0:T(8,128)(2,1)} %bitcast_multiply_fusion.refs_2_, bf16[2048,2048]{1,0:T(8,128)(2,1)} %place_blocks.10.refs_3_, ...), custom_call_target="tpu_custom_call" | custom-call | flops 18253611008 | bytes 30932992 | tf_op jit(solution)/shard_map/sum_products/pallas_call | solution.py:584
  475.3 13.5 %fusion.125 = (bf16[1024,2048]{1,0:T(8,128)(2,1)}, f32[1024,2048]{1,0:T(8,128)}) fusion(f32[1024,2048]{1,0:T(8,128)S(1)} %fusion.43, bf16[1024,2048]{1,0:T(8,128)(2,1)} %get-tuple-element.126, bf16[2048,2048]{1,0:T(8,128)(2,1)S(1)} %bitcast.177), kind=kOutput, calls=%fused_computation.275 | convolution fusion | flops 8594128896 | bytes 33554432 | tf_op jit(solution)/shard_map/dot_general | solution.py:32
  498.9 12.8 %collective-permute-done.61 = bf16[768,512]{1,0:T(8,128)(2,1)S(1)} collective-permute-done((bf16[768,512]{1,0:T(8,128)(2,1)S(1)}, bf16[768,512]{1,0:T(8,128)(2,1)S(1)}, u32[]{:S(2)}, u32[]{:S(2)}) %collective-permute-start.61) | collective-permute-done | bytes 786464 | tf_op jit(solution)/shard_map/ppermute | solution.py:90
  511.9 6.4 collective-permute-done.60
  525.9 4.8 fusion.12
  538.0 4.5 fusion.23
  551.4 24.9 %attend_backward.1.refs_0_ = bf16[1024,768]{1,0:T(8,128)(2,1)} custom-call(s32[4]{0:T(128)} %pad_add_fusion.refs_0_, bf16[1024,512]{1,0:T(8,128)(2,1)} %get-tuple-element.132.refs_1_, bf16[1024,256]{1,0:T(8,128)(2,1)} %get-tuple-element.133.refs_2_, bf16[1024,256]{1,0:T(8,128)(2,1)} %get-tuple-element.134.refs_3_, ...), custom_call_target="tpu_custom_call" | custom-call | tf_op jit(solution)/shard_map/attend_backward/pallas_call | solution.py:517
  576.4 8.6 %collective-permute-done.70 = bf16[640,512]{1,0:T(8,128)(2,1)} collective-permute-done((bf16[640,512]{1,0:T(8,128)(2,1)}, bf16[640,512]{1,0:T(8,128)(2,1)}, u32[]{:S(2)}, u32[]{:S(2)}) %collective-permute-start.70) | collective-permute-done | bytes 655392 | tf_op jit(solution)/shard_map/ppermute | solution.py:90
  599.1 8.4 %collective-permute-done.73 = bf16[192,512]{1,0:T(8,128)(2,1)S(1)} collective-permute-done((bf16[192,512]{1,0:T(8,128)(2,1)S(1)}, bf16[192,512]{1,0:T(8,128)(2,1)S(1)}, u32[]{:S(2)}, u32[]{:S(2)}) %collective-permute-start.73) | collective-permute-done | bytes 196640 | tf_op jit(solution)/shard_map/ppermute | solution.py:90
  609.0 5.4 collective-permute-done.74
  614.4 8.7 %sum_products.3 = (bf16[512,2048]{1,0:T(8,128)(2,1)}, bf16[512,2048]{1,0:T(8,128)(2,1)}) custom-call(bf16[1024,768]{1,0:T(8,128)(2,1)} %attend_backward.1.refs_0_, bf16[2048,768]{1,0:T(8,128)(2,1)} %place_blocks.8.refs_1_), custom_call_target="tpu_custom_call" | custom-call | flops 3221225472 | bytes 8912896 | tf_op jit(solution)/shard_map/sum_products/pallas_call | solution.py:584
  638.4 4.1 collective-permute-done.88
  642.7 20.2 %collective-permute-done.80 = bf16[192,512]{1,0:T(8,128)(2,1)S(1)} collective-permute-done((bf16[192,512]{1,0:T(8,128)(2,1)S(1)}, bf16[192,512]{1,0:T(8,128)(2,1)S(1)}, u32[]{:S(2)}, u32[]{:S(2)}) %collective-permute-start.80) | collective-permute-done | bytes 196640 | tf_op jit(solution)/shard_map/ppermute | solution.py:90
  668.3 6.6 collective-permute-done.89
  676.7 5.2 collective-permute-done.90
  682.5 6.4 collective-permute-done.91
  689.4 5.6 collective-permute-done.92
  697.8 5.4 collective-permute-done.95.refs_1_
  715.2 5.9 collective-permute-done.83
  721.2 5.0 collective-permute-done.84
  727.1 6.3 place_blocks.13
  733.4 9.2 %finish_units.1 = (f32[8192,128]{1,0:T(8,128)}, f32[2,128,8192]{2,1,0:T(8,128)}) custom-call(bf16[4,1536,512]{2,1,0:T(8,128)(2,1)} %bitcast.170, bf16[4,1536,512]{2,1,0:T(8,128)(2,1)} %bitcast.171, bf16[4,1536,512]{2,1,0:T(8,128)(2,1)} %bitcast.172), custom_call_target="tpu_custom_call" | custom-call | tf_op jit(solution)/shard_map/finish_units/pallas_call | solution.py:275
  744.8 5.3 collective-permute-done.86
  751.3 4.7 place_blocks.14
  756.0 5.3 finish_model.1
  772.4 4.3 finish_late.1
  (558 shorter events, 306.1 us)
Async XLA Ops:
  11.7 35.4 %collective-permute-start = (bf16[256,2048]{1,0:T(8,128)(2,1)}, bf16[256,2048]{1,0:T(8,128)(2,1)}, u32[]{:S(2)}, u32[]{:S(2)}) collective-permute-start(bf16[256,2048]{1,0:T(8,128)(2,1)} %fusion.20), channel_id=1, source_target_pairs={{0,16},{8,24},{16,0},{24,8},{1,17},{9,25},{17,1},{25,9},{2,18},{10... | collective-permute-start | bytes 3145736 | tf_op jit(solution)/shard_map/ppermute | solution.py:90
  47.1 51.2 %collective-permute-start.1 = (bf16[256,2048]{1,0:T(8,128)(2,1)}, bf16[256,2048]{1,0:T(8,128)(2,1)}, u32[]{:S(2)}, u32[]{:S(2)}) collective-permute-start(bf16[256,2048]{1,0:T(8,128)(2,1)} %fusion.20), channel_id=1, source_target_pairs={{0,8},{8,0},{16,24},{24,16},{1,9},{9,1},{17,25},{25,17},{2,10},{10... | collective-permute-start | bytes 3145736 | tf_op jit(solution)/shard_map/ppermute | solution.py:90
  47.2 48.8 %collective-permute-start.26 = (bf16[256,2048]{1,0:T(8,128)(2,1)}, bf16[256,2048]{1,0:T(8,128)(2,1)}, u32[]{:S(2)}, u32[]{:S(2)}) collective-permute-start(bf16[256,2048]{1,0:T(8,128)(2,1)} %get-tuple-element.97.refs_0_), channel_id=1, source_target_pairs={{0,2},{2,4},{4,6},{6,7},{7,5},{5,3},{3,1},{1,0},{8,10},{10,12},{12... | collective-permute-start | bytes 3145736 | tf_op jit(solution)/shard_map/ppermute | solution.py:149
  50.3 46.4 %collective-permute-start.31 = (bf16[256,2048]{1,0:T(8,128)(2,1)}, bf16[256,2048]{1,0:T(8,128)(2,1)}, u32[]{:S(2)}, u32[]{:S(2)}) collective-permute-start(bf16[256,2048]{1,0:T(8,128)(2,1)} %get-tuple-element.97.refs_0_), channel_id=1, source_target_pairs={{2,0},{4,2},{6,4},{7,6},{5,7},{3,5},{1,3},{0,1},{10,8},{12,10},{14... | collective-permute-start | bytes 3145736 | tf_op jit(solution)/shard_map/ppermute | solution.py:149
  50.6 47.7 %collective-permute-start.2 = (bf16[256,2048]{1,0:T(8,128)(2,1)}, bf16[256,2048]{1,0:T(8,128)(2,1)}, u32[]{:S(2)}, u32[]{:S(2)}) collective-permute-start(bf16[256,2048]{1,0:T(8,128)(2,1)} %collective-permute-done), channel_id=1, source_target_pairs={{0,8},{8,0},{16,24},{24,16},{1,9},{9,1},{17,25},{25,17},{2,10},{10... | collective-permute-start | bytes 3145736 | tf_op jit(solution)/shard_map/ppermute | solution.py:90
  55.9 24.1 %collective-permute-start.19 = (bf16[256,512]{1,0:T(8,128)(2,1)}, bf16[256,512]{1,0:T(8,128)(2,1)}, u32[]{:S(2)}, u32[]{:S(2)}) collective-permute-start(bf16[256,512]{1,0:T(8,128)(2,1)} %collective-permute-done.18.refs_5_), channel_id=1, source_target_pairs={{2,0},{4,2},{6,4},{7,6},{5,7},{3,5},{1,3},{0,1},{10,8},{12,10},{14... | collective-permute-start | bytes 786440 | tf_op jit(solution)/shard_map/ppermute | solution.py:149
  91.0 83.4 %collective-permute-start.20 = (bf16[2048,512]{1,0:T(8,128)(2,1)}, bf16[2048,512]{1,0:T(8,128)(2,1)}, u32[]{:S(2)}, u32[]{:S(2)}) collective-permute-start(bf16[2048,512]{1,0:T(8,128)(2,1)} %place_blocks.9), channel_id=1, source_target_pairs={{0,16},{8,24},{16,0},{24,8},{1,17},{9,25},{17,1},{25,9},{2,18},{10... | collective-permute-start | bytes 6291464 | tf_op jit(solution)/shard_map/ppermute | solution.py:90
  96.0 50.9 %collective-permute-start.27 = (bf16[256,2048]{1,0:T(8,128)(2,1)}, bf16[256,2048]{1,0:T(8,128)(2,1)}, u32[]{:S(2)}, u32[]{:S(2)}) collective-permute-start(bf16[256,2048]{1,0:T(8,128)(2,1)} %collective-permute-done.26.refs_1_), channel_id=1, source_target_pairs={{0,2},{2,4},{4,6},{6,7},{7,5},{5,3},{3,1},{1,0},{8,10},{10,12},{12... | collective-permute-start | bytes 3145736 | tf_op jit(solution)/shard_map/ppermute | solution.py:149
  96.6 53.4 %collective-permute-start.32 = (bf16[256,2048]{1,0:T(8,128)(2,1)}, bf16[256,2048]{1,0:T(8,128)(2,1)}, u32[]{:S(2)}, u32[]{:S(2)}) collective-permute-start(bf16[256,2048]{1,0:T(8,128)(2,1)} %collective-permute-done.31.refs_7_), channel_id=1, source_target_pairs={{2,0},{4,2},{6,4},{7,6},{5,7},{3,5},{1,3},{0,1},{10,8},{12,10},{14... | collective-permute-start | bytes 3145736 | tf_op jit(solution)/shard_map/ppermute | solution.py:149
  146.7 26.1 %collective-permute-start.29 = (bf16[256,2048]{1,0:T(8,128)(2,1)S(1)}, bf16[256,2048]{1,0:T(8,128)(2,1)}, u32[]{:S(2)}, u32[]{:S(2)}) collective-permute-start(bf16[256,2048]{1,0:T(8,128)(2,1)S(1)} %copy-done.31), channel_id=1, source_target_pairs={{0,2},{2,4},{4,6},{6,7},{7,5},{5,3},{3,1},{1,0},{8,10},{10,12},{12... | collective-permute-start | bytes 3145736 | tf_op jit(solution)/shard_map/ppermute | solution.py:149
  148.5 46.8 %collective-permute-start.28 = (bf16[256,2048]{1,0:T(8,128)(2,1)}, bf16[256,2048]{1,0:T(8,128)(2,1)}, u32[]{:S(2)}, u32[]{:S(2)}) collective-permute-start(bf16[256,2048]{1,0:T(8,128)(2,1)} %collective-permute-done.27.refs_2_), channel_id=1, source_target_pairs={{0,2},{2,4},{4,6},{6,7},{7,5},{5,3},{3,1},{1,0},{8,10},{10,12},{12... | collective-permute-start | bytes 3145736 | tf_op jit(solution)/shard_map/ppermute | solution.py:149
  150.0 74.5 %collective-permute-start.21 = (bf16[2048,512]{1,0:T(8,128)(2,1)}, bf16[2048,512]{1,0:T(8,128)(2,1)}, u32[]{:S(2)}, u32[]{:S(2)}) collective-permute-start(bf16[2048,512]{1,0:T(8,128)(2,1)} %place_blocks.9), channel_id=1, source_target_pairs={{0,8},{8,0},{16,24},{24,16},{1,9},{9,1},{17,25},{25,17},{2,10},{10... | collective-permute-start | bytes 6291464 | tf_op jit(solution)/shard_map/ppermute | solution.py:90
  172.8 31.4 %collective-permute-start.37 = (bf16[256,2048]{1,0:T(8,128)(2,1)}, bf16[256,2048]{1,0:T(8,128)(2,1)}, u32[]{:S(2)}, u32[]{:S(2)}) collective-permute-start(bf16[256,2048]{1,0:T(8,128)(2,1)} %collective-permute-done.36.refs_7_), channel_id=1, source_target_pairs={{2,0},{4,2},{6,4},{7,6},{5,7},{3,5},{1,3},{0,1},{10,8},{12,10},{14... | collective-permute-start | bytes 3145736 | tf_op jit(solution)/shard_map/ppermute | solution.py:149
  174.5 43.3 %collective-permute-start.34 = (bf16[256,2048]{1,0:T(8,128)(2,1)}, bf16[256,2048]{1,0:T(8,128)(2,1)}, u32[]{:S(2)}, u32[]{:S(2)}) collective-permute-start(bf16[256,2048]{1,0:T(8,128)(2,1)} %collective-permute-done.29.refs_1_), channel_id=1, source_target_pairs={{0,2},{2,4},{4,6},{6,7},{7,5},{5,3},{3,1},{1,0},{8,10},{10,12},{12... | collective-permute-start | bytes 3145736 | tf_op jit(solution)/shard_map/ppermute | solution.py:149
  175.6 79.0 %collective-permute-start.22 = (bf16[2048,512]{1,0:T(8,128)(2,1)}, bf16[2048,512]{1,0:T(8,128)(2,1)}, u32[]{:S(2)}, u32[]{:S(2)}) collective-permute-start(bf16[2048,512]{1,0:T(8,128)(2,1)} %collective-permute-done.20), channel_id=1, source_target_pairs={{0,8},{8,0},{16,24},{24,16},{1,9},{9,1},{17,25},{25,17},{2,10},{10... | collective-permute-start | bytes 6291464 | tf_op jit(solution)/shard_map/ppermute | solution.py:90
  195.3 28.8 %collective-permute-start.33 = (bf16[256,2048]{1,0:T(8,128)(2,1)}, bf16[256,2048]{1,0:T(8,128)(2,1)}, u32[]{:S(2)}, u32[]{:S(2)}) collective-permute-start(bf16[256,2048]{1,0:T(8,128)(2,1)} %collective-permute-done.32.refs_6_), channel_id=1, source_target_pairs={{2,0},{4,2},{6,4},{7,6},{5,7},{3,5},{1,3},{0,1},{10,8},{12,10},{14... | collective-permute-start | bytes 3145736 | tf_op jit(solution)/shard_map/ppermute | solution.py:149
  204.2 48.8 %collective-permute-start.30 = (bf16[256,2048]{1,0:T(8,128)(2,1)}, bf16[256,2048]{1,0:T(8,128)(2,1)S(1)}, u32[]{:S(2)}, u32[]{:S(2)}) collective-permute-start(bf16[256,2048]{1,0:T(8,128)(2,1)} %collective-permute-done.28.refs_3_), channel_id=1, source_target_pairs={{0,2},{2,4},{4,6},{6,7},{7,5},{5,3},{3,1},{1,0},{8,10},{10,12},{12... | collective-permute-start | bytes 3145736 | tf_op jit(solution)/shard_map/ppermute | solution.py:149
  217.8 30.7 %collective-permute-start.38 = (bf16[256,2048]{1,0:T(8,128)(2,1)}, bf16[256,2048]{1,0:T(8,128)(2,1)S(1)}, u32[]{:S(2)}, u32[]{:S(2)}) collective-permute-start(bf16[256,2048]{1,0:T(8,128)(2,1)} %collective-permute-done.37.refs_6_), channel_id=1, source_target_pairs={{2,0},{4,2},{6,4},{7,6},{5,7},{3,5},{1,3},{0,1},{10,8},{12,10},{14... | collective-permute-start | bytes 3145736 | tf_op jit(solution)/shard_map/ppermute | solution.py:149
  224.1 27.2 %collective-permute-start.43 = (bf16[128,2048]{1,0:T(8,128)(2,1)S(1)}, bf16[128,2048]{1,0:T(8,128)(2,1)S(1)}, u32[]{:S(2)}, u32[]{:S(2)}) collective-permute-start(bf16[128,2048]{1,0:T(8,128)(2,1)S(1)} %copy-done.21), channel_id=1, source_target_pairs={{0,2},{2,4},{4,6},{6,7},{7,5},{5,3},{3,1},{1,0},{8,10},{10,12},{12... | collective-permute-start | bytes 1572872 | tf_op jit(solution)/shard_map/ppermute | solution.py:149
  224.6 23.6 %collective-permute-start.48 = (bf16[128,2048]{1,0:T(8,128)(2,1)S(1)}, bf16[128,2048]{1,0:T(8,128)(2,1)S(1)}, u32[]{:S(2)}, u32[]{:S(2)}) collective-permute-start(bf16[128,2048]{1,0:T(8,128)(2,1)S(1)} %copy-done.21), channel_id=1, source_target_pairs={{2,0},{4,2},{6,4},{7,6},{5,7},{3,5},{1,3},{0,1},{10,8},{12,10},{14... | collective-permute-start | bytes 1572872 | tf_op jit(solution)/shard_map/ppermute | solution.py:149
  248.1 50.9 %collective-permute-start.40 = (bf16[256,2048]{1,0:T(8,128)(2,1)}, bf16[256,2048]{1,0:T(8,128)(2,1)}, u32[]{:S(2)}, u32[]{:S(2)}) collective-permute-start(bf16[256,2048]{1,0:T(8,128)(2,1)} %bitcast.27), channel_id=1, source_target_pairs={{0,16},{8,24},{16,0},{24,8},{1,17},{9,25},{17,1},{25,9},{2,18},{10... | collective-permute-start | bytes 3145736 | tf_op jit(solution)/shard_map/ppermute | solution.py:90
  248.5 26.2 %collective-permute-start.35 = (bf16[256,2048]{1,0:T(8,128)(2,1)}, bf16[256,2048]{1,0:T(8,128)(2,1)S(1)}, u32[]{:S(2)}, u32[]{:S(2)}) collective-permute-start(bf16[256,2048]{1,0:T(8,128)(2,1)} %collective-permute-done.34.refs_2_), channel_id=1, source_target_pairs={{0,2},{2,4},{4,6},{6,7},{7,5},{5,3},{3,1},{1,0},{8,10},{10,12},{12... | collective-permute-start | bytes 3145736 | tf_op jit(solution)/shard_map/ppermute | solution.py:149
  253.0 61.2 %collective-permute-start.39 = (bf16[256,2048]{1,0:T(8,128)(2,1)S(1)}, bf16[256,2048]{1,0:T(8,128)(2,1)S(1)}, u32[]{:S(2)}, u32[]{:S(2)}) collective-permute-start(bf16[256,2048]{1,0:T(8,128)(2,1)S(1)} %collective-permute-done.38.refs_5_), channel_id=1, source_target_pairs={{2,0},{4,2},{6,4},{7,6},{5,7},{3,5},{1,3},{0,1},{10,8},{12,10},{14... | collective-permute-start | bytes 3145736 | tf_op jit(solution)/shard_map/ppermute | solution.py:149
  254.6 42.7 %collective-permute-start.44 = (bf16[128,2048]{1,0:T(8,128)(2,1)S(1)}, bf16[128,2048]{1,0:T(8,128)(2,1)S(1)}, u32[]{:S(2)}, u32[]{:S(2)}) collective-permute-start(bf16[128,2048]{1,0:T(8,128)(2,1)S(1)} %collective-permute-done.43.refs_1_), channel_id=1, source_target_pairs={{0,2},{2,4},{4,6},{6,7},{7,5},{5,3},{3,1},{1,0},{8,10},{10,12},{12... | collective-permute-start | bytes 1572872 | tf_op jit(solution)/shard_map/ppermute | solution.py:149
  266.2 30.9 %collective-permute-start.49 = (bf16[128,2048]{1,0:T(8,128)(2,1)S(1)}, bf16[128,2048]{1,0:T(8,128)(2,1)}, u32[]{:S(2)}, u32[]{:S(2)}) collective-permute-start(bf16[128,2048]{1,0:T(8,128)(2,1)S(1)} %collective-permute-done.48.refs_7_), channel_id=1, source_target_pairs={{2,0},{4,2},{6,4},{7,6},{5,7},{3,5},{1,3},{0,1},{10,8},{12,10},{14... | collective-permute-start | bytes 1572872 | tf_op jit(solution)/shard_map/ppermute | solution.py:149
  274.7 41.2 %collective-permute-start.23 = (bf16[256,2048]{1,0:T(8,128)(2,1)}, bf16[256,2048]{1,0:T(8,128)(2,1)}, u32[]{:S(2)}, u32[]{:S(2)}) collective-permute-start(bf16[256,2048]{1,0:T(8,128)(2,1)} %multiply_convert_fusion.4), channel_id=1, source_target_pairs={{0,16},{8,24},{16,0},{24,8},{1,17},{9,25},{17,1},{25,9},{2,18},{10... | collective-permute-start | bytes 3145736 | tf_op jit(solution)/shard_map/ppermute | solution.py:90
  306.2 29.6 %collective-permute-start.41 = (bf16[256,2048]{1,0:T(8,128)(2,1)}, bf16[256,2048]{1,0:T(8,128)(2,1)}, u32[]{:S(2)}, u32[]{:S(2)}) collective-permute-start(bf16[256,2048]{1,0:T(8,128)(2,1)} %bitcast.27), channel_id=1, source_target_pairs={{0,8},{8,0},{16,24},{24,16},{1,9},{9,1},{17,25},{25,17},{2,10},{10... | collective-permute-start | bytes 3145736 | tf_op jit(solution)/shard_map/ppermute | solution.py:90
  306.5 30.9 %collective-permute-start.42 = (bf16[256,2048]{1,0:T(8,128)(2,1)}, bf16[256,2048]{1,0:T(8,128)(2,1)}, u32[]{:S(2)}, u32[]{:S(2)}) collective-permute-start(bf16[256,2048]{1,0:T(8,128)(2,1)} %collective-permute-done.40), channel_id=1, source_target_pairs={{0,8},{8,0},{16,24},{24,16},{1,9},{9,1},{17,25},{25,17},{2,10},{10... | collective-permute-start | bytes 3145736 | tf_op jit(solution)/shard_map/ppermute | solution.py:90
  323.1 44.9 %collective-permute-start.24 = (bf16[256,2048]{1,0:T(8,128)(2,1)}, bf16[256,2048]{1,0:T(8,128)(2,1)}, u32[]{:S(2)}, u32[]{:S(2)}) collective-permute-start(bf16[256,2048]{1,0:T(8,128)(2,1)} %multiply_convert_fusion.4), channel_id=1, source_target_pairs={{0,8},{8,0},{16,24},{24,16},{1,9},{9,1},{17,25},{25,17},{2,10},{10... | collective-permute-start | bytes 3145736 | tf_op jit(solution)/shard_map/ppermute | solution.py:90
  326.7 41.2 %collective-permute-start.25 = (bf16[256,2048]{1,0:T(8,128)(2,1)}, bf16[256,2048]{1,0:T(8,128)(2,1)}, u32[]{:S(2)}, u32[]{:S(2)}) collective-permute-start(bf16[256,2048]{1,0:T(8,128)(2,1)} %collective-permute-done.23), channel_id=1, source_target_pairs={{0,8},{8,0},{16,24},{24,16},{1,9},{9,1},{17,25},{25,17},{2,10},{10... | collective-permute-start | bytes 3145736 | tf_op jit(solution)/shard_map/ppermute | solution.py:90
  333.5 26.4 %collective-permute-start.47 = (bf16[128,2048]{1,0:T(8,128)(2,1)S(1)}, bf16[128,2048]{1,0:T(8,128)(2,1)S(1)}, u32[]{:S(2)}, u32[]{:S(2)}) collective-permute-start(bf16[128,2048]{1,0:T(8,128)(2,1)S(1)} %copy-done.55), channel_id=1, source_target_pairs={{0,2},{2,4},{4,6},{6,7},{7,5},{5,3},{3,1},{1,0},{8,10},{10,12},{12... | collective-permute-start | bytes 1572872 | tf_op jit(solution)/shard_map/ppermute | solution.py:149
  335.8 24.0 %collective-permute-start.52 = (bf16[128,2048]{1,0:T(8,128)(2,1)S(1)}, bf16[128,2048]{1,0:T(8,128)(2,1)}, u32[]{:S(2)}, u32[]{:S(2)}) collective-permute-start(bf16[128,2048]{1,0:T(8,128)(2,1)S(1)} %copy-done.57), channel_id=1, source_target_pairs={{0,2},{2,4},{4,6},{6,7},{7,5},{5,3},{3,1},{1,0},{8,10},{10,12},{12... | collective-permute-start | bytes 1572872 | tf_op jit(solution)/shard_map/ppermute | solution.py:149
  462.8 29.5 %collective-permute-start.59 = (bf16[512,2048]{1,0:T(8,128)(2,1)}, bf16[512,2048]{1,0:T(8,128)(2,1)S(1)}, u32[]{:S(2)}, u32[]{:S(2)}) collective-permute-start(bf16[512,2048]{1,0:T(8,128)(2,1)} %get-tuple-element.122), channel_id=1, source_target_pairs={{0,8},{8,0},{16,24},{24,16},{1,9},{9,1},{17,25},{25,17},{2,10},{10... | collective-permute-start | bytes 6291464 | tf_op jit(solution)/shard_map/ppermute | solution.py:90
  491.6 46.3 %collective-permute-start.58 = (bf16[256,2048]{1,0:T(8,128)(2,1)S(1)}, bf16[256,2048]{1,0:T(8,128)(2,1)S(1)}, u32[]{:S(2)}, u32[]{:S(2)}) collective-permute-start(bf16[256,2048]{1,0:T(8,128)(2,1)S(1)} %get-tuple-element.162), channel_id=1, source_target_pairs={{0,8},{8,0},{16,24},{24,16},{1,9},{9,1},{17,25},{25,17},{2,10},{10... | collective-permute-start | bytes 3145736 | tf_op jit(solution)/shard_map/ppermute | solution.py:90
  493.2 25.2 %collective-permute-start.60 = (bf16[256,2048]{1,0:T(8,128)(2,1)S(1)}, bf16[256,2048]{1,0:T(8,128)(2,1)S(1)}, u32[]{:S(2)}, u32[]{:S(2)}) collective-permute-start(bf16[256,2048]{1,0:T(8,128)(2,1)S(1)} %slice.414), channel_id=1, source_target_pairs={{0,16},{8,24},{16,0},{24,8},{1,17},{9,25},{17,1},{25,9},{2,18},{10... | collective-permute-start | bytes 3145736 | tf_op jit(solution)/shard_map/ppermute | solution.py:90
  542.5 44.5 %collective-permute-start.57 = (bf16[256,2048]{1,0:T(8,128)(2,1)}, bf16[256,2048]{1,0:T(8,128)(2,1)}, u32[]{:S(2)}, u32[]{:S(2)}) collective-permute-start(bf16[256,2048]{1,0:T(8,128)(2,1)} %get-tuple-element.161), channel_id=1, source_target_pairs={{0,8},{8,0},{16,24},{24,16},{1,9},{9,1},{17,25},{25,17},{2,10},{10... | collective-permute-start | bytes 3145736 | tf_op jit(solution)/shard_map/ppermute | solution.py:90
  542.5 33.9 %collective-permute-start.68 = (bf16[640,512]{1,0:T(8,128)(2,1)S(1)}, bf16[640,512]{1,0:T(8,128)(2,1)}, u32[]{:S(2)}, u32[]{:S(2)}) collective-permute-start(bf16[640,512]{1,0:T(8,128)(2,1)S(1)} %get-tuple-element.159), channel_id=1, source_target_pairs={{0,8},{8,0},{16,24},{24,16},{1,9},{9,1},{17,25},{25,17},{2,10},{10... | collective-permute-start | bytes 1966088 | tf_op jit(solution)/shard_map/ppermute | solution.py:90
  545.0 42.0 %collective-permute-start.66 = (bf16[256,2048]{1,0:T(8,128)(2,1)}, bf16[256,2048]{1,0:T(8,128)(2,1)}, u32[]{:S(2)}, u32[]{:S(2)}) collective-permute-start(bf16[256,2048]{1,0:T(8,128)(2,1)} %fusion.23), channel_id=1, source_target_pairs={{0,16},{8,24},{16,0},{24,8},{1,17},{9,25},{17,1},{25,9},{2,18},{10... | collective-permute-start | bytes 3145736 | tf_op jit(solution)/shard_map/ppermute | solution.py:90
  547.8 37.2 %collective-permute-start.70 = (bf16[640,512]{1,0:T(8,128)(2,1)}, bf16[640,512]{1,0:T(8,128)(2,1)}, u32[]{:S(2)}, u32[]{:S(2)}) collective-permute-start(bf16[640,512]{1,0:T(8,128)(2,1)} %add_convert_fusion.2), channel_id=1, source_target_pairs={{0,16},{8,24},{16,0},{24,8},{1,17},{9,25},{17,1},{25,9},{2,18},{10... | collective-permute-start | bytes 1966088 | tf_op jit(solution)/shard_map/ppermute | solution.py:90
  548.2 28.1 %collective-permute-start.67 = (bf16[192,512]{1,0:T(8,128)(2,1)S(1)}, bf16[192,512]{1,0:T(8,128)(2,1)S(1)}, u32[]{:S(2)}, u32[]{:S(2)}) collective-permute-start(bf16[192,512]{1,0:T(8,128)(2,1)S(1)} %constant_dynamic-slice_fusion.7), channel_id=1, source_target_pairs={{0,4},{1,5},{2,6},{3,7},{4,0},{5,1},{6,2},{7,3},{8,12},{9,13},{10,... | collective-permute-start | bytes 589832 | tf_op jit(solution)/shard_map/ppermute | solution.py:90
  630.5 33.0 %collective-permute-start.81 = (bf16[768,512]{1,0:T(8,128)(2,1)S(1)}, bf16[768,512]{1,0:T(8,128)(2,1)S(1)}, u32[]{:S(2)}, u32[]{:S(2)}) collective-permute-start(bf16[768,512]{1,0:T(8,128)(2,1)S(1)} %pad_maximum_fusion.12), channel_id=1, source_target_pairs={{0,1},{1,0},{2,3},{3,2},{4,5},{5,4},{6,7},{7,6},{8,9},{9,8},{10,11... | collective-permute-start | bytes 2359304 | tf_op jit(solution)/shard_map/ppermute | solution.py:90
  633.7 31.2 %collective-permute-start.79 = (bf16[256,2048]{1,0:T(8,128)(2,1)S(1)}, bf16[256,2048]{1,0:T(8,128)(2,1)S(1)}, u32[]{:S(2)}, u32[]{:S(2)}) collective-permute-start(bf16[256,2048]{1,0:T(8,128)(2,1)S(1)} %slice.413), channel_id=1, source_target_pairs={{0,16},{8,24},{16,0},{24,8},{1,17},{9,25},{17,1},{25,9},{2,18},{10... | collective-permute-start | bytes 3145736 | tf_op jit(solution)/shard_map/ppermute | solution.py:90
  636.6 26.2 %collective-permute-start.80 = (bf16[192,512]{1,0:T(8,128)(2,1)S(1)}, bf16[192,512]{1,0:T(8,128)(2,1)S(1)}, u32[]{:S(2)}, u32[]{:S(2)}) collective-permute-start(bf16[192,512]{1,0:T(8,128)(2,1)S(1)} %constant_dynamic-slice_fusion.6), channel_id=1, source_target_pairs={{0,1},{1,0},{2,3},{3,2},{4,5},{5,4},{6,7},{7,6},{8,9},{9,8},{10,11... | collective-permute-start | bytes 589832 | tf_op jit(solution)/shard_map/ppermute | solution.py:90
  667.2 36.0 %collective-permute-start.95 = (bf16[1536,512]{1,0:T(8,128)(2,1)}, bf16[1536,512]{1,0:T(8,128)(2,1)}, u32[]{:S(2)}, u32[]{:S(2)}) collective-permute-start(bf16[1536,512]{1,0:T(8,128)(2,1)} %pad_maximum_fusion.4.refs_0_), channel_id=1, source_target_pairs={{0,16},{8,24},{16,0},{24,8},{1,17},{9,25},{17,1},{25,9},{2,18},{10... | collective-permute-start | bytes 4718600 | tf_op jit(solution)/shard_map/ppermute | solution.py:90
  697.8 29.4 %collective-permute-start.96 = (bf16[1536,512]{1,0:T(8,128)(2,1)}, bf16[1536,512]{1,0:T(8,128)(2,1)}, u32[]{:S(2)}, u32[]{:S(2)}) collective-permute-start(bf16[1536,512]{1,0:T(8,128)(2,1)} %pad_maximum_fusion.4.refs_0_), channel_id=1, source_target_pairs={{0,8},{8,0},{16,24},{24,16},{1,9},{9,1},{17,25},{25,17},{2,10},{10... | collective-permute-start | bytes 4718600 | tf_op jit(solution)/shard_map/ppermute | solution.py:90
  703.2 24.0 %collective-permute-start.97 = (bf16[1536,512]{1,0:T(8,128)(2,1)}, bf16[1536,512]{1,0:T(8,128)(2,1)}, u32[]{:S(2)}, u32[]{:S(2)}) collective-permute-start(bf16[1536,512]{1,0:T(8,128)(2,1)} %collective-permute-done.95.refs_1_), channel_id=1, source_target_pairs={{0,8},{8,0},{16,24},{24,16},{1,9},{9,1},{17,25},{25,17},{2,10},{10... | collective-permute-start | bytes 4718600 | tf_op jit(solution)/shard_map/ppermute | solution.py:90
  707.2 35.4 %collective-permute-start.94 = (bf16[896,512]{1,0:T(8,128)(2,1)S(1)}, bf16[896,512]{1,0:T(8,128)(2,1)S(1)}, u32[]{:S(2)}, u32[]{:S(2)}) collective-permute-start(bf16[896,512]{1,0:T(8,128)(2,1)S(1)} %pad_maximum_fusion.9.refs_0_), channel_id=1, source_target_pairs={{0,16},{8,24},{16,0},{24,8},{1,17},{9,25},{17,1},{25,9},{2,18},{10... | collective-permute-start | bytes 2752520 | tf_op jit(solution)/shard_map/ppermute | solution.py:90
  727.1 24.2 %collective-permute-start.98 = (bf16[896,512]{1,0:T(8,128)(2,1)S(1)}, bf16[896,512]{1,0:T(8,128)(2,1)}, u32[]{:S(2)}, u32[]{:S(2)}) collective-permute-start(bf16[896,512]{1,0:T(8,128)(2,1)S(1)} %pad_maximum_fusion.9.refs_0_), channel_id=1, source_target_pairs={{0,8},{8,0},{16,24},{24,16},{1,9},{9,1},{17,25},{25,17},{2,10},{10... | collective-permute-start | bytes 2752520 | tf_op jit(solution)/shard_map/ppermute | solution.py:90
  (158 other events, 2292.8 us)

commit v4 on v3

--- a/solution.py
+++ b/solution.py
@@ -605,28 +605,47 @@
     return out
 
 
-def scatter_step(total, bit):
-    half = total.shape[0] // 2
-    high = ((lax.axis_index("fsdp") & bit) != 0).astype(jnp.int32)
-    keep = lax.dynamic_slice_in_dim(total, high * half, half, 0)
-    give = lax.dynamic_slice_in_dim(total, (1 - high) * half, half, 0)
-    got = swap(give, "fsdp", bit)
-    return (keep.astype(F32) + got.astype(F32)).astype(BF16)
+def pairs_of(bits):
+    return [bits[k : k + 2] for k in range(0, len(bits), 2)]
+
+
+def scatter_step(total, *bits):
+    me = lax.axis_index("fsdp")
+    rows = total.shape[0] >> len(bits)
+    offsets = [0]
+    for bit in bits:
+        offsets = offsets + [o ^ bit for o in offsets]
+
+    def run_of(device):
+        number = 0
+        for bit in bits:
+            number = 2 * number + ((device & bit) != 0).astype(jnp.int32)
+        return lax.dynamic_slice_in_dim(total, number * rows, rows, 0)
+
+    kept = run_of(me).astype(F32)
+    for got in [swap(run_of(me ^ o), "fsdp", o) for o in offsets[1:]]:
+        kept = kept + got.astype(F32)
+    return kept.astype(BF16)
 
 
 def reduce_scatter_rows(total):
-    for bit in reversed(bits_down(lax.axis_size("fsdp"))):
-        total = scatter_step(total, bit)
+    first, *rest = reversed(bits_down(lax.axis_size("fsdp")))
+    total = scatter_step(total, first)
+    for bits in pairs_of(rest):
+        total = scatter_step(total, *bits)
     return total
 
 
-def widen(piece, bit):
-    return jnp.concatenate([piece, swap(piece, "fsdp", bit)], axis=0)
+def widen(piece, *bits):
+    pieces, sent = [piece], [0]
+    for bit in bits:
+        sent = sent + [o ^ bit for o in sent]
+    return jnp.concatenate(pieces + [swap(piece, "fsdp", o) for o in sent[1:]], axis=0)
 
 
 def share_out(piece):
-    for bit in bits_down(lax.axis_size("fsdp")):
-        piece = widen(piece, bit)
+    for bits in pairs_of(bits_down(lax.axis_size("fsdp"))):
+        piece = widen(piece, *bits)
     return piece
 
 
@@ -919,10 +938,15 @@
         return part.transpose(2, 1, 3, 0, 4).reshape(SPAN, feed_units)
 
     late_sums = scatter_step(grad_a_qkv.astype(BF16), unit_bits[0])
-    unit_sums = widen(unit_sums, wide_bits[-1])
-    late_sums, unit_sums = after((late_sums, unit_sums), grad_normed_one)
-    for bit in unit_bits[1:]:
-        late_sums = scatter_step(late_sums, bit)
+    unit_sums = widen(after(unit_sums, late_sums), wide_bits[-1])
+    for bits in pairs_of(unit_bits[1:]):
+        late_sums = scatter_step(late_sums, *bits)
+    late_sums = after(late_sums, grad_normed_one)
+    first_bits, *rest_bits = pairs_of(wide_bits)
+    late_sums = widen(late_sums, *first_bits)
+    late_sums, unit_sums = after((late_sums, unit_sums))
+    for bits in rest_bits:
+        late_sums = widen(late_sums, *bits)
     unit_pieces = gather_relative(unit_sums, "seq")
     early = settle(unit_pieces)
     blank = jnp.zeros((SPAN, width - 2 * kv_width), BF16)
@@ -954,7 +978,6 @@
     middle = settle(middle_pieces)
     b_kv = middle[:, 6 * SPAN :, : 2 * kv_width].reshape(seqs, SPAN, 2, kv_width)
     a_all, b_model = finish_model(middle, factor)
-    late_sums = share_out(late_sums)
     late = settle(gather_relative(late_sums, "seq", [b_model]))
     return (
         layer_out[None],

time: 785 us -> 780 us (level)
  starting transfers between devices: 89.6 us -> 104 us
  waiting for transfers between devices: 274 us -> 260 us
    ppermute x60 -> x64, waiting for transfers between devices: 126 us -> 112 us  [swap(): return lax.ppermute(block, axis, [(i, i ^ offset) for i in range(count)])]
    ppermute x60 -> x64, starting transfers between devices: 41.1 us -> 55.3 us  [swap(): return lax.ppermute(block, axis, [(i, i ^ offset) for i in range(count)])]
  transfers between devices with their start and end apart: 102 -> 106, of which waited for: 42 -> 43; matrix products, arithmetic and copies ran while one was open for 21% -> 21% of each run, Pallas kernels for 16% -> 16%
where the time goes in v4:
time: 780 us; the launch traced here: 772 us
  waiting for transfers between devices  260 us (33%)
  Pallas kernels  174 us (22%)
  matrix products  120 us (15%)
  starting transfers between devices  104 us (13%)
  local copies, waits for them, and re-layouts  60.6 us (8%)
  other arithmetic  51.4 us (7%)
    ppermute x42, waiting for transfers between devices, send(): got = lax.ppermute(block, 'fsdp', self.perms[way])  148 us
    ppermute x64, waiting for transfers between devices, swap(): return lax.ppermute(block, axis, [(i, i ^ offset) for i in range(count)])  112 us
    dot_general x19, matrix products, mm(): return jnp.dot(left, right, preferred_element_type=F32)  85.2 us
    ppermute x64, starting transfers between devices, swap(): return lax.ppermute(block, axis, [(i, i ^ offset) for i in range(count)])  55.3 us
    ppermute x42, starting transfers between devices, send(): got = lax.ppermute(block, 'fsdp', self.perms[way])  48.5 us
    pallas_call x8, Pallas kernels, place_blocks(): pl.pallas_call(body, out_shape=jax.ShapeDtypeStruct((rows * total, column...  42.4 us
    pallas_call x2, Pallas kernels, sum_products(): pl.pallas_call(body, grid=(outs // tile,), in_specs=[pl.BlockSpec(a.shape...  34.5 us
    pallas_call x1, Pallas kernels, attend_backward(): pl.pallas_call(lambda *refs: backward_body(blocks, groups, *refs), grid_s...  24.9 us
  transfers between devices with their start and end apart: 106, of which 43 were waited for; matrix products, arithmetic and copies ran while one was open for 21% of the time, Pallas kernels for 16%

profile of v4, /device:TPU:0, one launch (start us, length us, event | category | flops | bytes accessed | tf_op | source)
XLA Modules:
  0.0 772.4 jit_solution(10149328899804307697)
XLA Ops:
  24.9 7.2 collective-permute-done.9.refs_6_
  40.4 5.9 take_units.2
  113.9 23.1 %attend_forward.1 = (bf16[1024,512]{1,0:T(8,128)(2,1)}, bf16[1024,256]{1,0:T(8,128)(2,1)}, bf16[1024,256]{1,0:T(8,128)(2,1)}, bf16[1024,512]{1,0:T(8,128)(2,1)}, f32[4,2,1024]{2,1,0:T(2,128)}) custom-call(s32[4]{0:T(128)} %pad_add_fusion.refs_0_, f32[1024,512]{1,0:T(8,128)} %slice_add_fusion.4.refs_1_, f32[1024,256]{1,0:T(8,128)} %pad_maximum_fusion.5.refs_2_, ...), custom_call_target="tpu_custom_call" | custom-call | flops 2147483648 | bytes 16777216 | tf_op jit(solution)/shard_map/attend_forward/pallas_call | solution.py:486
  142.1 4.6 collective-permute-done.12
  150.1 13.8 %collective-permute-done.36.refs_7_ = bf16[256,2048]{1,0:T(8,128)(2,1)} collective-permute-done((bf16[256,2048]{1,0:T(8,128)(2,1)S(1)}, bf16[256,2048]{1,0:T(8,128)(2,1)}, u32[]{:S(2)}, u32[]{:S(2)}) %collective-permute-start.36) | collective-permute-done | bytes 1048608 | tf_op jit(solution)/shard_map/ppermute | solution.py:149
  163.9 8.9 %collective-permute-done.29.refs_1_ = bf16[256,2048]{1,0:T(8,128)(2,1)} collective-permute-done((bf16[256,2048]{1,0:T(8,128)(2,1)S(1)}, bf16[256,2048]{1,0:T(8,128)(2,1)}, u32[]{:S(2)}, u32[]{:S(2)}) %collective-permute-start.29) | collective-permute-done | bytes 1048608 | tf_op jit(solution)/shard_map/ppermute | solution.py:149
  175.6 19.7 %collective-permute-done.28.refs_3_ = bf16[256,2048]{1,0:T(8,128)(2,1)} collective-permute-done((bf16[256,2048]{1,0:T(8,128)(2,1)}, bf16[256,2048]{1,0:T(8,128)(2,1)}, u32[]{:S(2)}, u32[]{:S(2)}) %collective-permute-start.28) | collective-permute-done | bytes 1048608 | tf_op jit(solution)/shard_map/ppermute | solution.py:149
  205.0 12.8 %collective-permute-done.34.refs_2_ = bf16[256,2048]{1,0:T(8,128)(2,1)} collective-permute-done((bf16[256,2048]{1,0:T(8,128)(2,1)}, bf16[256,2048]{1,0:T(8,128)(2,1)}, u32[]{:S(2)}, u32[]{:S(2)}) %collective-permute-start.34) | collective-permute-done | bytes 1048608 | tf_op jit(solution)/shard_map/ppermute | solution.py:149
  231.6 16.7 %collective-permute-done.48.refs_7_ = bf16[128,2048]{1,0:T(8,128)(2,1)S(1)} collective-permute-done((bf16[128,2048]{1,0:T(8,128)(2,1)S(1)}, bf16[128,2048]{1,0:T(8,128)(2,1)S(1)}, u32[]{:S(2)}, u32[]{:S(2)}) %collective-permute-start.48) | collective-permute-done | bytes 524320 | tf_op jit(solution)/shard_map/ppermute | solution.py:149
  259.5 6.7 collective-permute-done.53.refs_15_
  269.1 5.7 collective-permute-done.35.refs_3_
  276.5 20.5 %collective-permute-done.49.refs_6_ = bf16[128,2048]{1,0:T(8,128)(2,1)} collective-permute-done((bf16[128,2048]{1,0:T(8,128)(2,1)S(1)}, bf16[128,2048]{1,0:T(8,128)(2,1)}, u32[]{:S(2)}, u32[]{:S(2)}) %collective-permute-start.49) | collective-permute-done | bytes 524320 | tf_op jit(solution)/shard_map/ppermute | solution.py:149
  299.4 6.8 collective-permute-done.46.refs_9_
  306.8 7.0 collective-permute-done.45.refs_3_
  323.1 3.7 collective-permute-done.55.refs_13_
  328.2 5.3 take_units.3
  345.7 7.1 place_blocks.10.refs_3_
  352.8 7.2 place_blocks.11.refs_4_
  360.7 7.3 place_blocks.12.down_ref
  372.7 4.5 fusion.52
  377.2 14.6 %convolution_add_fusion.2.gate_ref = f32[1024,2048]{1,0:T(8,128)} fusion(f32[1024,2048]{1,0:T(8,128)S(1)} %fusion.55, bf16[2048,2048]{1,0:T(8,128)(2,1)} %place_blocks.10.refs_3_, bf16[256,2048]{1,0:T(8,128)(2,1)} %collective-permute-done.25, bf16[256,2048]{1,0:T(8,128)(2,1)} %collective-permute-done.24, bf16[256,2048]{1,0:T(8,128)(2,1)} %collective-permute-done.23, ...), kind=kOutput, calls=%fused_computation.22 | convolution fusion | flops 8608808960 | bytes 29360128 | tf_op jit(solution)/shard_map/dot_general | solution.py:32
  391.8 20.2 %multiply_convert_fusion.1 = (bf16[1024,2048]{1,0:T(8,128)(2,1)}, f32[1024,2048]{1,0:T(8,128)}) fusion(f32[1024,2048]{1,0:T(8,128)} %convolution_add_fusion.2.gate_ref, f32[1024,2048]{1,0:T(8,128)} %fusion.52, bf16[2048,2048]{1,0:T(8,128)(2,1)} %place_blocks.11.refs_4_, bf16[256,2048]{1,0:T(8,128)(2,1)} %collective-permute-done.25, ...), kind=kOutput, calls=%fused_computation.9 | convolution fusion | flops 8621391872 | bytes 41943040 | tf_op jit(solution)/shard_map/dot_general | solution.py:32
  412.0 19.4 %gate_grads.1 = (bf16[1024,2048]{1,0:T(8,128)(2,1)}, bf16[1024,2048]{1,0:T(8,128)(2,1)}) custom-call(bf16[1024,2048]{1,0:T(8,128)(2,1)} %copy-done.6, bf16[2048,2048]{1,0:T(8,128)(2,1)} %place_blocks.12.down_ref, bf16[1024,128]{1,0:T(8,128)(2,1)} %fusion.27.gl_ref, bf16[2048,128]{1,0:T(8,128)(2,1)} %bitcast.187, ...), custom_call_target="tpu_custom_call" | custom-call | flops 8589934592 | bytes 33554432 | tf_op jit(solution)/shard_map/gate_grads/pallas_call | solution.py:556
  431.4 3.6 convolution_convert_fusion.7
  437.2 25.8 %sum_products.2 = (bf16[512,2048]{1,0:T(8,128)(2,1)}, bf16[512,2048]{1,0:T(8,128)(2,1)}) custom-call(bf16[1024,2048]{1,0:T(8,128)(2,1)} %get-tuple-element.126.refs_0_, bf16[1024,2048]{1,0:T(8,128)(2,1)} %get-tuple-element.127.refs_1_, bf16[1024,256]{1,0:T(8,128)(2,1)} %bitcast_multiply_fusion.refs_2_, bf16[2048,2048]{1,0:T(8,128)(2,1)} %place_blocks.10.refs_3_, ...), custom_call_target="tpu_custom_call" | custom-call | flops 18253611008 | bytes 30932992 | tf_op jit(solution)/shard_map/sum_products/pallas_call | solution.py:584
  475.5 13.5 %fusion.125 = (bf16[1024,2048]{1,0:T(8,128)(2,1)}, f32[1024,2048]{1,0:T(8,128)}) fusion(f32[1024,2048]{1,0:T(8,128)S(1)} %fusion.43, bf16[1024,2048]{1,0:T(8,128)(2,1)} %get-tuple-element.128, bf16[2048,2048]{1,0:T(8,128)(2,1)S(1)} %bitcast.177), kind=kOutput, calls=%fused_computation.278 | convolution fusion | flops 8594128896 | bytes 33554432 | tf_op jit(solution)/shard_map/dot_general | solution.py:32
  499.0 12.9 %collective-permute-done.61 = bf16[768,512]{1,0:T(8,128)(2,1)S(1)} collective-permute-done((bf16[768,512]{1,0:T(8,128)(2,1)S(1)}, bf16[768,512]{1,0:T(8,128)(2,1)S(1)}, u32[]{:S(2)}, u32[]{:S(2)}) %collective-permute-start.61) | collective-permute-done | bytes 786464 | tf_op jit(solution)/shard_map/ppermute | solution.py:90
  512.1 6.4 collective-permute-done.60
  526.1 4.8 fusion.12
  538.2 4.5 fusion.23
  551.7 24.9 %attend_backward.1.refs_0_ = bf16[1024,768]{1,0:T(8,128)(2,1)} custom-call(s32[4]{0:T(128)} %pad_add_fusion.refs_0_, bf16[1024,512]{1,0:T(8,128)(2,1)} %get-tuple-element.134.refs_1_, bf16[1024,256]{1,0:T(8,128)(2,1)} %get-tuple-element.135.refs_2_, bf16[1024,256]{1,0:T(8,128)(2,1)} %get-tuple-element.136.refs_3_, ...), custom_call_target="tpu_custom_call" | custom-call | tf_op jit(solution)/shard_map/attend_backward/pallas_call | solution.py:517
  576.6 8.5 %collective-permute-done.70 = bf16[640,512]{1,0:T(8,128)(2,1)} collective-permute-done((bf16[640,512]{1,0:T(8,128)(2,1)}, bf16[640,512]{1,0:T(8,128)(2,1)}, u32[]{:S(2)}, u32[]{:S(2)}) %collective-permute-start.70) | collective-permute-done | bytes 655392 | tf_op jit(solution)/shard_map/ppermute | solution.py:90
  587.2 4.0 fusion.30
  599.4 8.3 %collective-permute-done.73 = bf16[192,512]{1,0:T(8,128)(2,1)S(1)} collective-permute-done((bf16[192,512]{1,0:T(8,128)(2,1)S(1)}, bf16[192,512]{1,0:T(8,128)(2,1)S(1)}, u32[]{:S(2)}, u32[]{:S(2)}) %collective-permute-start.73) | collective-permute-done | bytes 196640 | tf_op jit(solution)/shard_map/ppermute | solution.py:90
  609.1 5.4 collective-permute-done.74
  614.6 8.7 %sum_products.3 = (bf16[512,2048]{1,0:T(8,128)(2,1)}, bf16[512,2048]{1,0:T(8,128)(2,1)}) custom-call(bf16[1024,768]{1,0:T(8,128)(2,1)} %attend_backward.1.refs_0_, bf16[2048,768]{1,0:T(8,128)(2,1)} %place_blocks.8.refs_1_), custom_call_target="tpu_custom_call" | custom-call | flops 3221225472 | bytes 8912896 | tf_op jit(solution)/shard_map/sum_products/pallas_call | solution.py:584
  641.2 15.8 %collective-permute-done.79 = bf16[256,2048]{1,0:T(8,128)(2,1)S(1)} collective-permute-done((bf16[256,2048]{1,0:T(8,128)(2,1)S(1)}, bf16[256,2048]{1,0:T(8,128)(2,1)S(1)}, u32[]{:S(2)}, u32[]{:S(2)}) %collective-permute-start.79) | collective-permute-done | bytes 1048608 | tf_op jit(solution)/shard_map/ppermute | solution.py:90
  670.8 9.2 %collective-permute-done.90 = bf16[448,512]{1,0:T(8,128)(2,1)S(1)} collective-permute-done((bf16[448,512]{1,0:T(8,128)(2,1)S(1)}, bf16[448,512]{1,0:T(8,128)(2,1)S(1)}, u32[]{:S(2)}, u32[]{:S(2)}) %collective-permute-start.90) | collective-permute-done | bytes 458784 | tf_op jit(solution)/shard_map/ppermute | solution.py:90
  695.1 7.5 collective-permute-done.99.refs_1_
  704.2 11.4 %collective-permute-done.97 = bf16[448,512]{1,0:T(8,128)(2,1)S(1)} collective-permute-done((bf16[448,512]{1,0:T(8,128)(2,1)S(1)}, bf16[448,512]{1,0:T(8,128)(2,1)S(1)}, u32[]{:S(2)}, u32[]{:S(2)}) %collective-permute-start.97) | collective-permute-done | bytes 458784 | tf_op jit(solution)/shard_map/ppermute | solution.py:90
  717.9 6.3 place_blocks.13
  724.2 9.2 %finish_units.1 = (f32[8192,128]{1,0:T(8,128)}, f32[2,128,8192]{2,1,0:T(8,128)}) custom-call(bf16[4,1536,512]{2,1,0:T(8,128)(2,1)} %bitcast.170, bf16[4,1536,512]{2,1,0:T(8,128)(2,1)} %bitcast.171, bf16[4,1536,512]{2,1,0:T(8,128)(2,1)} %bitcast.172), custom_call_target="tpu_custom_call" | custom-call | tf_op jit(solution)/shard_map/finish_units/pallas_call | solution.py:275
  733.4 4.3 collective-permute-done.98.refs_1_
  740.1 5.1 collective-permute-done.88
  746.8 4.7 place_blocks.14
  751.6 5.3 finish_model.1
  757.4 3.8 fusion.31
  768.0 4.3 finish_late.1
  (562 shorter events, 302.9 us)
Async XLA Ops:
  11.8 35.4 %collective-permute-start = (bf16[256,2048]{1,0:T(8,128)(2,1)}, bf16[256,2048]{1,0:T(8,128)(2,1)}, u32[]{:S(2)}, u32[]{:S(2)}) collective-permute-start(bf16[256,2048]{1,0:T(8,128)(2,1)} %fusion.20), channel_id=1, source_target_pairs={{0,16},{8,24},{16,0},{24,8},{1,17},{9,25},{17,1},{25,9},{2,18},{10... | collective-permute-start | bytes 3145736 | tf_op jit(solution)/shard_map/ppermute | solution.py:90
  47.1 51.2 %collective-permute-start.1 = (bf16[256,2048]{1,0:T(8,128)(2,1)}, bf16[256,2048]{1,0:T(8,128)(2,1)}, u32[]{:S(2)}, u32[]{:S(2)}) collective-permute-start(bf16[256,2048]{1,0:T(8,128)(2,1)} %fusion.20), channel_id=1, source_target_pairs={{0,8},{8,0},{16,24},{24,16},{1,9},{9,1},{17,25},{25,17},{2,10},{10... | collective-permute-start | bytes 3145736 | tf_op jit(solution)/shard_map/ppermute | solution.py:90
  47.2 48.9 %collective-permute-start.26 = (bf16[256,2048]{1,0:T(8,128)(2,1)}, bf16[256,2048]{1,0:T(8,128)(2,1)}, u32[]{:S(2)}, u32[]{:S(2)}) collective-permute-start(bf16[256,2048]{1,0:T(8,128)(2,1)} %get-tuple-element.99.refs_0_), channel_id=1, source_target_pairs={{0,2},{2,4},{4,6},{6,7},{7,5},{5,3},{3,1},{1,0},{8,10},{10,12},{12... | collective-permute-start | bytes 3145736 | tf_op jit(solution)/shard_map/ppermute | solution.py:149
  50.3 46.4 %collective-permute-start.31 = (bf16[256,2048]{1,0:T(8,128)(2,1)}, bf16[256,2048]{1,0:T(8,128)(2,1)}, u32[]{:S(2)}, u32[]{:S(2)}) collective-permute-start(bf16[256,2048]{1,0:T(8,128)(2,1)} %get-tuple-element.99.refs_0_), channel_id=1, source_target_pairs={{2,0},{4,2},{6,4},{7,6},{5,7},{3,5},{1,3},{0,1},{10,8},{12,10},{14... | collective-permute-start | bytes 3145736 | tf_op jit(solution)/shard_map/ppermute | solution.py:149
  50.6 47.8 %collective-permute-start.2 = (bf16[256,2048]{1,0:T(8,128)(2,1)}, bf16[256,2048]{1,0:T(8,128)(2,1)}, u32[]{:S(2)}, u32[]{:S(2)}) collective-permute-start(bf16[256,2048]{1,0:T(8,128)(2,1)} %collective-permute-done), channel_id=1, source_target_pairs={{0,8},{8,0},{16,24},{24,16},{1,9},{9,1},{17,25},{25,17},{2,10},{10... | collective-permute-start | bytes 3145736 | tf_op jit(solution)/shard_map/ppermute | solution.py:90
  55.9 24.1 %collective-permute-start.19 = (bf16[256,512]{1,0:T(8,128)(2,1)}, bf16[256,512]{1,0:T(8,128)(2,1)}, u32[]{:S(2)}, u32[]{:S(2)}) collective-permute-start(bf16[256,512]{1,0:T(8,128)(2,1)} %collective-permute-done.18.refs_5_), channel_id=1, source_target_pairs={{2,0},{4,2},{6,4},{7,6},{5,7},{3,5},{1,3},{0,1},{10,8},{12,10},{14... | collective-permute-start | bytes 786440 | tf_op jit(solution)/shard_map/ppermute | solution.py:149
  91.1 83.4 %collective-permute-start.20 = (bf16[2048,512]{1,0:T(8,128)(2,1)}, bf16[2048,512]{1,0:T(8,128)(2,1)}, u32[]{:S(2)}, u32[]{:S(2)}) collective-permute-start(bf16[2048,512]{1,0:T(8,128)(2,1)} %place_blocks.9), channel_id=1, source_target_pairs={{0,16},{8,24},{16,0},{24,8},{1,17},{9,25},{17,1},{25,9},{2,18},{10... | collective-permute-start | bytes 6291464 | tf_op jit(solution)/shard_map/ppermute | solution.py:90
  96.1 50.9 %collective-permute-start.27 = (bf16[256,2048]{1,0:T(8,128)(2,1)}, bf16[256,2048]{1,0:T(8,128)(2,1)}, u32[]{:S(2)}, u32[]{:S(2)}) collective-permute-start(bf16[256,2048]{1,0:T(8,128)(2,1)} %collective-permute-done.26.refs_1_), channel_id=1, source_target_pairs={{0,2},{2,4},{4,6},{6,7},{7,5},{5,3},{3,1},{1,0},{8,10},{10,12},{12... | collective-permute-start | bytes 3145736 | tf_op jit(solution)/shard_map/ppermute | solution.py:149
  96.7 53.4 %collective-permute-start.32 = (bf16[256,2048]{1,0:T(8,128)(2,1)}, bf16[256,2048]{1,0:T(8,128)(2,1)}, u32[]{:S(2)}, u32[]{:S(2)}) collective-permute-start(bf16[256,2048]{1,0:T(8,128)(2,1)} %collective-permute-done.31.refs_7_), channel_id=1, source_target_pairs={{2,0},{4,2},{6,4},{7,6},{5,7},{3,5},{1,3},{0,1},{10,8},{12,10},{14... | collective-permute-start | bytes 3145736 | tf_op jit(solution)/shard_map/ppermute | solution.py:149
  140.6 23.3 %collective-permute-start.36 = (bf16[256,2048]{1,0:T(8,128)(2,1)S(1)}, bf16[256,2048]{1,0:T(8,128)(2,1)}, u32[]{:S(2)}, u32[]{:S(2)}) collective-permute-start(bf16[256,2048]{1,0:T(8,128)(2,1)S(1)} %copy-done.30), channel_id=1, source_target_pairs={{2,0},{4,2},{6,4},{7,6},{5,7},{3,5},{1,3},{0,1},{10,8},{12,10},{14... | collective-permute-start | bytes 3145736 | tf_op jit(solution)/shard_map/ppermute | solution.py:149
  146.7 26.1 %collective-permute-start.29 = (bf16[256,2048]{1,0:T(8,128)(2,1)S(1)}, bf16[256,2048]{1,0:T(8,128)(2,1)}, u32[]{:S(2)}, u32[]{:S(2)}) collective-permute-start(bf16[256,2048]{1,0:T(8,128)(2,1)S(1)} %copy-done.30), channel_id=1, source_target_pairs={{0,2},{2,4},{4,6},{6,7},{7,5},{5,3},{3,1},{1,0},{8,10},{10,12},{12... | collective-permute-start | bytes 3145736 | tf_op jit(solution)/shard_map/ppermute | solution.py:149
  148.5 46.8 %collective-permute-start.28 = (bf16[256,2048]{1,0:T(8,128)(2,1)}, bf16[256,2048]{1,0:T(8,128)(2,1)}, u32[]{:S(2)}, u32[]{:S(2)}) collective-permute-start(bf16[256,2048]{1,0:T(8,128)(2,1)} %collective-permute-done.27.refs_2_), channel_id=1, source_target_pairs={{0,2},{2,4},{4,6},{6,7},{7,5},{5,3},{3,1},{1,0},{8,10},{10,12},{12... | collective-permute-start | bytes 3145736 | tf_op jit(solution)/shard_map/ppermute | solution.py:149
  150.1 74.5 %collective-permute-start.21 = (bf16[2048,512]{1,0:T(8,128)(2,1)}, bf16[2048,512]{1,0:T(8,128)(2,1)}, u32[]{:S(2)}, u32[]{:S(2)}) collective-permute-start(bf16[2048,512]{1,0:T(8,128)(2,1)} %place_blocks.9), channel_id=1, source_target_pairs={{0,8},{8,0},{16,24},{24,16},{1,9},{9,1},{17,25},{25,17},{2,10},{10... | collective-permute-start | bytes 6291464 | tf_op jit(solution)/shard_map/ppermute | solution.py:90
  172.9 31.4 %collective-permute-start.37 = (bf16[256,2048]{1,0:T(8,128)(2,1)}, bf16[256,2048]{1,0:T(8,128)(2,1)}, u32[]{:S(2)}, u32[]{:S(2)}) collective-permute-start(bf16[256,2048]{1,0:T(8,128)(2,1)} %collective-permute-done.36.refs_7_), channel_id=1, source_target_pairs={{2,0},{4,2},{6,4},{7,6},{5,7},{3,5},{1,3},{0,1},{10,8},{12,10},{14... | collective-permute-start | bytes 3145736 | tf_op jit(solution)/shard_map/ppermute | solution.py:149
  174.5 43.3 %collective-permute-start.34 = (bf16[256,2048]{1,0:T(8,128)(2,1)}, bf16[256,2048]{1,0:T(8,128)(2,1)}, u32[]{:S(2)}, u32[]{:S(2)}) collective-permute-start(bf16[256,2048]{1,0:T(8,128)(2,1)} %collective-permute-done.29.refs_1_), channel_id=1, source_target_pairs={{0,2},{2,4},{4,6},{6,7},{7,5},{5,3},{3,1},{1,0},{8,10},{10,12},{12... | collective-permute-start | bytes 3145736 | tf_op jit(solution)/shard_map/ppermute | solution.py:149
  175.6 79.0 %collective-permute-start.22 = (bf16[2048,512]{1,0:T(8,128)(2,1)}, bf16[2048,512]{1,0:T(8,128)(2,1)}, u32[]{:S(2)}, u32[]{:S(2)}) collective-permute-start(bf16[2048,512]{1,0:T(8,128)(2,1)} %collective-permute-done.20), channel_id=1, source_target_pairs={{0,8},{8,0},{16,24},{24,16},{1,9},{9,1},{17,25},{25,17},{2,10},{10... | collective-permute-start | bytes 6291464 | tf_op jit(solution)/shard_map/ppermute | solution.py:90
  195.3 28.8 %collective-permute-start.33 = (bf16[256,2048]{1,0:T(8,128)(2,1)}, bf16[256,2048]{1,0:T(8,128)(2,1)}, u32[]{:S(2)}, u32[]{:S(2)}) collective-permute-start(bf16[256,2048]{1,0:T(8,128)(2,1)} %collective-permute-done.32.refs_6_), channel_id=1, source_target_pairs={{2,0},{4,2},{6,4},{7,6},{5,7},{3,5},{1,3},{0,1},{10,8},{12,10},{14... | collective-permute-start | bytes 3145736 | tf_op jit(solution)/shard_map/ppermute | solution.py:149
  204.3 48.8 %collective-permute-start.30 = (bf16[256,2048]{1,0:T(8,128)(2,1)}, bf16[256,2048]{1,0:T(8,128)(2,1)S(1)}, u32[]{:S(2)}, u32[]{:S(2)}) collective-permute-start(bf16[256,2048]{1,0:T(8,128)(2,1)} %collective-permute-done.28.refs_3_), channel_id=1, source_target_pairs={{0,2},{2,4},{4,6},{6,7},{7,5},{5,3},{3,1},{1,0},{8,10},{10,12},{12... | collective-permute-start | bytes 3145736 | tf_op jit(solution)/shard_map/ppermute | solution.py:149
  217.8 30.7 %collective-permute-start.38 = (bf16[256,2048]{1,0:T(8,128)(2,1)}, bf16[256,2048]{1,0:T(8,128)(2,1)S(1)}, u32[]{:S(2)}, u32[]{:S(2)}) collective-permute-start(bf16[256,2048]{1,0:T(8,128)(2,1)} %collective-permute-done.37.refs_6_), channel_id=1, source_target_pairs={{2,0},{4,2},{6,4},{7,6},{5,7},{3,5},{1,3},{0,1},{10,8},{12,10},{14... | collective-permute-start | bytes 3145736 | tf_op jit(solution)/shard_map/ppermute | solution.py:149
  224.2 27.2 %collective-permute-start.43 = (bf16[128,2048]{1,0:T(8,128)(2,1)S(1)}, bf16[128,2048]{1,0:T(8,128)(2,1)S(1)}, u32[]{:S(2)}, u32[]{:S(2)}) collective-permute-start(bf16[128,2048]{1,0:T(8,128)(2,1)S(1)} %copy-done.21), channel_id=1, source_target_pairs={{0,2},{2,4},{4,6},{6,7},{7,5},{5,3},{3,1},{1,0},{8,10},{10,12},{12... | collective-permute-start | bytes 1572872 | tf_op jit(solution)/shard_map/ppermute | solution.py:149
  224.6 23.6 %collective-permute-start.48 = (bf16[128,2048]{1,0:T(8,128)(2,1)S(1)}, bf16[128,2048]{1,0:T(8,128)(2,1)S(1)}, u32[]{:S(2)}, u32[]{:S(2)}) collective-permute-start(bf16[128,2048]{1,0:T(8,128)(2,1)S(1)} %copy-done.21), channel_id=1, source_target_pairs={{2,0},{4,2},{6,4},{7,6},{5,7},{3,5},{1,3},{0,1},{10,8},{12,10},{14... | collective-permute-start | bytes 1572872 | tf_op jit(solution)/shard_map/ppermute | solution.py:149
  248.2 50.9 %collective-permute-start.40 = (bf16[256,2048]{1,0:T(8,128)(2,1)}, bf16[256,2048]{1,0:T(8,128)(2,1)}, u32[]{:S(2)}, u32[]{:S(2)}) collective-permute-start(bf16[256,2048]{1,0:T(8,128)(2,1)} %bitcast.27), channel_id=1, source_target_pairs={{0,16},{8,24},{16,0},{24,8},{1,17},{9,25},{17,1},{25,9},{2,18},{10... | collective-permute-start | bytes 3145736 | tf_op jit(solution)/shard_map/ppermute | solution.py:90
  248.5 26.2 %collective-permute-start.35 = (bf16[256,2048]{1,0:T(8,128)(2,1)}, bf16[256,2048]{1,0:T(8,128)(2,1)S(1)}, u32[]{:S(2)}, u32[]{:S(2)}) collective-permute-start(bf16[256,2048]{1,0:T(8,128)(2,1)} %collective-permute-done.34.refs_2_), channel_id=1, source_target_pairs={{0,2},{2,4},{4,6},{6,7},{7,5},{5,3},{3,1},{1,0},{8,10},{10,12},{12... | collective-permute-start | bytes 3145736 | tf_op jit(solution)/shard_map/ppermute | solution.py:149
  253.1 61.2 %collective-permute-start.39 = (bf16[256,2048]{1,0:T(8,128)(2,1)S(1)}, bf16[256,2048]{1,0:T(8,128)(2,1)S(1)}, u32[]{:S(2)}, u32[]{:S(2)}) collective-permute-start(bf16[256,2048]{1,0:T(8,128)(2,1)S(1)} %collective-permute-done.38.refs_5_), channel_id=1, source_target_pairs={{2,0},{4,2},{6,4},{7,6},{5,7},{3,5},{1,3},{0,1},{10,8},{12,10},{14... | collective-permute-start | bytes 3145736 | tf_op jit(solution)/shard_map/ppermute | solution.py:149
  254.6 42.7 %collective-permute-start.44 = (bf16[128,2048]{1,0:T(8,128)(2,1)S(1)}, bf16[128,2048]{1,0:T(8,128)(2,1)S(1)}, u32[]{:S(2)}, u32[]{:S(2)}) collective-permute-start(bf16[128,2048]{1,0:T(8,128)(2,1)S(1)} %collective-permute-done.43.refs_1_), channel_id=1, source_target_pairs={{0,2},{2,4},{4,6},{6,7},{7,5},{5,3},{3,1},{1,0},{8,10},{10,12},{12... | collective-permute-start | bytes 1572872 | tf_op jit(solution)/shard_map/ppermute | solution.py:149
  266.2 30.8 %collective-permute-start.49 = (bf16[128,2048]{1,0:T(8,128)(2,1)S(1)}, bf16[128,2048]{1,0:T(8,128)(2,1)}, u32[]{:S(2)}, u32[]{:S(2)}) collective-permute-start(bf16[128,2048]{1,0:T(8,128)(2,1)S(1)} %collective-permute-done.48.refs_7_), channel_id=1, source_target_pairs={{2,0},{4,2},{6,4},{7,6},{5,7},{3,5},{1,3},{0,1},{10,8},{12,10},{14... | collective-permute-start | bytes 1572872 | tf_op jit(solution)/shard_map/ppermute | solution.py:149
  274.8 41.2 %collective-permute-start.23 = (bf16[256,2048]{1,0:T(8,128)(2,1)}, bf16[256,2048]{1,0:T(8,128)(2,1)}, u32[]{:S(2)}, u32[]{:S(2)}) collective-permute-start(bf16[256,2048]{1,0:T(8,128)(2,1)} %multiply_convert_fusion.4), channel_id=1, source_target_pairs={{0,16},{8,24},{16,0},{24,8},{1,17},{9,25},{17,1},{25,9},{2,18},{10... | collective-permute-start | bytes 3145736 | tf_op jit(solution)/shard_map/ppermute | solution.py:90
  306.2 29.7 %collective-permute-start.41 = (bf16[256,2048]{1,0:T(8,128)(2,1)}, bf16[256,2048]{1,0:T(8,128)(2,1)}, u32[]{:S(2)}, u32[]{:S(2)}) collective-permute-start(bf16[256,2048]{1,0:T(8,128)(2,1)} %bitcast.27), channel_id=1, source_target_pairs={{0,8},{8,0},{16,24},{24,16},{1,9},{9,1},{17,25},{25,17},{2,10},{10... | collective-permute-start | bytes 3145736 | tf_op jit(solution)/shard_map/ppermute | solution.py:90
  306.6 31.1 %collective-permute-start.42 = (bf16[256,2048]{1,0:T(8,128)(2,1)}, bf16[256,2048]{1,0:T(8,128)(2,1)}, u32[]{:S(2)}, u32[]{:S(2)}) collective-permute-start(bf16[256,2048]{1,0:T(8,128)(2,1)} %collective-permute-done.40), channel_id=1, source_target_pairs={{0,8},{8,0},{16,24},{24,16},{1,9},{9,1},{17,25},{25,17},{2,10},{10... | collective-permute-start | bytes 3145736 | tf_op jit(solution)/shard_map/ppermute | solution.py:90
  323.1 44.9 %collective-permute-start.24 = (bf16[256,2048]{1,0:T(8,128)(2,1)}, bf16[256,2048]{1,0:T(8,128)(2,1)}, u32[]{:S(2)}, u32[]{:S(2)}) collective-permute-start(bf16[256,2048]{1,0:T(8,128)(2,1)} %multiply_convert_fusion.4), channel_id=1, source_target_pairs={{0,8},{8,0},{16,24},{24,16},{1,9},{9,1},{17,25},{25,17},{2,10},{10... | collective-permute-start | bytes 3145736 | tf_op jit(solution)/shard_map/ppermute | solution.py:90
  326.8 41.3 %collective-permute-start.25 = (bf16[256,2048]{1,0:T(8,128)(2,1)}, bf16[256,2048]{1,0:T(8,128)(2,1)}, u32[]{:S(2)}, u32[]{:S(2)}) collective-permute-start(bf16[256,2048]{1,0:T(8,128)(2,1)} %collective-permute-done.23), channel_id=1, source_target_pairs={{0,8},{8,0},{16,24},{24,16},{1,9},{9,1},{17,25},{25,17},{2,10},{10... | collective-permute-start | bytes 3145736 | tf_op jit(solution)/shard_map/ppermute | solution.py:90
  333.5 26.4 %collective-permute-start.47 = (bf16[128,2048]{1,0:T(8,128)(2,1)S(1)}, bf16[128,2048]{1,0:T(8,128)(2,1)S(1)}, u32[]{:S(2)}, u32[]{:S(2)}) collective-permute-start(bf16[128,2048]{1,0:T(8,128)(2,1)S(1)} %copy-done.54), channel_id=1, source_target_pairs={{0,2},{2,4},{4,6},{6,7},{7,5},{5,3},{3,1},{1,0},{8,10},{10,12},{12... | collective-permute-start | bytes 1572872 | tf_op jit(solution)/shard_map/ppermute | solution.py:149
  335.9 24.1 %collective-permute-start.52 = (bf16[128,2048]{1,0:T(8,128)(2,1)S(1)}, bf16[128,2048]{1,0:T(8,128)(2,1)}, u32[]{:S(2)}, u32[]{:S(2)}) collective-permute-start(bf16[128,2048]{1,0:T(8,128)(2,1)S(1)} %copy-done.56), channel_id=1, source_target_pairs={{0,2},{2,4},{4,6},{6,7},{7,5},{5,3},{3,1},{1,0},{8,10},{10,12},{12... | collective-permute-start | bytes 1572872 | tf_op jit(solution)/shard_map/ppermute | solution.py:149
  337.7 22.3 %collective-permute-start.56 = (bf16[128,2048]{1,0:T(8,128)(2,1)S(1)}, bf16[128,2048]{1,0:T(8,128)(2,1)}, u32[]{:S(2)}, u32[]{:S(2)}) collective-permute-start(bf16[128,2048]{1,0:T(8,128)(2,1)S(1)} %copy-done.58), channel_id=1, source_target_pairs={{2,0},{4,2},{6,4},{7,6},{5,7},{3,5},{1,3},{0,1},{10,8},{12,10},{14... | collective-permute-start | bytes 1572872 | tf_op jit(solution)/shard_map/ppermute | solution.py:149
  463.0 29.5 %collective-permute-start.59 = (bf16[512,2048]{1,0:T(8,128)(2,1)}, bf16[512,2048]{1,0:T(8,128)(2,1)S(1)}, u32[]{:S(2)}, u32[]{:S(2)}) collective-permute-start(bf16[512,2048]{1,0:T(8,128)(2,1)} %get-tuple-element.124), channel_id=1, source_target_pairs={{0,8},{8,0},{16,24},{24,16},{1,9},{9,1},{17,25},{25,17},{2,10},{10... | collective-permute-start | bytes 6291464 | tf_op jit(solution)/shard_map/ppermute | solution.py:90
  491.8 46.3 %collective-permute-start.58 = (bf16[256,2048]{1,0:T(8,128)(2,1)S(1)}, bf16[256,2048]{1,0:T(8,128)(2,1)S(1)}, u32[]{:S(2)}, u32[]{:S(2)}) collective-permute-start(bf16[256,2048]{1,0:T(8,128)(2,1)S(1)} %get-tuple-element.168), channel_id=1, source_target_pairs={{0,8},{8,0},{16,24},{24,16},{1,9},{9,1},{17,25},{25,17},{2,10},{10... | collective-permute-start | bytes 3145736 | tf_op jit(solution)/shard_map/ppermute | solution.py:90
  493.4 25.2 %collective-permute-start.60 = (bf16[256,2048]{1,0:T(8,128)(2,1)S(1)}, bf16[256,2048]{1,0:T(8,128)(2,1)S(1)}, u32[]{:S(2)}, u32[]{:S(2)}) collective-permute-start(bf16[256,2048]{1,0:T(8,128)(2,1)S(1)} %slice.414), channel_id=1, source_target_pairs={{0,16},{8,24},{16,0},{24,8},{1,17},{9,25},{17,1},{25,9},{2,18},{10... | collective-permute-start | bytes 3145736 | tf_op jit(solution)/shard_map/ppermute | solution.py:90
  542.7 44.5 %collective-permute-start.57 = (bf16[256,2048]{1,0:T(8,128)(2,1)}, bf16[256,2048]{1,0:T(8,128)(2,1)}, u32[]{:S(2)}, u32[]{:S(2)}) collective-permute-start(bf16[256,2048]{1,0:T(8,128)(2,1)} %get-tuple-element.167), channel_id=1, source_target_pairs={{0,8},{8,0},{16,24},{24,16},{1,9},{9,1},{17,25},{25,17},{2,10},{10... | collective-permute-start | bytes 3145736 | tf_op jit(solution)/shard_map/ppermute | solution.py:90
  542.7 34.0 %collective-permute-start.68 = (bf16[640,512]{1,0:T(8,128)(2,1)S(1)}, bf16[640,512]{1,0:T(8,128)(2,1)}, u32[]{:S(2)}, u32[]{:S(2)}) collective-permute-start(bf16[640,512]{1,0:T(8,128)(2,1)S(1)} %get-tuple-element.165), channel_id=1, source_target_pairs={{0,8},{8,0},{16,24},{24,16},{1,9},{9,1},{17,25},{25,17},{2,10},{10... | collective-permute-start | bytes 1966088 | tf_op jit(solution)/shard_map/ppermute | solution.py:90
  545.2 42.0 %collective-permute-start.66 = (bf16[256,2048]{1,0:T(8,128)(2,1)}, bf16[256,2048]{1,0:T(8,128)(2,1)}, u32[]{:S(2)}, u32[]{:S(2)}) collective-permute-start(bf16[256,2048]{1,0:T(8,128)(2,1)} %fusion.23), channel_id=1, source_target_pairs={{0,16},{8,24},{16,0},{24,8},{1,17},{9,25},{17,1},{25,9},{2,18},{10... | collective-permute-start | bytes 3145736 | tf_op jit(solution)/shard_map/ppermute | solution.py:90
  548.0 37.1 %collective-permute-start.70 = (bf16[640,512]{1,0:T(8,128)(2,1)}, bf16[640,512]{1,0:T(8,128)(2,1)}, u32[]{:S(2)}, u32[]{:S(2)}) collective-permute-start(bf16[640,512]{1,0:T(8,128)(2,1)} %add_convert_fusion.2), channel_id=1, source_target_pairs={{0,16},{8,24},{16,0},{24,8},{1,17},{9,25},{17,1},{25,9},{2,18},{10... | collective-permute-start | bytes 1966088 | tf_op jit(solution)/shard_map/ppermute | solution.py:90
  548.4 28.1 %collective-permute-start.67 = (bf16[192,512]{1,0:T(8,128)(2,1)S(1)}, bf16[192,512]{1,0:T(8,128)(2,1)S(1)}, u32[]{:S(2)}, u32[]{:S(2)}) collective-permute-start(bf16[192,512]{1,0:T(8,128)(2,1)S(1)} %constant_dynamic-slice_fusion.9), channel_id=1, source_target_pairs={{0,4},{1,5},{2,6},{3,7},{4,0},{5,1},{6,2},{7,3},{8,12},{9,13},{10,... | collective-permute-start | bytes 589832 | tf_op jit(solution)/shard_map/ppermute | solution.py:90
  631.5 25.5 %collective-permute-start.79 = (bf16[256,2048]{1,0:T(8,128)(2,1)S(1)}, bf16[256,2048]{1,0:T(8,128)(2,1)S(1)}, u32[]{:S(2)}, u32[]{:S(2)}) collective-permute-start(bf16[256,2048]{1,0:T(8,128)(2,1)S(1)} %slice.413), channel_id=1, source_target_pairs={{0,16},{8,24},{16,0},{24,8},{1,17},{9,25},{17,1},{25,9},{2,18},{10... | collective-permute-start | bytes 3145736 | tf_op jit(solution)/shard_map/ppermute | solution.py:90
  637.6 26.1 %collective-permute-start.87 = (bf16[768,512]{1,0:T(8,128)(2,1)S(1)}, bf16[768,512]{1,0:T(8,128)(2,1)S(1)}, u32[]{:S(2)}, u32[]{:S(2)}) collective-permute-start(bf16[768,512]{1,0:T(8,128)(2,1)S(1)} %pad_maximum_fusion.11), channel_id=1, source_target_pairs={{0,1},{1,0},{2,3},{3,2},{4,5},{5,4},{6,7},{7,6},{8,9},{9,8},{10,11... | collective-permute-start | bytes 2359304 | tf_op jit(solution)/shard_map/ppermute | solution.py:90
  667.5 35.2 %collective-permute-start.99 = (bf16[1536,512]{1,0:T(8,128)(2,1)}, bf16[1536,512]{1,0:T(8,128)(2,1)}, u32[]{:S(2)}, u32[]{:S(2)}) collective-permute-start(bf16[1536,512]{1,0:T(8,128)(2,1)} %pad_maximum_fusion.4.refs_0_), channel_id=1, source_target_pairs={{0,16},{8,24},{16,0},{24,8},{1,17},{9,25},{17,1},{25,9},{2,18},{10... | collective-permute-start | bytes 4718600 | tf_op jit(solution)/shard_map/ppermute | solution.py:90
  695.1 22.8 %collective-permute-start.100 = (bf16[1536,512]{1,0:T(8,128)(2,1)}, bf16[1536,512]{1,0:T(8,128)(2,1)}, u32[]{:S(2)}, u32[]{:S(2)}) collective-permute-start(bf16[1536,512]{1,0:T(8,128)(2,1)} %pad_maximum_fusion.4.refs_0_), channel_id=1, source_target_pairs={{0,8},{8,0},{16,24},{24,16},{1,9},{9,1},{17,25},{25,17},{2,10},{10... | collective-permute-start | bytes 4718600 | tf_op jit(solution)/shard_map/ppermute | solution.py:90
  715.7 22.0 %collective-permute-start.98 = (bf16[896,512]{1,0:T(8,128)(2,1)S(1)}, bf16[896,512]{1,0:T(8,128)(2,1)S(1)}, u32[]{:S(2)}, u32[]{:S(2)}) collective-permute-start(bf16[896,512]{1,0:T(8,128)(2,1)S(1)} %constant_dynamic-update-slice_fusion.2.refs_0_), channel_id=1, source_target_pairs={{0,16},{8,24},{16,0},{24,8},{1,17},{9,25},{17,1},{25,9},{2,18},{10... | collective-permute-start | bytes 2752520 | tf_op jit(solution)/shard_map/ppermute | solution.py:90
  717.8 29.0 %collective-permute-start.102 = (bf16[896,512]{1,0:T(8,128)(2,1)S(1)}, bf16[896,512]{1,0:T(8,128)(2,1)}, u32[]{:S(2)}, u32[]{:S(2)}) collective-permute-start(bf16[896,512]{1,0:T(8,128)(2,1)S(1)} %constant_dynamic-update-slice_fusion.2.refs_0_), channel_id=1, source_target_pairs={{0,8},{8,0},{16,24},{24,16},{1,9},{9,1},{17,25},{25,17},{2,10},{10... | collective-permute-start | bytes 2752520 | tf_op jit(solution)/shard_map/ppermute | solution.py:90
  (161 other events, 2299.2 us)

commit v5 on v4

--- a/solution.py
+++ b/solution.py
@@ -125,7 +125,7 @@
 
 
 class Rings:
-    WINDOW = 3
+    WINDOW = 4
 
     def __init__(self):
         self.count = lax.axis_size("fsdp")

time: 780 us -> 775 us (level)
    ppermute x42, waiting for transfers between devices: 148 us -> 135 us  [send(): got = lax.ppermute(block, 'fsdp', self.perms[way])]
    ppermute x64, waiting for transfers between devices: 112 us -> 122 us  [swap(): return lax.ppermute(block, axis, [(i, i ^ offset) for i in range(count)])]
    unnamed x225 -> x217, local copies, waits for them, and re-layouts: 13.4 us -> 18.3 us
  transfers between devices with their start and end apart: 106 -> 106, of which waited for: 43 -> 40; matrix products, arithmetic and copies ran while one was open for 21% -> 22% of each run, Pallas kernels for 16% -> 16%
where the time goes in v5:
time: 775 us; the launch traced here: 767 us
  waiting for transfers between devices  257 us (33%)
  Pallas kernels  174 us (22%)
  matrix products  120 us (15%)
  starting transfers between devices  97.3 us (13%)
  local copies, waits for them, and re-layouts  65.3 us (8%)
  other arithmetic  51.4 us (7%)
    ppermute x42, waiting for transfers between devices, send(): got = lax.ppermute(block, 'fsdp', self.perms[way])  135 us
    ppermute x64, waiting for transfers between devices, swap(): return lax.ppermute(block, axis, [(i, i ^ offset) for i in range(count)])  122 us
    dot_general x19, matrix products, mm(): return jnp.dot(left, right, preferred_element_type=F32)  85 us
    ppermute x64, starting transfers between devices, swap(): return lax.ppermute(block, axis, [(i, i ^ offset) for i in range(count)])  49.6 us
    ppermute x42, starting transfers between devices, send(): got = lax.ppermute(block, 'fsdp', self.perms[way])  47.7 us
    pallas_call x8, Pallas kernels, place_blocks(): pl.pallas_call(body, out_shape=jax.ShapeDtypeStruct((rows * total, column...  42.3 us
    pallas_call x2, Pallas kernels, sum_products(): pl.pallas_call(body, grid=(outs // tile,), in_specs=[pl.BlockSpec(a.shape...  34.5 us
    pallas_call x1, Pallas kernels, attend_backward(): pl.pallas_call(lambda *refs: backward_body(blocks, groups, *refs), grid_s...  24.9 us
  transfers between devices with their start and end apart: 106, of which 40 were waited for; matrix products, arithmetic and copies ran while one was open for 22% of the time, Pallas kernels for 16%

profile of v5, /device:TPU:0, one launch (start us, length us, event | category | flops | bytes accessed | tf_op | source)
XLA Modules:
  0.0 767.4 jit_solution(9566842018275850668)
XLA Ops:
  14.7 7.5 collective-permute-done.16.refs_7_
  34.4 4.5 collective-permute-done.18.refs_5_
  49.1 5.8 take_units.2
  84.7 7.0 collective-permute-done.11.refs_5_
  127.1 23.0 %attend_forward.1 = (bf16[1024,512]{1,0:T(8,128)(2,1)}, bf16[1024,256]{1,0:T(8,128)(2,1)}, bf16[1024,256]{1,0:T(8,128)(2,1)}, bf16[1024,512]{1,0:T(8,128)(2,1)}, f32[4,2,1024]{2,1,0:T(2,128)}) custom-call(s32[4]{0:T(128)} %pad_add_fusion.refs_0_, f32[1024,512]{1,0:T(8,128)} %slice_add_fusion.4.refs_1_, f32[1024,256]{1,0:T(8,128)} %pad_maximum_fusion.5.refs_2_, ...), custom_call_target="tpu_custom_call" | custom-call | flops 2147483648 | bytes 16777216 | tf_op jit(solution)/shard_map/attend_forward/pallas_call | solution.py:486
  153.7 5.9 collective-permute-done.12
  160.9 7.0 collective-permute-done.14
  179.0 14.1 %collective-permute-done.37.refs_6_ = bf16[256,2048]{1,0:T(8,128)(2,1)} collective-permute-done((bf16[256,2048]{1,0:T(8,128)(2,1)}, bf16[256,2048]{1,0:T(8,128)(2,1)}, u32[]{:S(2)}, u32[]{:S(2)}) %collective-permute-start.37) | collective-permute-done | bytes 1048608 | tf_op jit(solution)/shard_map/ppermute | solution.py:149
  200.5 15.8 %collective-permute-done.28.refs_3_ = bf16[256,2048]{1,0:T(8,128)(2,1)} collective-permute-done((bf16[256,2048]{1,0:T(8,128)(2,1)}, bf16[256,2048]{1,0:T(8,128)(2,1)}, u32[]{:S(2)}, u32[]{:S(2)}) %collective-permute-start.28) | collective-permute-done | bytes 1048608 | tf_op jit(solution)/shard_map/ppermute | solution.py:149
  225.3 14.5 %collective-permute-done.38.refs_5_ = bf16[256,2048]{1,0:T(8,128)(2,1)S(1)} collective-permute-done((bf16[256,2048]{1,0:T(8,128)(2,1)}, bf16[256,2048]{1,0:T(8,128)(2,1)S(1)}, u32[]{:S(2)}, u32[]{:S(2)}) %collective-permute-start.38) | collective-permute-done | bytes 1048608 | tf_op jit(solution)/shard_map/ppermute | solution.py:149
  246.9 7.8 %collective-permute-done.47.refs_7_ = bf16[128,2048]{1,0:T(8,128)(2,1)S(1)} collective-permute-done((bf16[128,2048]{1,0:T(8,128)(2,1)S(1)}, bf16[128,2048]{1,0:T(8,128)(2,1)S(1)}, u32[]{:S(2)}, u32[]{:S(2)}) %collective-permute-start.47) | collective-permute-done | bytes 524320 | tf_op jit(solution)/shard_map/ppermute | solution.py:149
  258.0 18.1 %collective-permute-done.29.refs_4_ = bf16[256,2048]{1,0:T(8,128)(2,1)S(1)} collective-permute-done((bf16[256,2048]{1,0:T(8,128)(2,1)}, bf16[256,2048]{1,0:T(8,128)(2,1)S(1)}, u32[]{:S(2)}, u32[]{:S(2)}) %collective-permute-start.29) | collective-permute-done | bytes 1048608 | tf_op jit(solution)/shard_map/ppermute | solution.py:149
  276.6 9.0 %collective-permute-done.53.refs_15_ = bf16[128,2048]{1,0:T(8,128)(2,1)S(1)} collective-permute-done((bf16[128,2048]{1,0:T(8,128)(2,1)S(1)}, bf16[128,2048]{1,0:T(8,128)(2,1)S(1)}, u32[]{:S(2)}, u32[]{:S(2)}) %collective-permute-start.53) | collective-permute-done | bytes 524320 | tf_op jit(solution)/shard_map/ppermute | solution.py:149
  289.7 10.8 %collective-permute-done.48.refs_6_ = bf16[128,2048]{1,0:T(8,128)(2,1)} collective-permute-done((bf16[128,2048]{1,0:T(8,128)(2,1)S(1)}, bf16[128,2048]{1,0:T(8,128)(2,1)}, u32[]{:S(2)}, u32[]{:S(2)}) %collective-permute-start.48) | collective-permute-done | bytes 524320 | tf_op jit(solution)/shard_map/ppermute | solution.py:149
  301.1 7.0 collective-permute-done.54.refs_14_
  315.0 4.6 collective-permute-done.51.refs_10_
  319.6 5.1 collective-permute-done.55.refs_13_
  326.1 5.3 take_units.3
  343.2 7.1 place_blocks.10.refs_3_
  350.3 7.1 place_blocks.11.refs_4_
  358.3 7.3 place_blocks.12.down_ref
  370.3 4.5 fusion.52
  374.8 14.6 %convolution_add_fusion.2.gate_ref = f32[1024,2048]{1,0:T(8,128)} fusion(f32[1024,2048]{1,0:T(8,128)S(1)} %fusion.55, bf16[2048,2048]{1,0:T(8,128)(2,1)} %place_blocks.10.refs_3_, bf16[256,2048]{1,0:T(8,128)(2,1)} %collective-permute-done.25, bf16[256,2048]{1,0:T(8,128)(2,1)} %collective-permute-done.24, bf16[256,2048]{1,0:T(8,128)(2,1)} %collective-permute-done.23, ...), kind=kOutput, calls=%fused_computation.22 | convolution fusion | flops 8608808960 | bytes 29360128 | tf_op jit(solution)/shard_map/dot_general | solution.py:32
  389.4 20.2 %multiply_convert_fusion.1 = (bf16[1024,2048]{1,0:T(8,128)(2,1)}, f32[1024,2048]{1,0:T(8,128)}) fusion(f32[1024,2048]{1,0:T(8,128)} %convolution_add_fusion.2.gate_ref, f32[1024,2048]{1,0:T(8,128)} %fusion.52, bf16[2048,2048]{1,0:T(8,128)(2,1)} %place_blocks.11.refs_4_, bf16[256,2048]{1,0:T(8,128)(2,1)} %collective-permute-done.25, ...), kind=kOutput, calls=%fused_computation.9 | convolution fusion | flops 8621391872 | bytes 41943040 | tf_op jit(solution)/shard_map/dot_general | solution.py:32
  409.6 19.4 %gate_grads.1 = (bf16[1024,2048]{1,0:T(8,128)(2,1)}, bf16[1024,2048]{1,0:T(8,128)(2,1)}) custom-call(bf16[1024,2048]{1,0:T(8,128)(2,1)} %copy-done.6, bf16[2048,2048]{1,0:T(8,128)(2,1)} %place_blocks.12.down_ref, bf16[1024,128]{1,0:T(8,128)(2,1)} %fusion.27.gl_ref, bf16[2048,128]{1,0:T(8,128)(2,1)} %bitcast.187, ...), custom_call_target="tpu_custom_call" | custom-call | flops 8589934592 | bytes 33554432 | tf_op jit(solution)/shard_map/gate_grads/pallas_call | solution.py:556
  434.8 25.7 %sum_products.2 = (bf16[512,2048]{1,0:T(8,128)(2,1)}, bf16[512,2048]{1,0:T(8,128)(2,1)}) custom-call(bf16[1024,2048]{1,0:T(8,128)(2,1)} %get-tuple-element.122.refs_0_, bf16[1024,2048]{1,0:T(8,128)(2,1)} %get-tuple-element.123.refs_1_, bf16[1024,256]{1,0:T(8,128)(2,1)} %bitcast_multiply_fusion.refs_2_, bf16[2048,2048]{1,0:T(8,128)(2,1)} %place_blocks.10.refs_3_, ...), custom_call_target="tpu_custom_call" | custom-call | flops 18253611008 | bytes 30932992 | tf_op jit(solution)/shard_map/sum_products/pallas_call | solution.py:584
  473.0 13.5 %fusion.125 = (bf16[1024,2048]{1,0:T(8,128)(2,1)}, f32[1024,2048]{1,0:T(8,128)}) fusion(f32[1024,2048]{1,0:T(8,128)S(1)} %fusion.43, bf16[1024,2048]{1,0:T(8,128)(2,1)} %get-tuple-element.124, bf16[2048,2048]{1,0:T(8,128)(2,1)S(1)} %bitcast.177), kind=kOutput, calls=%fused_computation.278 | convolution fusion | flops 8594128896 | bytes 33554432 | tf_op jit(solution)/shard_map/dot_general | solution.py:32
  496.6 12.9 %collective-permute-done.61 = bf16[768,512]{1,0:T(8,128)(2,1)S(1)} collective-permute-done((bf16[768,512]{1,0:T(8,128)(2,1)S(1)}, bf16[768,512]{1,0:T(8,128)(2,1)S(1)}, u32[]{:S(2)}, u32[]{:S(2)}) %collective-permute-start.61) | collective-permute-done | bytes 786464 | tf_op jit(solution)/shard_map/ppermute | solution.py:90
  509.7 6.4 collective-permute-done.60
  523.6 4.8 fusion.12
  535.1 4.5 fusion.23
  547.5 24.9 %attend_backward.1.refs_0_ = bf16[1024,768]{1,0:T(8,128)(2,1)} custom-call(s32[4]{0:T(128)} %pad_add_fusion.refs_0_, bf16[1024,512]{1,0:T(8,128)(2,1)} %get-tuple-element.130.refs_1_, bf16[1024,256]{1,0:T(8,128)(2,1)} %get-tuple-element.131.refs_2_, bf16[1024,256]{1,0:T(8,128)(2,1)} %get-tuple-element.132.refs_3_, ...), custom_call_target="tpu_custom_call" | custom-call | tf_op jit(solution)/shard_map/attend_backward/pallas_call | solution.py:517
  572.4 10.2 %collective-permute-done.70 = bf16[640,512]{1,0:T(8,128)(2,1)} collective-permute-done((bf16[640,512]{1,0:T(8,128)(2,1)}, bf16[640,512]{1,0:T(8,128)(2,1)}, u32[]{:S(2)}, u32[]{:S(2)}) %collective-permute-start.70) | collective-permute-done | bytes 655392 | tf_op jit(solution)/shard_map/ppermute | solution.py:90
  584.7 4.0 fusion.30
  595.2 9.5 %collective-permute-done.73 = bf16[192,512]{1,0:T(8,128)(2,1)S(1)} collective-permute-done((bf16[192,512]{1,0:T(8,128)(2,1)S(1)}, bf16[192,512]{1,0:T(8,128)(2,1)S(1)}, u32[]{:S(2)}, u32[]{:S(2)}) %collective-permute-start.73) | collective-permute-done | bytes 196640 | tf_op jit(solution)/shard_map/ppermute | solution.py:90
  605.8 5.4 collective-permute-done.74
  611.3 8.7 %sum_products.3 = (bf16[512,2048]{1,0:T(8,128)(2,1)}, bf16[512,2048]{1,0:T(8,128)(2,1)}) custom-call(bf16[1024,768]{1,0:T(8,128)(2,1)} %attend_backward.1.refs_0_, bf16[2048,768]{1,0:T(8,128)(2,1)} %place_blocks.8.refs_1_), custom_call_target="tpu_custom_call" | custom-call | flops 3221225472 | bytes 8912896 | tf_op jit(solution)/shard_map/sum_products/pallas_call | solution.py:584
  637.9 15.8 %collective-permute-done.79 = bf16[256,2048]{1,0:T(8,128)(2,1)S(1)} collective-permute-done((bf16[256,2048]{1,0:T(8,128)(2,1)S(1)}, bf16[256,2048]{1,0:T(8,128)(2,1)S(1)}, u32[]{:S(2)}, u32[]{:S(2)}) %collective-permute-start.79) | collective-permute-done | bytes 1048608 | tf_op jit(solution)/shard_map/ppermute | solution.py:90
  666.7 8.4 %collective-permute-done.90 = bf16[448,512]{1,0:T(8,128)(2,1)S(1)} collective-permute-done((bf16[448,512]{1,0:T(8,128)(2,1)S(1)}, bf16[448,512]{1,0:T(8,128)(2,1)S(1)}, u32[]{:S(2)}, u32[]{:S(2)}) %collective-permute-start.90) | collective-permute-done | bytes 458784 | tf_op jit(solution)/shard_map/ppermute | solution.py:90
  690.9 7.2 collective-permute-done.99.refs_1_
  699.7 11.4 %collective-permute-done.97 = bf16[448,512]{1,0:T(8,128)(2,1)S(1)} collective-permute-done((bf16[448,512]{1,0:T(8,128)(2,1)S(1)}, bf16[448,512]{1,0:T(8,128)(2,1)S(1)}, u32[]{:S(2)}, u32[]{:S(2)}) %collective-permute-start.97) | collective-permute-done | bytes 458784 | tf_op jit(solution)/shard_map/ppermute | solution.py:90
  712.9 6.3 place_blocks.13
  719.2 9.2 %finish_units.1 = (f32[8192,128]{1,0:T(8,128)}, f32[2,128,8192]{2,1,0:T(8,128)}) custom-call(bf16[4,1536,512]{2,1,0:T(8,128)(2,1)} %bitcast.170, bf16[4,1536,512]{2,1,0:T(8,128)(2,1)} %bitcast.171, bf16[4,1536,512]{2,1,0:T(8,128)(2,1)} %bitcast.172), custom_call_target="tpu_custom_call" | custom-call | tf_op jit(solution)/shard_map/finish_units/pallas_call | solution.py:275
  728.4 4.8 collective-permute-done.98.refs_1_
  735.6 5.1 collective-permute-done.88
  741.9 4.7 place_blocks.14
  746.6 5.3 finish_model.1
  763.0 4.3 finish_late.1
  (554 shorter events, 298.5 us)
Async XLA Ops:
  5.9 24.9 %collective-permute-start.9 = (bf16[256,768]{1,0:T(8,128)(2,1)S(1)}, bf16[256,768]{1,0:T(8,128)(2,1)}, u32[]{:S(2)}, u32[]{:S(2)}) collective-permute-start(bf16[256,768]{1,0:T(8,128)(2,1)S(1)} %pad_maximum_fusion.15.refs_0_), channel_id=1, source_target_pairs={{2,0},{4,2},{6,4},{7,6},{5,7},{3,5},{1,3},{0,1},{10,8},{12,10},{14... | collective-permute-start | bytes 1179656 | tf_op jit(solution)/shard_map/ppermute | solution.py:149
  11.8 44.4 %collective-permute-start = (bf16[256,2048]{1,0:T(8,128)(2,1)}, bf16[256,2048]{1,0:T(8,128)(2,1)}, u32[]{:S(2)}, u32[]{:S(2)}) collective-permute-start(bf16[256,2048]{1,0:T(8,128)(2,1)} %fusion.20), channel_id=1, source_target_pairs={{0,16},{8,24},{16,0},{24,8},{1,17},{9,25},{17,1},{25,9},{2,18},{10... | collective-permute-start | bytes 3145736 | tf_op jit(solution)/shard_map/ppermute | solution.py:90
  30.8 25.3 %collective-permute-start.10 = (bf16[256,768]{1,0:T(8,128)(2,1)}, bf16[256,768]{1,0:T(8,128)(2,1)}, u32[]{:S(2)}, u32[]{:S(2)}) collective-permute-start(bf16[256,768]{1,0:T(8,128)(2,1)} %collective-permute-done.9.refs_7_), channel_id=1, source_target_pairs={{2,0},{4,2},{6,4},{7,6},{5,7},{3,5},{1,3},{0,1},{10,8},{12,10},{14... | collective-permute-start | bytes 1179656 | tf_op jit(solution)/shard_map/ppermute | solution.py:149
  33.0 24.8 %collective-permute-start.15 = (bf16[256,512]{1,0:T(8,128)(2,1)}, bf16[256,512]{1,0:T(8,128)(2,1)S(1)}, u32[]{:S(2)}, u32[]{:S(2)}) collective-permute-start(bf16[256,512]{1,0:T(8,128)(2,1)} %collective-permute-done.7.refs_2_), channel_id=1, source_target_pairs={{0,2},{2,4},{4,6},{6,7},{7,5},{5,3},{3,1},{1,0},{8,10},{10,12},{12... | collective-permute-start | bytes 786440 | tf_op jit(solution)/shard_map/ppermute | solution.py:149
  56.1 53.4 %collective-permute-start.1 = (bf16[256,2048]{1,0:T(8,128)(2,1)}, bf16[256,2048]{1,0:T(8,128)(2,1)}, u32[]{:S(2)}, u32[]{:S(2)}) collective-permute-start(bf16[256,2048]{1,0:T(8,128)(2,1)} %fusion.20), channel_id=1, source_target_pairs={{0,8},{8,0},{16,24},{24,16},{1,9},{9,1},{17,25},{25,17},{2,10},{10... | collective-permute-start | bytes 3145736 | tf_op jit(solution)/shard_map/ppermute | solution.py:90
  56.2 51.3 %collective-permute-start.26 = (bf16[256,2048]{1,0:T(8,128)(2,1)}, bf16[256,2048]{1,0:T(8,128)(2,1)}, u32[]{:S(2)}, u32[]{:S(2)}) collective-permute-start(bf16[256,2048]{1,0:T(8,128)(2,1)} %get-tuple-element.93.refs_0_), channel_id=1, source_target_pairs={{0,2},{2,4},{4,6},{6,7},{7,5},{5,3},{3,1},{1,0},{8,10},{10,12},{12... | collective-permute-start | bytes 3145736 | tf_op jit(solution)/shard_map/ppermute | solution.py:149
  57.8 50.2 %collective-permute-start.30 = (bf16[256,2048]{1,0:T(8,128)(2,1)}, bf16[256,2048]{1,0:T(8,128)(2,1)}, u32[]{:S(2)}, u32[]{:S(2)}) collective-permute-start(bf16[256,2048]{1,0:T(8,128)(2,1)} %get-tuple-element.93.refs_0_), channel_id=1, source_target_pairs={{2,0},{4,2},{6,4},{7,6},{5,7},{3,5},{1,3},{0,1},{10,8},{12,10},{14... | collective-permute-start | bytes 3145736 | tf_op jit(solution)/shard_map/ppermute | solution.py:149
  58.5 52.6 %collective-permute-start.2 = (bf16[256,2048]{1,0:T(8,128)(2,1)}, bf16[256,2048]{1,0:T(8,128)(2,1)}, u32[]{:S(2)}, u32[]{:S(2)}) collective-permute-start(bf16[256,2048]{1,0:T(8,128)(2,1)} %collective-permute-done), channel_id=1, source_target_pairs={{0,8},{8,0},{16,24},{24,16},{1,9},{9,1},{17,25},{25,17},{2,10},{10... | collective-permute-start | bytes 3145736 | tf_op jit(solution)/shard_map/ppermute | solution.py:90
  60.5 31.3 %collective-permute-start.11 = (bf16[256,768]{1,0:T(8,128)(2,1)}, bf16[256,768]{1,0:T(8,128)(2,1)}, u32[]{:S(2)}, u32[]{:S(2)}) collective-permute-start(bf16[256,768]{1,0:T(8,128)(2,1)} %collective-permute-done.10.refs_6_), channel_id=1, source_target_pairs={{2,0},{4,2},{6,4},{7,6},{5,7},{3,5},{1,3},{0,1},{10,8},{12,10},{14... | collective-permute-start | bytes 1179656 | tf_op jit(solution)/shard_map/ppermute | solution.py:149
  102.4 50.8 %collective-permute-start.33 = (bf16[256,2048]{1,0:T(8,128)(2,1)}, bf16[256,2048]{1,0:T(8,128)(2,1)}, u32[]{:S(2)}, u32[]{:S(2)}) collective-permute-start(bf16[256,2048]{1,0:T(8,128)(2,1)} %get-tuple-element.100.refs_0_), channel_id=1, source_target_pairs={{0,2},{2,4},{4,6},{6,7},{7,5},{5,3},{3,1},{1,0},{8,10},{10,12},{12... | collective-permute-start | bytes 3145736 | tf_op jit(solution)/shard_map/ppermute | solution.py:149
  107.5 46.3 %collective-permute-start.36 = (bf16[256,2048]{1,0:T(8,128)(2,1)}, bf16[256,2048]{1,0:T(8,128)(2,1)}, u32[]{:S(2)}, u32[]{:S(2)}) collective-permute-start(bf16[256,2048]{1,0:T(8,128)(2,1)} %get-tuple-element.100.refs_0_), channel_id=1, source_target_pairs={{2,0},{4,2},{6,4},{7,6},{5,7},{3,5},{1,3},{0,1},{10,8},{12,10},{14... | collective-permute-start | bytes 3145736 | tf_op jit(solution)/shard_map/ppermute | solution.py:149
  108.0 60.4 %collective-permute-start.20 = (bf16[2048,512]{1,0:T(8,128)(2,1)}, bf16[2048,512]{1,0:T(8,128)(2,1)}, u32[]{:S(2)}, u32[]{:S(2)}) collective-permute-start(bf16[2048,512]{1,0:T(8,128)(2,1)} %place_blocks.9), channel_id=1, source_target_pairs={{0,16},{8,24},{16,0},{24,8},{1,17},{9,25},{17,1},{25,9},{2,18},{10... | collective-permute-start | bytes 6291464 | tf_op jit(solution)/shard_map/ppermute | solution.py:90
  109.5 60.7 %collective-permute-start.27 = (bf16[256,2048]{1,0:T(8,128)(2,1)}, bf16[256,2048]{1,0:T(8,128)(2,1)}, u32[]{:S(2)}, u32[]{:S(2)}) collective-permute-start(bf16[256,2048]{1,0:T(8,128)(2,1)} %collective-permute-done.26.refs_1_), channel_id=1, source_target_pairs={{0,2},{2,4},{4,6},{6,7},{7,5},{5,3},{3,1},{1,0},{8,10},{10,12},{12... | collective-permute-start | bytes 3145736 | tf_op jit(solution)/shard_map/ppermute | solution.py:149
  111.1 59.1 %collective-permute-start.31 = (bf16[256,2048]{1,0:T(8,128)(2,1)}, bf16[256,2048]{1,0:T(8,128)(2,1)}, u32[]{:S(2)}, u32[]{:S(2)}) collective-permute-start(bf16[256,2048]{1,0:T(8,128)(2,1)} %collective-permute-done.30.refs_7_), channel_id=1, source_target_pairs={{2,0},{4,2},{6,4},{7,6},{5,7},{3,5},{1,3},{0,1},{10,8},{12,10},{14... | collective-permute-start | bytes 3145736 | tf_op jit(solution)/shard_map/ppermute | solution.py:149
  159.6 60.9 %collective-permute-start.21 = (bf16[2048,512]{1,0:T(8,128)(2,1)}, bf16[2048,512]{1,0:T(8,128)(2,1)}, u32[]{:S(2)}, u32[]{:S(2)}) collective-permute-start(bf16[2048,512]{1,0:T(8,128)(2,1)} %place_blocks.9), channel_id=1, source_target_pairs={{0,8},{8,0},{16,24},{24,16},{1,9},{9,1},{17,25},{25,17},{2,10},{10... | collective-permute-start | bytes 6291464 | tf_op jit(solution)/shard_map/ppermute | solution.py:90
  167.9 25.2 %collective-permute-start.37 = (bf16[256,2048]{1,0:T(8,128)(2,1)}, bf16[256,2048]{1,0:T(8,128)(2,1)}, u32[]{:S(2)}, u32[]{:S(2)}) collective-permute-start(bf16[256,2048]{1,0:T(8,128)(2,1)} %collective-permute-done.36.refs_7_), channel_id=1, source_target_pairs={{2,0},{4,2},{6,4},{7,6},{5,7},{3,5},{1,3},{0,1},{10,8},{12,10},{14... | collective-permute-start | bytes 3145736 | tf_op jit(solution)/shard_map/ppermute | solution.py:149
  168.6 26.3 %collective-permute-start.34 = (bf16[256,2048]{1,0:T(8,128)(2,1)}, bf16[256,2048]{1,0:T(8,128)(2,1)}, u32[]{:S(2)}, u32[]{:S(2)}) collective-permute-start(bf16[256,2048]{1,0:T(8,128)(2,1)} %collective-permute-done.33.refs_1_), channel_id=1, source_target_pairs={{0,2},{2,4},{4,6},{6,7},{7,5},{5,3},{3,1},{1,0},{8,10},{10,12},{12... | collective-permute-start | bytes 3145736 | tf_op jit(solution)/shard_map/ppermute | solution.py:149
  170.2 71.7 %collective-permute-start.22 = (bf16[2048,512]{1,0:T(8,128)(2,1)}, bf16[2048,512]{1,0:T(8,128)(2,1)}, u32[]{:S(2)}, u32[]{:S(2)}) collective-permute-start(bf16[2048,512]{1,0:T(8,128)(2,1)} %collective-permute-done.20), channel_id=1, source_target_pairs={{0,8},{8,0},{16,24},{24,16},{1,9},{9,1},{17,25},{25,17},{2,10},{10... | collective-permute-start | bytes 6291464 | tf_op jit(solution)/shard_map/ppermute | solution.py:90
  170.2 46.1 %collective-permute-start.28 = (bf16[256,2048]{1,0:T(8,128)(2,1)}, bf16[256,2048]{1,0:T(8,128)(2,1)}, u32[]{:S(2)}, u32[]{:S(2)}) collective-permute-start(bf16[256,2048]{1,0:T(8,128)(2,1)} %collective-permute-done.27.refs_2_), channel_id=1, source_target_pairs={{0,2},{2,4},{4,6},{6,7},{7,5},{5,3},{3,1},{1,0},{8,10},{10,12},{12... | collective-permute-start | bytes 3145736 | tf_op jit(solution)/shard_map/ppermute | solution.py:149
  193.1 31.6 %collective-permute-start.32 = (bf16[256,2048]{1,0:T(8,128)(2,1)}, bf16[256,2048]{1,0:T(8,128)(2,1)S(1)}, u32[]{:S(2)}, u32[]{:S(2)}) collective-permute-start(bf16[256,2048]{1,0:T(8,128)(2,1)} %collective-permute-done.31.refs_6_), channel_id=1, source_target_pairs={{2,0},{4,2},{6,4},{7,6},{5,7},{3,5},{1,3},{0,1},{10,8},{12,10},{14... | collective-permute-start | bytes 3145736 | tf_op jit(solution)/shard_map/ppermute | solution.py:149
  195.0 44.9 %collective-permute-start.38 = (bf16[256,2048]{1,0:T(8,128)(2,1)}, bf16[256,2048]{1,0:T(8,128)(2,1)S(1)}, u32[]{:S(2)}, u32[]{:S(2)}) collective-permute-start(bf16[256,2048]{1,0:T(8,128)(2,1)} %collective-permute-done.37.refs_6_), channel_id=1, source_target_pairs={{2,0},{4,2},{6,4},{7,6},{5,7},{3,5},{1,3},{0,1},{10,8},{12,10},{14... | collective-permute-start | bytes 3145736 | tf_op jit(solution)/shard_map/ppermute | solution.py:149
  216.3 24.0 %collective-permute-start.43 = (bf16[128,2048]{1,0:T(8,128)(2,1)S(1)}, bf16[128,2048]{1,0:T(8,128)(2,1)S(1)}, u32[]{:S(2)}, u32[]{:S(2)}) collective-permute-start(bf16[128,2048]{1,0:T(8,128)(2,1)S(1)} %copy-done.21), channel_id=1, source_target_pairs={{0,2},{2,4},{4,6},{6,7},{7,5},{5,3},{3,1},{1,0},{8,10},{10,12},{12... | collective-permute-start | bytes 1572872 | tf_op jit(solution)/shard_map/ppermute | solution.py:149
  220.5 34.6 %collective-permute-start.35 = (bf16[256,2048]{1,0:T(8,128)(2,1)}, bf16[256,2048]{1,0:T(8,128)(2,1)S(1)}, u32[]{:S(2)}, u32[]{:S(2)}) collective-permute-start(bf16[256,2048]{1,0:T(8,128)(2,1)} %collective-permute-done.34.refs_2_), channel_id=1, source_target_pairs={{0,2},{2,4},{4,6},{6,7},{7,5},{5,3},{3,1},{1,0},{8,10},{10,12},{12... | collective-permute-start | bytes 3145736 | tf_op jit(solution)/shard_map/ppermute | solution.py:149
  224.7 63.4 %collective-permute-start.40 = (bf16[256,2048]{1,0:T(8,128)(2,1)}, bf16[256,2048]{1,0:T(8,128)(2,1)}, u32[]{:S(2)}, u32[]{:S(2)}) collective-permute-start(bf16[256,2048]{1,0:T(8,128)(2,1)} %bitcast.27), channel_id=1, source_target_pairs={{0,16},{8,24},{16,0},{24,8},{1,17},{9,25},{17,1},{25,9},{2,18},{10... | collective-permute-start | bytes 3145736 | tf_op jit(solution)/shard_map/ppermute | solution.py:90
  240.3 35.7 %collective-permute-start.29 = (bf16[256,2048]{1,0:T(8,128)(2,1)}, bf16[256,2048]{1,0:T(8,128)(2,1)S(1)}, u32[]{:S(2)}, u32[]{:S(2)}) collective-permute-start(bf16[256,2048]{1,0:T(8,128)(2,1)} %collective-permute-done.28.refs_3_), channel_id=1, source_target_pairs={{0,2},{2,4},{4,6},{6,7},{7,5},{5,3},{3,1},{1,0},{8,10},{10,12},{12... | collective-permute-start | bytes 3145736 | tf_op jit(solution)/shard_map/ppermute | solution.py:149
  241.9 44.2 %collective-permute-start.39 = (bf16[256,2048]{1,0:T(8,128)(2,1)S(1)}, bf16[256,2048]{1,0:T(8,128)(2,1)S(1)}, u32[]{:S(2)}, u32[]{:S(2)}) collective-permute-start(bf16[256,2048]{1,0:T(8,128)(2,1)S(1)} %collective-permute-done.38.refs_5_), channel_id=1, source_target_pairs={{2,0},{4,2},{6,4},{7,6},{5,7},{3,5},{1,3},{0,1},{10,8},{12,10},{14... | collective-permute-start | bytes 3145736 | tf_op jit(solution)/shard_map/ppermute | solution.py:149
  254.7 31.0 %collective-permute-start.53 = (bf16[128,2048]{1,0:T(8,128)(2,1)S(1)}, bf16[128,2048]{1,0:T(8,128)(2,1)S(1)}, u32[]{:S(2)}, u32[]{:S(2)}) collective-permute-start(bf16[128,2048]{1,0:T(8,128)(2,1)S(1)} %copy-done.20), channel_id=1, source_target_pairs={{2,0},{4,2},{6,4},{7,6},{5,7},{3,5},{1,3},{0,1},{10,8},{12,10},{14... | collective-permute-start | bytes 1572872 | tf_op jit(solution)/shard_map/ppermute | solution.py:149
  255.1 32.5 %collective-permute-start.44 = (bf16[128,2048]{1,0:T(8,128)(2,1)S(1)}, bf16[128,2048]{1,0:T(8,128)(2,1)S(1)}, u32[]{:S(2)}, u32[]{:S(2)}) collective-permute-start(bf16[128,2048]{1,0:T(8,128)(2,1)S(1)} %collective-permute-done.43.refs_1_), channel_id=1, source_target_pairs={{0,2},{2,4},{4,6},{6,7},{7,5},{5,3},{3,1},{1,0},{8,10},{10,12},{12... | collective-permute-start | bytes 1572872 | tf_op jit(solution)/shard_map/ppermute | solution.py:149
  276.1 34.2 %collective-permute-start.23 = (bf16[256,2048]{1,0:T(8,128)(2,1)}, bf16[256,2048]{1,0:T(8,128)(2,1)}, u32[]{:S(2)}, u32[]{:S(2)}) collective-permute-start(bf16[256,2048]{1,0:T(8,128)(2,1)} %multiply_convert_fusion.4), channel_id=1, source_target_pairs={{0,16},{8,24},{16,0},{24,8},{1,17},{9,25},{17,1},{25,9},{2,18},{10... | collective-permute-start | bytes 3145736 | tf_op jit(solution)/shard_map/ppermute | solution.py:90
  300.5 30.9 %collective-permute-start.41 = (bf16[256,2048]{1,0:T(8,128)(2,1)}, bf16[256,2048]{1,0:T(8,128)(2,1)}, u32[]{:S(2)}, u32[]{:S(2)}) collective-permute-start(bf16[256,2048]{1,0:T(8,128)(2,1)} %bitcast.27), channel_id=1, source_target_pairs={{0,8},{8,0},{16,24},{24,16},{1,9},{9,1},{17,25},{25,17},{2,10},{10... | collective-permute-start | bytes 3145736 | tf_op jit(solution)/shard_map/ppermute | solution.py:90
  300.9 32.5 %collective-permute-start.42 = (bf16[256,2048]{1,0:T(8,128)(2,1)}, bf16[256,2048]{1,0:T(8,128)(2,1)}, u32[]{:S(2)}, u32[]{:S(2)}) collective-permute-start(bf16[256,2048]{1,0:T(8,128)(2,1)} %collective-permute-done.40), channel_id=1, source_target_pairs={{0,8},{8,0},{16,24},{24,16},{1,9},{9,1},{17,25},{25,17},{2,10},{10... | collective-permute-start | bytes 3145736 | tf_op jit(solution)/shard_map/ppermute | solution.py:90
  310.2 24.4 %collective-permute-start.49 = (bf16[128,2048]{1,0:T(8,128)(2,1)}, bf16[128,2048]{1,0:T(8,128)(2,1)}, u32[]{:S(2)}, u32[]{:S(2)}) collective-permute-start(bf16[128,2048]{1,0:T(8,128)(2,1)} %collective-permute-done.48.refs_6_), channel_id=1, source_target_pairs={{2,0},{4,2},{6,4},{7,6},{5,7},{3,5},{1,3},{0,1},{10,8},{12,10},{14... | collective-permute-start | bytes 1572872 | tf_op jit(solution)/shard_map/ppermute | solution.py:149
  319.6 46.0 %collective-permute-start.24 = (bf16[256,2048]{1,0:T(8,128)(2,1)}, bf16[256,2048]{1,0:T(8,128)(2,1)}, u32[]{:S(2)}, u32[]{:S(2)}) collective-permute-start(bf16[256,2048]{1,0:T(8,128)(2,1)} %multiply_convert_fusion.4), channel_id=1, source_target_pairs={{0,8},{8,0},{16,24},{24,16},{1,9},{9,1},{17,25},{25,17},{2,10},{10... | collective-permute-start | bytes 3145736 | tf_op jit(solution)/shard_map/ppermute | solution.py:90
  324.7 40.9 %collective-permute-start.25 = (bf16[256,2048]{1,0:T(8,128)(2,1)}, bf16[256,2048]{1,0:T(8,128)(2,1)}, u32[]{:S(2)}, u32[]{:S(2)}) collective-permute-start(bf16[256,2048]{1,0:T(8,128)(2,1)} %collective-permute-done.23), channel_id=1, source_target_pairs={{0,8},{8,0},{16,24},{24,16},{1,9},{9,1},{17,25},{25,17},{2,10},{10... | collective-permute-start | bytes 3145736 | tf_op jit(solution)/shard_map/ppermute | solution.py:90
  331.4 26.1 %collective-permute-start.46 = (bf16[128,2048]{1,0:T(8,128)(2,1)S(1)}, bf16[128,2048]{1,0:T(8,128)(2,1)S(1)}, u32[]{:S(2)}, u32[]{:S(2)}) collective-permute-start(bf16[128,2048]{1,0:T(8,128)(2,1)S(1)} %copy-done.53), channel_id=1, source_target_pairs={{0,2},{2,4},{4,6},{6,7},{7,5},{5,3},{3,1},{1,0},{8,10},{10,12},{12... | collective-permute-start | bytes 1572872 | tf_op jit(solution)/shard_map/ppermute | solution.py:149
  333.4 24.1 %collective-permute-start.52 = (bf16[128,2048]{1,0:T(8,128)(2,1)S(1)}, bf16[128,2048]{1,0:T(8,128)(2,1)}, u32[]{:S(2)}, u32[]{:S(2)}) collective-permute-start(bf16[128,2048]{1,0:T(8,128)(2,1)S(1)} %copy-done.55), channel_id=1, source_target_pairs={{0,2},{2,4},{4,6},{6,7},{7,5},{5,3},{3,1},{1,0},{8,10},{10,12},{12... | collective-permute-start | bytes 1572872 | tf_op jit(solution)/shard_map/ppermute | solution.py:149
  460.5 29.5 %collective-permute-start.59 = (bf16[512,2048]{1,0:T(8,128)(2,1)}, bf16[512,2048]{1,0:T(8,128)(2,1)S(1)}, u32[]{:S(2)}, u32[]{:S(2)}) collective-permute-start(bf16[512,2048]{1,0:T(8,128)(2,1)} %get-tuple-element.120), channel_id=1, source_target_pairs={{0,8},{8,0},{16,24},{24,16},{1,9},{9,1},{17,25},{25,17},{2,10},{10... | collective-permute-start | bytes 6291464 | tf_op jit(solution)/shard_map/ppermute | solution.py:90
  489.4 45.7 %collective-permute-start.58 = (bf16[256,2048]{1,0:T(8,128)(2,1)S(1)}, bf16[256,2048]{1,0:T(8,128)(2,1)S(1)}, u32[]{:S(2)}, u32[]{:S(2)}) collective-permute-start(bf16[256,2048]{1,0:T(8,128)(2,1)S(1)} %get-tuple-element.164), channel_id=1, source_target_pairs={{0,8},{8,0},{16,24},{24,16},{1,9},{9,1},{17,25},{25,17},{2,10},{10... | collective-permute-start | bytes 3145736 | tf_op jit(solution)/shard_map/ppermute | solution.py:90
  491.0 25.2 %collective-permute-start.60 = (bf16[256,2048]{1,0:T(8,128)(2,1)S(1)}, bf16[256,2048]{1,0:T(8,128)(2,1)S(1)}, u32[]{:S(2)}, u32[]{:S(2)}) collective-permute-start(bf16[256,2048]{1,0:T(8,128)(2,1)S(1)} %slice.414), channel_id=1, source_target_pairs={{0,16},{8,24},{16,0},{24,8},{1,17},{9,25},{17,1},{25,9},{2,18},{10... | collective-permute-start | bytes 3145736 | tf_op jit(solution)/shard_map/ppermute | solution.py:90
  539.6 45.1 %collective-permute-start.57 = (bf16[256,2048]{1,0:T(8,128)(2,1)}, bf16[256,2048]{1,0:T(8,128)(2,1)}, u32[]{:S(2)}, u32[]{:S(2)}) collective-permute-start(bf16[256,2048]{1,0:T(8,128)(2,1)} %get-tuple-element.163), channel_id=1, source_target_pairs={{0,8},{8,0},{16,24},{24,16},{1,9},{9,1},{17,25},{25,17},{2,10},{10... | collective-permute-start | bytes 3145736 | tf_op jit(solution)/shard_map/ppermute | solution.py:90
  539.6 32.8 %collective-permute-start.68 = (bf16[640,512]{1,0:T(8,128)(2,1)S(1)}, bf16[640,512]{1,0:T(8,128)(2,1)}, u32[]{:S(2)}, u32[]{:S(2)}) collective-permute-start(bf16[640,512]{1,0:T(8,128)(2,1)S(1)} %get-tuple-element.161), channel_id=1, source_target_pairs={{0,8},{8,0},{16,24},{24,16},{1,9},{9,1},{17,25},{25,17},{2,10},{10... | collective-permute-start | bytes 1966088 | tf_op jit(solution)/shard_map/ppermute | solution.py:90
  542.7 42.0 %collective-permute-start.66 = (bf16[256,2048]{1,0:T(8,128)(2,1)}, bf16[256,2048]{1,0:T(8,128)(2,1)}, u32[]{:S(2)}, u32[]{:S(2)}) collective-permute-start(bf16[256,2048]{1,0:T(8,128)(2,1)} %fusion.23), channel_id=1, source_target_pairs={{0,16},{8,24},{16,0},{24,8},{1,17},{9,25},{17,1},{25,9},{2,18},{10... | collective-permute-start | bytes 3145736 | tf_op jit(solution)/shard_map/ppermute | solution.py:90
  545.5 37.2 %collective-permute-start.70 = (bf16[640,512]{1,0:T(8,128)(2,1)}, bf16[640,512]{1,0:T(8,128)(2,1)}, u32[]{:S(2)}, u32[]{:S(2)}) collective-permute-start(bf16[640,512]{1,0:T(8,128)(2,1)} %add_convert_fusion.2), channel_id=1, source_target_pairs={{0,16},{8,24},{16,0},{24,8},{1,17},{9,25},{17,1},{25,9},{2,18},{10... | collective-permute-start | bytes 1966088 | tf_op jit(solution)/shard_map/ppermute | solution.py:90
  545.9 26.5 %collective-permute-start.67 = (bf16[192,512]{1,0:T(8,128)(2,1)S(1)}, bf16[192,512]{1,0:T(8,128)(2,1)S(1)}, u32[]{:S(2)}, u32[]{:S(2)}) collective-permute-start(bf16[192,512]{1,0:T(8,128)(2,1)S(1)} %constant_dynamic-slice_fusion.9), channel_id=1, source_target_pairs={{0,4},{1,5},{2,6},{3,7},{4,0},{5,1},{6,2},{7,3},{8,12},{9,13},{10,... | collective-permute-start | bytes 589832 | tf_op jit(solution)/shard_map/ppermute | solution.py:90
  628.2 25.5 %collective-permute-start.79 = (bf16[256,2048]{1,0:T(8,128)(2,1)S(1)}, bf16[256,2048]{1,0:T(8,128)(2,1)S(1)}, u32[]{:S(2)}, u32[]{:S(2)}) collective-permute-start(bf16[256,2048]{1,0:T(8,128)(2,1)S(1)} %slice.413), channel_id=1, source_target_pairs={{0,16},{8,24},{16,0},{24,8},{1,17},{9,25},{17,1},{25,9},{2,18},{10... | collective-permute-start | bytes 3145736 | tf_op jit(solution)/shard_map/ppermute | solution.py:90
  634.3 26.1 %collective-permute-start.87 = (bf16[768,512]{1,0:T(8,128)(2,1)S(1)}, bf16[768,512]{1,0:T(8,128)(2,1)S(1)}, u32[]{:S(2)}, u32[]{:S(2)}) collective-permute-start(bf16[768,512]{1,0:T(8,128)(2,1)S(1)} %pad_maximum_fusion.11), channel_id=1, source_target_pairs={{0,1},{1,0},{2,3},{3,2},{4,5},{5,4},{6,7},{7,6},{8,9},{9,8},{10,11... | collective-permute-start | bytes 2359304 | tf_op jit(solution)/shard_map/ppermute | solution.py:90
  663.5 34.7 %collective-permute-start.99 = (bf16[1536,512]{1,0:T(8,128)(2,1)}, bf16[1536,512]{1,0:T(8,128)(2,1)}, u32[]{:S(2)}, u32[]{:S(2)}) collective-permute-start(bf16[1536,512]{1,0:T(8,128)(2,1)} %pad_maximum_fusion.4.refs_0_), channel_id=1, source_target_pairs={{0,16},{8,24},{16,0},{24,8},{1,17},{9,25},{17,1},{25,9},{2,18},{10... | collective-permute-start | bytes 4718600 | tf_op jit(solution)/shard_map/ppermute | solution.py:90
  712.9 29.0 %collective-permute-start.102 = (bf16[896,512]{1,0:T(8,128)(2,1)S(1)}, bf16[896,512]{1,0:T(8,128)(2,1)}, u32[]{:S(2)}, u32[]{:S(2)}) collective-permute-start(bf16[896,512]{1,0:T(8,128)(2,1)S(1)} %constant_dynamic-update-slice_fusion.2.refs_0_), channel_id=1, source_target_pairs={{0,8},{8,0},{16,24},{24,16},{1,9},{9,1},{17,25},{25,17},{2,10},{10... | collective-permute-start | bytes 2752520 | tf_op jit(solution)/shard_map/ppermute | solution.py:90
  (157 other events, 2381.2 us)
